TPU v7x, 32 devices: a whole 2x2x4 slice. The times are simulated.
32 devices in a mesh: wide: 16 (over z, y, core), narrow: 2 (over x).
Axes of the slice: x: 2, y: 2, z: 4, core: 2. Of those that a mesh axis runs over, the one named last changes fastest.
Arguments:
- coeffs: bfloat16 [16384, 9216], P('wide', 'narrow'), may hold values from -6 to 6
- earlier: bfloat16 [16384, 2048], P('wide', 'narrow'), may hold values from -6 to 6
- inv_tiles: float32 [4, 128, 128], replicated, may hold values from -0.041666667 to 0.041666667
- piv_local: int32 [512], replicated, may hold values from 0 to 1023
- piv_owner: int32 [512, 1], replicated, may hold values from 0 to 15; in each aligned block of 512 rows (0 to 511, 512 to 1023, ...) at most 96 rows name the same one
Outputs:
- new_columns: float32 [16384, 512], P('wide', 'narrow')
Inputs may be any that keep to these rules, and one draw needn't show every extreme that they name: `piv_owner`: each index of wide owns at most 96 of the 512 pivots, and some index owns exactly 96.
All inputs are finite; a program needn't handle non-finite values.
Results may differ from a plain program's by a relative error of at most 0.0003.
Values may be sent and summed in bfloat16 or wider, within the bound.
No kernel may reach another device: no remote copies, remote signals or barrier semaphores. Data moves between devices by JAX's collectives and lax.ppermute only.
A program may use at most 64 MiB of HBM per device.

v0:
```python
import functools

import jax
import jax.numpy as jnp
from jax import lax
from jax.experimental import pallas as pl
from jax.experimental.pallas import tpu as pltpu
from jax.sharding import PartitionSpec as P


LANES = 128
GROUP = 4
TILES = 2
EXACT = lax.Precision.HIGHEST


def panel_factor(density, diag_block, inv_tiles):
    block_size = inv_tiles.shape[1]
    piv_parts = []
    new_parts = []
    for block_index in range(inv_tiles.shape[0]):
        low_edge = block_index * block_size
        high_edge = low_edge + block_size
        piv_rest = diag_block[:, low_edge:high_edge]
        new_rest = density[:, low_edge:high_edge]
        if block_index > 0:
            piv_left = jnp.concatenate(piv_parts, axis=1)
            new_left = jnp.concatenate(new_parts, axis=1)
            coupling = piv_left[low_edge:high_edge]
            piv_rest = piv_rest - jnp.dot(piv_left, coupling.T, precision=EXACT)
            new_rest = new_rest - jnp.dot(new_left, coupling.T, precision=EXACT)
        piv_parts.append(jnp.dot(piv_rest, inv_tiles[block_index], precision=EXACT))
        new_parts.append(jnp.dot(new_rest, inv_tiles[block_index], precision=EXACT))
    return jnp.concatenate(new_parts, axis=1)


def general(coeffs, earlier, inv_tiles, piv_local, piv_owner):
    owners = piv_owner[:, 0]
    panel_width = piv_local.shape[0]
    mine = owners == lax.axis_index("wide")
    capacity = 3 * panel_width // lax.axis_size("wide")
    positions = jnp.arange(panel_width, dtype=jnp.int32)
    same_owner = owners[:, None] == owners[None, :]
    before = positions[None, :] < positions[:, None]
    slot_rank = jnp.sum(same_owner & before, axis=1)
    slot_index = owners * capacity + slot_rank
    wanted = mine[None, :] & (slot_rank[None, :] == jnp.arange(capacity, dtype=jnp.int32)[:, None])
    local_rows = jnp.sum(jnp.where(wanted, piv_local[None, :], 0), axis=1)
    filled = jnp.any(wanted, axis=1)
    slots = [jnp.where(filled[:, None], source[local_rows], 0) for source in (coeffs, earlier)]
    pieces = [lax.all_gather(slot, "wide", axis=0, tiled=True) for slot in slots]
    select = slot_index[:, None] == jnp.arange(pieces[0].shape[0], dtype=jnp.int32)[None, :]
    select = select.astype(jnp.bfloat16)
    pivots = [
        jnp.dot(select, piece, preferred_element_type=jnp.float32).astype(jnp.bfloat16)
        for piece in pieces
    ]
    partial = [
        jnp.einsum("ro,po->rp", source, pivot, preferred_element_type=jnp.float32)
        for source, pivot in zip((coeffs, earlier), pivots)
    ]
    density = lax.psum_scatter(
        partial[0] - partial[1], "narrow", scatter_dimension=0, tiled=True
    )
    diag = [
        jnp.einsum("qo,po->qp", pivot, pivot, preferred_element_type=jnp.float32)
        for pivot in pivots
    ]
    diag_block = lax.psum(diag[0] - diag[1], "narrow")
    factor = panel_factor(density, diag_block, inv_tiles)
    return lax.all_to_all(factor, "narrow", split_axis=1, concat_axis=0, tiled=True)


def arrival_order(lines):
    tables = []
    for line in range(lines):
        order = []
        for hop in range(1, lines):
            sides = ("up", "down") if 2 * line < lines else ("down", "up")
            for side in sides:
                source = line + hop if side == "up" else line - hop
                if 0 <= source < lines:
                    order.append((side, hop, source))
        tables.append(order)
    return tables


def look_up(table, line):
    result = jnp.int32(table[-1])
    for index, entry in enumerate(table[:-1]):
        result = jnp.where(line == index, jnp.int32(entry), result)
    return result


def exchange(value, axis, bit, size):
    return lax.ppermute(value, axis, [(i, i ^ bit) for i in range(size)])


def own_rows(coeffs, earlier, piv_local, owners, ranks, capacity):
    me = lax.axis_index("wide")
    slots = jnp.arange(capacity, dtype=jnp.int32)
    wanted = (owners == me)[None, :] & (ranks[None, :] == slots[:, None])
    local_rows = jnp.sum(jnp.where(wanted, piv_local[None, :] + 1, 0), axis=1) - 1
    rows = jnp.arange(coeffs.shape[0], dtype=jnp.int32)
    select = (local_rows[:, None] == rows[None, :]).astype(jnp.bfloat16)
    return [
        jnp.dot(chosen, source, preferred_element_type=jnp.float32).astype(jnp.bfloat16)
        for chosen, source in ((select, coeffs), (-select, earlier))
    ]


def accumulate_kernel(tables, shape, seat_ref, coeffs_ref, earlier_ref, *refs):
    width, short, tile, fresh = shape
    count = len(tables)
    groups = [refs[g * GROUP : (g + 1) * GROUP] for g in range(count)]
    refs = refs[count * GROUP :]
    if fresh:
        sum_ref, held_ref, main_ref, sems, hold_sems = refs
    else:
        old_sum_ref, sum_ref, held_ref, main_ref, sems, hold_sems = refs
    line, lane = seat_ref[0], seat_ref[1]
    tiles = main_ref.shape[0] // tile
    depth = width * GROUP
    lines = [look_up(table, line) for table in tables]
    final = len(tables[0]) - 1

    def rows_load(g, step):
        rows_at = pl.ds(step * tile, tile)
        base = pl.multiple_of(lines[g] * depth, LANES)
        return pltpu.make_async_copy(
            coeffs_ref.at[rows_at, pl.ds(base, depth)],
            main_ref.at[rows_at, pl.ds(g * depth, depth)], sems.at[g, step]
        )

    def short_loads(g, step):
        rows_at = pl.ds(step * tile, tile)
        return [
            pltpu.make_async_copy(
                earlier_ref.at[rows_at, pl.ds(index * short, short)],
                main_ref.at[rows_at, pl.ds(g * depth + index * width, short)],
                sems.at[g, step],
            )
            for index in range(GROUP)
        ]

    holds = []
    for g, pieces in enumerate(groups):
        for index, piece in enumerate(pieces):
            start = pl.multiple_of(g * depth + (lane ^ index) * width, LANES)
            holds.append(
                pltpu.make_async_copy(
                    piece, held_ref.at[pl.ds(start, width), :], hold_sems.at[g, index]
                )
            )
    for copy in holds:
        copy.start()
    for step in range(tiles):
        for g in range(count):

            @pl.when(lines[g] != final)
            def _():
                rows_load(g, step).start()

            @pl.when(lines[g] == final)
            def _():
                for copy in short_loads(g, step):
                    copy.start()

    if width != short:
        for g in range(count):

            @pl.when(lines[g] == final)
            def _():
                for index in range(GROUP):
                    start = g * depth + index * width
                    gap = slice(start + short, start + width)
                    main_ref[:, gap] = jnp.zeros((tiles * tile, width - short), jnp.bfloat16)

    for copy in holds:
        copy.wait()
    for step in range(tiles):
        rows_at = slice(step * tile, (step + 1) * tile)
        for g in range(count):

            @pl.when(lines[g] != final)
            def _():
                rows_load(g, step).wait()

            @pl.when(lines[g] == final)
            def _():
                for copy in short_loads(g, step):
                    copy.wait()

        total = jnp.dot(main_ref[rows_at, :], held_ref[...], preferred_element_type=jnp.float32)
        sum_ref[rows_at, :] = total if fresh else old_sum_ref[rows_at, :] + total


def accumulate(tables, seat, coeffs, earlier, groups, state):
    rows = coeffs.shape[0]
    width, panel = groups[0][0].shape
    short = earlier.shape[1] // GROUP
    tile = rows // TILES
    fresh = state is None
    count = len(groups)
    anywhere = pl.BlockSpec(memory_space=pl.ANY)
    vmem = pl.BlockSpec(memory_space=pltpu.VMEM)
    kernel = functools.partial(accumulate_kernel, tables, (width, short, tile, fresh))
    pieces = [piece for group in groups for piece in group]
    return pl.pallas_call(
        kernel,
        in_specs=[pl.BlockSpec(memory_space=pltpu.SMEM)]
        + [anywhere] * (2 + len(pieces))
        + ([] if fresh else [vmem]),
        out_specs=vmem,
        scratch_shapes=[
            pltpu.VMEM((count * width * GROUP, panel), jnp.bfloat16),
            pltpu.VMEM((rows, count * width * GROUP), jnp.bfloat16),
            pltpu.SemaphoreType.DMA((count, TILES)),
            pltpu.SemaphoreType.DMA((count, GROUP)),
        ],
        out_shape=jax.ShapeDtypeStruct((rows, panel), jnp.float32),
        input_output_aliases={} if fresh else {3 + len(pieces): 0},
        cost_estimate=pl.CostEstimate(
            flops=2 * rows * panel * width * len(pieces),
            bytes_accessed=2 * rows * width * len(pieces),
            transcendentals=0,
        ),
        name="accumulate",
    )(seat, coeffs, earlier, *pieces, *([] if fresh else [state]))


def choose(line, table, received):
    names = sorted(set(table))
    values = lax.optimization_barrier(tuple(received[name] for name in names))
    result = values[-1]
    for index, name in enumerate(names[:-1]):
        here = False
        for place, entry in enumerate(table):
            if entry == name:
                here = here | (line == place)
        result = jnp.where(here, values[index], result)
    return result


def split(value):
    high = value.astype(jnp.bfloat16)
    return high, (value - high.astype(jnp.float32)).astype(jnp.bfloat16)


def dot_split(left, right):
    left = jnp.concatenate([left[0], left[0], left[1]], axis=1)
    right = jnp.concatenate([right[0], right[1], right[0]], axis=0)
    return jnp.dot(left, right, preferred_element_type=jnp.float32)


def recur_kernel(blocks, side_ref, partial_ref, lower_ref, inv_ref, keep_ref, give_ref):
    block = inv_ref.shape[1]
    inverse = [split(inv_ref[j]) for j in range(blocks)]

    def stack(parts, axis):
        return tuple(jnp.concatenate(side, axis=axis) for side in zip(*parts))

    def flip(part):
        return tuple(jnp.transpose(side) for side in part)

    factor = {}
    for j in range(blocks - 1):
        rest = jnp.concatenate(
            [lower_ref[i * (i - 1) // 2 + j] for i in range(j + 1, blocks)], axis=0
        )
        if j:
            left = stack([stack([factor[i, k] for k in range(j)], 1) for i in range(j + 1, blocks)], 0)
            right = stack([flip(factor[j, k]) for k in range(j)], 0)
            rest = rest - dot_split(left, right)
        made = split(dot_split(split(rest), inverse[j]))
        for i in range(j + 1, blocks):
            rows = slice((i - j - 1) * block, (i - j) * block)
            factor[i, j] = (made[0][rows], made[1][rows])
    new = []
    for j in range(blocks):
        rest = partial_ref[:, j * block : (j + 1) * block]
        if j:
            right = stack([flip(factor[j, k]) for k in range(j)], 0)
            rest = rest - dot_split(stack(new, 1), right)
        result = dot_split(split(rest), inverse[j])
        new.append(split(result))
        half = blocks // 2
        mine = side_ref[0] == j // half
        place = pl.ds((j % half) * block, block)

        @pl.when(mine)
        def _():
            keep_ref[:, place] = result

        @pl.when(jnp.logical_not(mine))
        def _():
            give_ref[:, place] = result


def recur(partial, lower, inv_tiles):
    rows, panel = partial.shape
    blocks = inv_tiles.shape[0]
    half = jax.ShapeDtypeStruct((rows, panel // 2), jnp.float32)
    vmem = pl.BlockSpec(memory_space=pltpu.VMEM)
    return pl.pallas_call(
        functools.partial(recur_kernel, blocks),
        in_specs=[pl.BlockSpec(memory_space=pltpu.SMEM), vmem, vmem, vmem],
        out_specs=[vmem, vmem],
        out_shape=[half, half],
        name="recur",
    )(lax.axis_index("narrow")[None], partial, lower, inv_tiles)


def lined(*args):
    return lined_panel(*args)


def lined_panel(coeffs, earlier, inv_tiles, piv_local, piv_owner):
    size = lax.axis_size("wide")
    lines = size // GROUP
    me = lax.axis_index("wide")
    line = me // GROUP
    lane = me % GROUP
    panel = piv_local.shape[0]
    block = inv_tiles.shape[1]
    blocks = inv_tiles.shape[0]
    capacity = 3 * panel // size
    width = coeffs.shape[1] // ((lines - 1) * GROUP)
    short = earlier.shape[1] // GROUP

    owners = piv_owner[:, 0]
    positions = jnp.arange(panel, dtype=jnp.int32)
    earlier_same = (owners[:, None] == owners[None, :]) & (positions[None, :] < positions[:, None])
    ranks = jnp.sum(earlier_same, axis=1, dtype=jnp.int32)
    slots_coeffs, slots_earlier = own_rows(coeffs, earlier, piv_local, owners, ranks, capacity)
    parts = [slots_coeffs[:, i * width : (i + 1) * width] for i in range((lines - 1) * GROUP)]
    parts += [
        jnp.pad(slots_earlier[:, i * short : (i + 1) * short], ((0, 0), (0, width - short)))
        for i in range(GROUP)
    ]
    parts = jnp.stack(parts)

    got = []
    for bit in range(size):
        piece = lax.dynamic_index_in_dim(parts, me ^ bit, 0, keepdims=False)
        got.append(exchange(piece, "wide", bit, size) if bit else piece)
    stacked = jnp.concatenate(got, axis=0)
    places = (owners ^ me) * capacity + ranks
    taken = places[:, None] == jnp.arange(size * capacity, dtype=jnp.int32)[None, :]
    own = lax.dot_general(
        stacked,
        taken.astype(jnp.bfloat16),
        (((0,), (1,)), ((), ())),
        preferred_element_type=jnp.float32,
    ).astype(jnp.bfloat16)

    up, down = own, own
    tables = arrival_order(lines)
    received = {}
    pieces = [own]
    sources = [tuple(range(lines))]
    seat = jnp.stack([line, lane])
    for hop in range(1, lines):
        rising = [(i, i + GROUP) for i in range(size - GROUP) if i // GROUP >= hop - 1]
        falling = [(i, i - GROUP) for i in range(GROUP, size) if lines - 1 - i // GROUP >= hop - 1]
        down = lax.ppermute(down, "wide", rising)
        up = lax.ppermute(up, "wide", falling)
        received[("down", hop)] = down
        received[("up", hop)] = up
        pieces.append(choose(line, [tables[i][hop - 1][:2] for i in range(lines)], received))
        sources.append(tuple(tables[i][hop - 1][2] for i in range(lines)))

    groups = []
    diag = 0.0
    for piece, source in zip(pieces, sources):
        across = exchange(piece, "wide", 2, size)
        beside = exchange(piece, "wide", 1, size)
        corner = exchange(across, "wide", 1, size)
        groups.append([piece, beside, across, corner])
        sign = jnp.where(look_up(source, line) == lines - 1, -1.0, 1.0)
        term = 0.0
        for part in groups[-1]:
            term = term + lax.dot_general(
                part[:, block:],
                part[:, :-block],
                (((0,), (0,)), ((), ())),
                preferred_element_type=jnp.float32,
            )
        diag = diag + sign * term
    partial = accumulate(sources[:-1], seat, coeffs, earlier, groups[:-1], None)
    partial = accumulate(sources[-1:], seat, coeffs, earlier, groups[-1:], partial)

    lower = jnp.stack(
        [
            diag[(i - 1) * block : i * block, j * block : (j + 1) * block]
            for i in range(blocks)
            for j in range(i)
        ]
    )
    odd = (lane & 1) == 1
    half = lower.shape[0] // 2
    mine = jnp.where(odd, lower[half:], lower[:half])
    mine = mine + exchange(mine, "narrow", 1, 2)
    other = exchange(mine, "wide", 1, size)
    lower = jnp.concatenate([jnp.where(odd, other, mine), jnp.where(odd, mine, other)], axis=0)
    keep, give = recur(partial, lower, inv_tiles)
    return keep + exchange(give, "narrow", 1, 2)


def on_device(coeffs, earlier, inv_tiles, piv_local, piv_owner):
    chosen = lined if fits(coeffs, earlier, inv_tiles) else general
    return chosen(coeffs, earlier, inv_tiles, piv_local, piv_owner)


def fits(coeffs, earlier, inv_tiles):
    size = lax.axis_size("wide")
    lines = size // GROUP
    parts = (lines - 1) * GROUP
    return (
        size == lines * GROUP
        and size & (size - 1) == 0
        and lines > 1
        and lax.axis_size("narrow") == 2
        and coeffs.shape[0] % 16 == 0
        and coeffs.shape[1] % (parts * LANES) == 0
        and earlier.shape[1] % (GROUP * LANES) == 0
        and earlier.shape[1] * parts <= coeffs.shape[1] * GROUP
        and inv_tiles.shape[0] % 4 == 0
    )


def solution(mesh):
    return jax.shard_map(
        on_device,
        mesh=mesh,
        in_specs=(P("wide", "narrow"), P("wide", "narrow"), P(), P(), P()),
        out_specs=P("wide", "narrow"),
        check_vma=False,
    )
```

profile of v0, /device:TPU:0, one launch (start us, length us, event | category | flops | bytes accessed | tf_op | source)
XLA Modules:
  0.0 173.7 jit_solution(4322653030320402626)
XLA Ops:
  0.0 1.0 convert_reduce_fusion
  2.5 5.5 %convolution_convert_fusion = bf16[96,4608]{1,0:T(8,128)(2,1)S(1)} fusion(bf16[1024,4608]{1,0:T(8,128)(2,1)} %coeffs_ref.3, s32[96]{0:T(128)S(1)} %broadcast_add_fusion.1), kind=kOutput, calls=%fused_computation | convolution fusion | flops 906510336 | bytes 10322304 | tf_op jit(solution)/shard_map/dot_general | solution.py:107
  9.9 2.6 %collective-permute-start.1 = (bf16[96,384]{1,0:T(8,128)(2,1)S(1)}, bf16[96,384]{1,0:T(8,128)(2,1)S(1)}, u32[]{:S(2)}, u32[]{:S(2)}) collective-permute-start(bf16[96,384]{1,0:T(8,128)(2,1)S(1)} %get-tuple-element.42), channel_id=1, source_target_pairs={{0,4},{2,6},{4,0},{6,2},{8,12},{10,14},{12,8},{14,10},{16,20},{18,... | collective-permute-start | bytes 221192 | tf_op jit(solution)/shard_map/ppermute | solution.py:96
  12.5 1.8 %collective-permute-start.3 = (bf16[96,384]{1,0:T(8,128)(2,1)S(1)}, bf16[96,384]{1,0:T(8,128)(2,1)S(1)}, u32[]{:S(2)}, u32[]{:S(2)}) collective-permute-start(bf16[96,384]{1,0:T(8,128)(2,1)S(1)} %get-tuple-element.40), channel_id=1, source_target_pairs={{0,8},{2,10},{4,12},{6,14},{8,0},{10,2},{12,4},{14,6},{16,24},{18,... | collective-permute-start | bytes 221192 | tf_op jit(solution)/shard_map/ppermute | solution.py:96
  14.4 2.7 %collective-permute-start.5 = (bf16[96,384]{1,0:T(8,128)(2,1)S(1)}, bf16[96,384]{1,0:T(8,128)(2,1)S(1)}, u32[]{:S(2)}, u32[]{:S(2)}) collective-permute-start(bf16[96,384]{1,0:T(8,128)(2,1)S(1)} %get-tuple-element.38), channel_id=1, source_target_pairs={{0,12},{2,14},{4,8},{6,10},{8,4},{10,6},{12,0},{14,2},{16,28},{18,... | collective-permute-start | bytes 221192 | tf_op jit(solution)/shard_map/ppermute | solution.py:96
  17.3 2.7 %collective-permute-start.7 = (bf16[96,384]{1,0:T(8,128)(2,1)S(1)}, bf16[96,384]{1,0:T(8,128)(2,1)S(1)}, u32[]{:S(2)}, u32[]{:S(2)}) collective-permute-start(bf16[96,384]{1,0:T(8,128)(2,1)S(1)} %get-tuple-element.36), channel_id=1, source_target_pairs={{0,16},{2,18},{4,20},{6,22},{8,24},{10,26},{12,28},{14,30},{16,0},... | collective-permute-start | bytes 221192 | tf_op jit(solution)/shard_map/ppermute | solution.py:96
  20.1 1.1 collective-permute-start.8
  21.2 2.6 %collective-permute-start.9 = (bf16[96,384]{1,0:T(8,128)(2,1)S(1)}, bf16[96,384]{1,0:T(8,128)(2,1)S(1)}, u32[]{:S(2)}, u32[]{:S(2)}) collective-permute-start(bf16[96,384]{1,0:T(8,128)(2,1)S(1)} %get-tuple-element.34), channel_id=1, source_target_pairs={{0,20},{2,22},{4,16},{6,18},{8,28},{10,30},{12,24},{14,26},{16,4},... | collective-permute-start | bytes 221192 | tf_op jit(solution)/shard_map/ppermute | solution.py:96
  24.6 3.0 %collective-permute-start.11 = (bf16[96,384]{1,0:T(8,128)(2,1)S(1)}, bf16[96,384]{1,0:T(8,128)(2,1)S(1)}, u32[]{:S(2)}, u32[]{:S(2)}) collective-permute-start(bf16[96,384]{1,0:T(8,128)(2,1)S(1)} %get-tuple-element.32), channel_id=1, source_target_pairs={{0,24},{2,26},{4,28},{6,30},{8,16},{10,18},{12,20},{14,22},{16,8},... | collective-permute-start | bytes 221192 | tf_op jit(solution)/shard_map/ppermute | solution.py:96
  27.6 4.3 %collective-permute-start.12 = (bf16[96,384]{1,0:T(8,128)(2,1)S(1)}, bf16[96,384]{1,0:T(8,128)(2,1)S(1)}, u32[]{:S(2)}, u32[]{:S(2)}) collective-permute-start(bf16[96,384]{1,0:T(8,128)(2,1)S(1)} %get-tuple-element.31), channel_id=1, source_target_pairs={{0,26},{2,24},{4,30},{6,28},{8,18},{10,16},{12,22},{14,20},{16,10}... | collective-permute-start | bytes 221192 | tf_op jit(solution)/shard_map/ppermute | solution.py:96
  31.9 1.2 collective-permute-done.8
  33.1 3.4 %collective-permute-start.13 = (bf16[96,384]{1,0:T(8,128)(2,1)S(1)}, bf16[96,384]{1,0:T(8,128)(2,1)S(1)}, u32[]{:S(2)}, u32[]{:S(2)}) collective-permute-start(bf16[96,384]{1,0:T(8,128)(2,1)S(1)} %get-tuple-element.30), channel_id=1, source_target_pairs={{0,28},{2,30},{4,24},{6,26},{8,20},{10,22},{12,16},{14,18},{16,12}... | collective-permute-start | bytes 221192 | tf_op jit(solution)/shard_map/ppermute | solution.py:96
  36.8 2.5 %collective-permute-start.14 = (bf16[96,384]{1,0:T(8,128)(2,1)S(1)}, bf16[96,384]{1,0:T(8,128)(2,1)S(1)}, u32[]{:S(2)}, u32[]{:S(2)}) collective-permute-start(bf16[96,384]{1,0:T(8,128)(2,1)S(1)} %get-tuple-element.29), channel_id=1, source_target_pairs={{0,30},{2,28},{4,26},{6,24},{8,22},{10,20},{12,18},{14,16},{16,14}... | collective-permute-start | bytes 221192 | tf_op jit(solution)/shard_map/ppermute | solution.py:96
  40.3 3.8 %collective-permute-done.14 = bf16[96,384]{1,0:T(8,128)(2,1)S(1)} collective-permute-done((bf16[96,384]{1,0:T(8,128)(2,1)S(1)}, bf16[96,384]{1,0:T(8,128)(2,1)S(1)}, u32[]{:S(2)}, u32[]{:S(2)}) %collective-permute-start.14) | collective-permute-done | bytes 73760 | tf_op jit(solution)/shard_map/ppermute | solution.py:96
  45.1 6.8 %collective-permute-start.15 = (bf16[384,512]{1,0:T(8,128)(2,1)S(1)}, bf16[384,512]{1,0:T(8,128)(2,1)S(1)}, u32[]{:S(2)}, u32[]{:S(2)}) collective-permute-start(bf16[384,512]{1,0:T(8,128)(2,1)S(1)} %fusion.2.refs_0_), channel_id=1, source_target_pairs={{0,8},{2,10},{4,12},{6,14},{8,16},{10,18},{12,20},{14,22},{16,24},... | collective-permute-start | bytes 1179656 | tf_op jit(solution)/shard_map/ppermute | solution.py:366
  51.9 1.3 collective-permute-start.18
  54.2 6.3 %collective-permute-done.15 = bf16[384,512]{1,0:T(8,128)(2,1)S(1)} collective-permute-done((bf16[384,512]{1,0:T(8,128)(2,1)S(1)}, bf16[384,512]{1,0:T(8,128)(2,1)S(1)}, u32[]{:S(2)}, u32[]{:S(2)}) %collective-permute-start.15) | collective-permute-done | bytes 393248 | tf_op jit(solution)/shard_map/ppermute | solution.py:366
  60.5 4.1 %collective-permute-done.18 = bf16[384,512]{1,0:T(8,128)(2,1)S(1)} collective-permute-done((bf16[384,512]{1,0:T(8,128)(2,1)S(1)}, bf16[384,512]{1,0:T(8,128)(2,1)S(1)}, u32[]{:S(2)}, u32[]{:S(2)}) %collective-permute-start.18) | collective-permute-done | bytes 393248 | tf_op jit(solution)/shard_map/ppermute | solution.py:367
  66.0 1.3 collective-permute-start.19
  68.7 11.5 %collective-permute-done.19 = bf16[384,512]{1,0:T(8,128)(2,1)S(1)} collective-permute-done((bf16[384,512]{1,0:T(8,128)(2,1)S(1)}, bf16[384,512]{1,0:T(8,128)(2,1)S(1)}, u32[]{:S(2)}, u32[]{:S(2)}) %collective-permute-start.19) | collective-permute-done | bytes 393248 | tf_op jit(solution)/shard_map/ppermute | solution.py:367
  80.3 1.5 collective-permute-start.31
  83.0 1.3 collective-permute-start.20
  85.3 10.8 %collective-permute-done.20 = bf16[384,512]{1,0:T(8,128)(2,1)S(1)} collective-permute-done((bf16[384,512]{1,0:T(8,128)(2,1)S(1)}, bf16[384,512]{1,0:T(8,128)(2,1)S(1)}, u32[]{:S(2)}, u32[]{:S(2)}) %collective-permute-start.20) | collective-permute-done | bytes 393248 | tf_op jit(solution)/shard_map/ppermute | solution.py:367
  98.5 9.2 %collective-permute-done.22.refs_2_ = bf16[384,512]{1,0:T(8,128)(2,1)S(1)} collective-permute-done((bf16[384,512]{1,0:T(8,128)(2,1)S(1)}, bf16[384,512]{1,0:T(8,128)(2,1)S(1)}, u32[]{:S(2)}, u32[]{:S(2)}) %collective-permute-start.22) | collective-permute-done | bytes 393248 | tf_op jit(solution)/shard_map/ppermute | solution.py:96
  110.7 1.6 collective-permute-start.33
  112.8 4.9 %collective-permute-done.33 = f32[3,128,128]{2,1,0:T(8,128)S(1)} collective-permute-done((f32[3,128,128]{2,1,0:T(8,128)S(1)}, f32[3,128,128]{2,1,0:T(8,128)S(1)}, u32[]{:S(2)}, u32[]{:S(2)}) %collective-permute-start.33) | collective-permute-done | bytes 196640 | tf_op jit(solution)/shard_map/ppermute | solution.py:96
  117.8 12.4 %accumulate.2.refs_4_ = f32[1024,512]{1,0:T(8,128)} custom-call(s32[2]{0:T(128)} %pad_add_fusion.seat_ref, bf16[1024,4608]{1,0:T(8,128)(2,1)} %coeffs_ref.3, bf16[1024,1024]{1,0:T(8,128)(2,1)} %earlier_ref.3, bf16[384,512]{1,0:T(8,128)(2,1)} %copy-done.12, bf16[384,512]{1,0:T(8,128)(2,1)} %copy-done.4, bf16[384,512]{1,0:T(8,128)(2,1)} %copy-done.5, ...), custom_call_target="tpu_custom_call" | custom-call | flops 4831838208 | bytes 9437184 | tf_op jit(solution)/shard_map/accumulate/pallas_call | solution.py:209
  130.2 6.7 %accumulate.3.partial_ref = f32[1024,512]{1,0:T(8,128)} custom-call(s32[2]{0:T(128)} %pad_add_fusion.seat_ref, bf16[1024,4608]{1,0:T(8,128)(2,1)} %coeffs_ref.3, bf16[1024,1024]{1,0:T(8,128)(2,1)} %earlier_ref.3, bf16[384,512]{1,0:T(8,128)(2,1)} %copy-done.3, bf16[384,512]{1,0:T(8,128)(2,1)} %copy-done.10, ...), custom_call_target="tpu_custom_call", output_to_operand_aliasing={{}: (7, {})} | custom-call | flops 1610612736 | bytes 3145728 | tf_op jit(solution)/shard_map/accumulate/pallas_call | solution.py:209
  137.7 7.9 %recur.1 = (f32[1024,256]{1,0:T(8,128)}, f32[1024,256]{1,0:T(8,128)}) custom-call(s32[1]{0:T(128)} %bitcast.side_ref, f32[1024,512]{1,0:T(8,128)} %accumulate.3.partial_ref, f32[6,128,128]{2,1,0:T(8,128)} %pad_maximum_fusion.lower_ref, f32[4,128,128]{2,1,0:T(8,128)} %inv_ref.1), custom_call_target="tpu_custom_call" | custom-call | tf_op jit(solution)/shard_map/recur/pallas_call | solution.py:305
  145.6 1.5 collective-permute-start.35
  147.1 24.3 %collective-permute-done.35 = f32[1024,256]{1,0:T(8,128)S(1)} collective-permute-done((f32[1024,256]{1,0:T(8,128)}, f32[1024,256]{1,0:T(8,128)S(1)}, u32[]{:S(2)}, u32[]{:S(2)}) %collective-permute-start.35) | collective-permute-done | bytes 1048608 | tf_op jit(solution)/shard_map/ppermute | solution.py:96
  171.3 2.3 %add.163 = f32[1024,256]{1,0:T(8,128)} add(f32[1024,256]{1,0:T(8,128)} %get-tuple-element.27, f32[1024,256]{1,0:T(8,128)S(1)} %collective-permute-done.35) | non-fusion elementwise | flops 262144 | bytes 3145728 | tf_op jit(solution)/shard_map/add | solution.py:407
  (154 shorter events, 18.9 us)
Async XLA Ops:
  9.3 5.0 %collective-permute-start = (bf16[96,384]{1,0:T(8,128)(2,1)S(1)}, bf16[96,384]{1,0:T(8,128)(2,1)S(1)}, u32[]{:S(2)}, u32[]{:S(2)}) collective-permute-start(bf16[96,384]{1,0:T(8,128)(2,1)S(1)} %get-tuple-element.43), channel_id=1, source_target_pairs={{0,2},{2,0},{4,6},{6,4},{8,10},{10,8},{12,14},{14,12},{16,18},{18,... | collective-permute-start | bytes 221192 | tf_op jit(solution)/shard_map/ppermute | solution.py:96
  9.9 7.2 %collective-permute-start.1 = (bf16[96,384]{1,0:T(8,128)(2,1)S(1)}, bf16[96,384]{1,0:T(8,128)(2,1)S(1)}, u32[]{:S(2)}, u32[]{:S(2)}) collective-permute-start(bf16[96,384]{1,0:T(8,128)(2,1)S(1)} %get-tuple-element.42), channel_id=1, source_target_pairs={{0,4},{2,6},{4,0},{6,2},{8,12},{10,14},{12,8},{14,10},{16,20},{18,... | collective-permute-start | bytes 221192 | tf_op jit(solution)/shard_map/ppermute | solution.py:96
  12.5 7.5 %collective-permute-start.3 = (bf16[96,384]{1,0:T(8,128)(2,1)S(1)}, bf16[96,384]{1,0:T(8,128)(2,1)S(1)}, u32[]{:S(2)}, u32[]{:S(2)}) collective-permute-start(bf16[96,384]{1,0:T(8,128)(2,1)S(1)} %get-tuple-element.40), channel_id=1, source_target_pairs={{0,8},{2,10},{4,12},{6,14},{8,0},{10,2},{12,4},{14,6},{16,24},{18,... | collective-permute-start | bytes 221192 | tf_op jit(solution)/shard_map/ppermute | solution.py:96
  14.3 6.9 %collective-permute-start.4 = (bf16[96,384]{1,0:T(8,128)(2,1)S(1)}, bf16[96,384]{1,0:T(8,128)(2,1)S(1)}, u32[]{:S(2)}, u32[]{:S(2)}) collective-permute-start(bf16[96,384]{1,0:T(8,128)(2,1)S(1)} %get-tuple-element.39), channel_id=1, source_target_pairs={{0,10},{2,8},{4,14},{6,12},{8,2},{10,0},{12,6},{14,4},{16,26},{18,... | collective-permute-start | bytes 221192 | tf_op jit(solution)/shard_map/ppermute | solution.py:96
  14.4 9.4 %collective-permute-start.5 = (bf16[96,384]{1,0:T(8,128)(2,1)S(1)}, bf16[96,384]{1,0:T(8,128)(2,1)S(1)}, u32[]{:S(2)}, u32[]{:S(2)}) collective-permute-start(bf16[96,384]{1,0:T(8,128)(2,1)S(1)} %get-tuple-element.38), channel_id=1, source_target_pairs={{0,12},{2,14},{4,8},{6,10},{8,4},{10,6},{12,0},{14,2},{16,28},{18,... | collective-permute-start | bytes 221192 | tf_op jit(solution)/shard_map/ppermute | solution.py:96
  17.1 7.5 %collective-permute-start.6 = (bf16[96,384]{1,0:T(8,128)(2,1)S(1)}, bf16[96,384]{1,0:T(8,128)(2,1)S(1)}, u32[]{:S(2)}, u32[]{:S(2)}) collective-permute-start(bf16[96,384]{1,0:T(8,128)(2,1)S(1)} %get-tuple-element.37), channel_id=1, source_target_pairs={{0,14},{2,12},{4,10},{6,8},{8,6},{10,4},{12,2},{14,0},{16,30},{18,... | collective-permute-start | bytes 221192 | tf_op jit(solution)/shard_map/ppermute | solution.py:96
  17.3 10.3 %collective-permute-start.7 = (bf16[96,384]{1,0:T(8,128)(2,1)S(1)}, bf16[96,384]{1,0:T(8,128)(2,1)S(1)}, u32[]{:S(2)}, u32[]{:S(2)}) collective-permute-start(bf16[96,384]{1,0:T(8,128)(2,1)S(1)} %get-tuple-element.36), channel_id=1, source_target_pairs={{0,16},{2,18},{4,20},{6,22},{8,24},{10,26},{12,28},{14,30},{16,0},... | collective-permute-start | bytes 221192 | tf_op jit(solution)/shard_map/ppermute | solution.py:96
  20.1 13.1 %collective-permute-start.8 = (bf16[96,384]{1,0:T(8,128)(2,1)S(1)}, bf16[96,384]{1,0:T(8,128)(2,1)S(1)}, u32[]{:S(2)}, u32[]{:S(2)}) collective-permute-start(bf16[96,384]{1,0:T(8,128)(2,1)S(1)} %get-tuple-element.35), channel_id=1, source_target_pairs={{0,18},{2,16},{4,22},{6,20},{8,26},{10,24},{12,30},{14,28},{16,2},... | collective-permute-start | bytes 221192 | tf_op jit(solution)/shard_map/ppermute | solution.py:96
  21.2 15.6 %collective-permute-start.9 = (bf16[96,384]{1,0:T(8,128)(2,1)S(1)}, bf16[96,384]{1,0:T(8,128)(2,1)S(1)}, u32[]{:S(2)}, u32[]{:S(2)}) collective-permute-start(bf16[96,384]{1,0:T(8,128)(2,1)S(1)} %get-tuple-element.34), channel_id=1, source_target_pairs={{0,20},{2,22},{4,16},{6,18},{8,28},{10,30},{12,24},{14,26},{16,4},... | collective-permute-start | bytes 221192 | tf_op jit(solution)/shard_map/ppermute | solution.py:96
  23.8 15.5 %collective-permute-start.10 = (bf16[96,384]{1,0:T(8,128)(2,1)S(1)}, bf16[96,384]{1,0:T(8,128)(2,1)S(1)}, u32[]{:S(2)}, u32[]{:S(2)}) collective-permute-start(bf16[96,384]{1,0:T(8,128)(2,1)S(1)} %get-tuple-element.33), channel_id=1, source_target_pairs={{0,22},{2,20},{4,18},{6,16},{8,30},{10,28},{12,26},{14,24},{16,6},... | collective-permute-start | bytes 221192 | tf_op jit(solution)/shard_map/ppermute | solution.py:96
  24.6 14.7 %collective-permute-start.11 = (bf16[96,384]{1,0:T(8,128)(2,1)S(1)}, bf16[96,384]{1,0:T(8,128)(2,1)S(1)}, u32[]{:S(2)}, u32[]{:S(2)}) collective-permute-start(bf16[96,384]{1,0:T(8,128)(2,1)S(1)} %get-tuple-element.32), channel_id=1, source_target_pairs={{0,24},{2,26},{4,28},{6,30},{8,16},{10,18},{12,20},{14,22},{16,8},... | collective-permute-start | bytes 221192 | tf_op jit(solution)/shard_map/ppermute | solution.py:96
  27.6 11.8 %collective-permute-start.12 = (bf16[96,384]{1,0:T(8,128)(2,1)S(1)}, bf16[96,384]{1,0:T(8,128)(2,1)S(1)}, u32[]{:S(2)}, u32[]{:S(2)}) collective-permute-start(bf16[96,384]{1,0:T(8,128)(2,1)S(1)} %get-tuple-element.31), channel_id=1, source_target_pairs={{0,26},{2,24},{4,30},{6,28},{8,18},{10,16},{12,22},{14,20},{16,10}... | collective-permute-start | bytes 221192 | tf_op jit(solution)/shard_map/ppermute | solution.py:96
  33.1 7.1 %collective-permute-start.13 = (bf16[96,384]{1,0:T(8,128)(2,1)S(1)}, bf16[96,384]{1,0:T(8,128)(2,1)S(1)}, u32[]{:S(2)}, u32[]{:S(2)}) collective-permute-start(bf16[96,384]{1,0:T(8,128)(2,1)S(1)} %get-tuple-element.30), channel_id=1, source_target_pairs={{0,28},{2,30},{4,24},{6,26},{8,20},{10,22},{12,16},{14,18},{16,12}... | collective-permute-start | bytes 221192 | tf_op jit(solution)/shard_map/ppermute | solution.py:96
  36.8 7.2 %collective-permute-start.14 = (bf16[96,384]{1,0:T(8,128)(2,1)S(1)}, bf16[96,384]{1,0:T(8,128)(2,1)S(1)}, u32[]{:S(2)}, u32[]{:S(2)}) collective-permute-start(bf16[96,384]{1,0:T(8,128)(2,1)S(1)} %get-tuple-element.29), channel_id=1, source_target_pairs={{0,30},{2,28},{4,26},{6,24},{8,22},{10,20},{12,18},{14,16},{16,14}... | collective-permute-start | bytes 221192 | tf_op jit(solution)/shard_map/ppermute | solution.py:96
  45.1 15.5 %collective-permute-start.15 = (bf16[384,512]{1,0:T(8,128)(2,1)S(1)}, bf16[384,512]{1,0:T(8,128)(2,1)S(1)}, u32[]{:S(2)}, u32[]{:S(2)}) collective-permute-start(bf16[384,512]{1,0:T(8,128)(2,1)S(1)} %fusion.2.refs_0_), channel_id=1, source_target_pairs={{0,8},{2,10},{4,12},{6,14},{8,16},{10,18},{12,20},{14,22},{16,24},... | collective-permute-start | bytes 1179656 | tf_op jit(solution)/shard_map/ppermute | solution.py:366
  51.9 12.7 %collective-permute-start.18 = (bf16[384,512]{1,0:T(8,128)(2,1)S(1)}, bf16[384,512]{1,0:T(8,128)(2,1)S(1)}, u32[]{:S(2)}, u32[]{:S(2)}) collective-permute-start(bf16[384,512]{1,0:T(8,128)(2,1)S(1)} %fusion.2.refs_0_), channel_id=1, source_target_pairs={{8,0},{10,2},{12,4},{14,6},{16,8},{18,10},{20,12},{22,14},{24,16},... | collective-permute-start | bytes 1179656 | tf_op jit(solution)/shard_map/ppermute | solution.py:367
  53.3 12.6 %collective-permute-start.24 = (bf16[384,512]{1,0:T(8,128)(2,1)S(1)}, bf16[384,512]{1,0:T(8,128)(2,1)S(1)}, u32[]{:S(2)}, u32[]{:S(2)}) collective-permute-start(bf16[384,512]{1,0:T(8,128)(2,1)S(1)} %fusion.2.refs_0_), channel_id=1, source_target_pairs={{0,2},{2,0},{4,6},{6,4},{8,10},{10,8},{12,14},{14,12},{16,18},{18,... | collective-permute-start | bytes 1179656 | tf_op jit(solution)/shard_map/ppermute | solution.py:96
  53.4 13.9 %collective-permute-start.25 = (bf16[384,512]{1,0:T(8,128)(2,1)S(1)}, bf16[384,512]{1,0:T(8,128)(2,1)S(1)}, u32[]{:S(2)}, u32[]{:S(2)}) collective-permute-start(bf16[384,512]{1,0:T(8,128)(2,1)S(1)} %fusion.2.refs_0_), channel_id=1, source_target_pairs={{0,4},{2,6},{4,0},{6,2},{8,12},{10,14},{12,8},{14,10},{16,20},{18,... | collective-permute-start | bytes 1179656 | tf_op jit(solution)/shard_map/ppermute | solution.py:96
  64.7 17.1 %collective-permute-start.27 = (bf16[384,512]{1,0:T(8,128)(2,1)S(1)}, bf16[384,512]{1,0:T(8,128)(2,1)S(1)}, u32[]{:S(2)}, u32[]{:S(2)}) collective-permute-start(bf16[384,512]{1,0:T(8,128)(2,1)S(1)} %broadcast_select_fusion.refs_4_), channel_id=1, source_target_pairs={{0,2},{2,0},{4,6},{6,4},{8,10},{10,8},{12,14},{14,12},{16,18},{18,... | collective-permute-start | bytes 1179656 | tf_op jit(solution)/shard_map/ppermute | solution.py:96
  64.8 18.1 %collective-permute-start.28 = (bf16[384,512]{1,0:T(8,128)(2,1)S(1)}, bf16[384,512]{1,0:T(8,128)(2,1)S(1)}, u32[]{:S(2)}, u32[]{:S(2)}) collective-permute-start(bf16[384,512]{1,0:T(8,128)(2,1)S(1)} %broadcast_select_fusion.refs_4_), channel_id=1, source_target_pairs={{0,4},{2,6},{4,0},{6,2},{8,12},{10,14},{12,8},{14,10},{16,20},{18,... | collective-permute-start | bytes 1179656 | tf_op jit(solution)/shard_map/ppermute | solution.py:96
  66.0 14.2 %collective-permute-start.19 = (bf16[384,512]{1,0:T(8,128)(2,1)S(1)}, bf16[384,512]{1,0:T(8,128)(2,1)S(1)}, u32[]{:S(2)}, u32[]{:S(2)}) collective-permute-start(bf16[384,512]{1,0:T(8,128)(2,1)S(1)} %collective-permute-done.18), channel_id=1, source_target_pairs={{8,0},{10,2},{12,4},{14,6},{16,8},{18,10},{20,12},{22,14},{9,1},{1... | collective-permute-start | bytes 1179656 | tf_op jit(solution)/shard_map/ppermute | solution.py:367
  67.3 42.6 %collective-permute-start.26 = (bf16[384,512]{1,0:T(8,128)(2,1)S(1)}, bf16[384,512]{1,0:T(8,128)(2,1)S(1)}, u32[]{:S(2)}, u32[]{:S(2)}) collective-permute-start(bf16[384,512]{1,0:T(8,128)(2,1)S(1)} %collective-permute-done.25.refs_2_), channel_id=1, source_target_pairs={{0,2},{2,0},{4,6},{6,4},{8,10},{10,8},{12,14},{14,12},{16,18},{18,... | collective-permute-start | bytes 1179656 | tf_op jit(solution)/shard_map/ppermute | solution.py:96
  80.2 15.9 %collective-permute-start.30 = (bf16[384,512]{1,0:T(8,128)(2,1)S(1)}, bf16[384,512]{1,0:T(8,128)(2,1)S(1)}, u32[]{:S(2)}, u32[]{:S(2)}) collective-permute-start(bf16[384,512]{1,0:T(8,128)(2,1)S(1)} %select_select_fusion.refs_8_), channel_id=1, source_target_pairs={{0,2},{2,0},{4,6},{6,4},{8,10},{10,8},{12,14},{14,12},{16,18},{18,... | collective-permute-start | bytes 1179656 | tf_op jit(solution)/shard_map/ppermute | solution.py:96
  80.3 16.5 %collective-permute-start.31 = (bf16[384,512]{1,0:T(8,128)(2,1)S(1)}, bf16[384,512]{1,0:T(8,128)(2,1)S(1)}, u32[]{:S(2)}, u32[]{:S(2)}) collective-permute-start(bf16[384,512]{1,0:T(8,128)(2,1)S(1)} %select_select_fusion.refs_8_), channel_id=1, source_target_pairs={{0,4},{2,6},{4,0},{6,2},{8,12},{10,14},{12,8},{14,10},{16,20},{18,... | collective-permute-start | bytes 1179656 | tf_op jit(solution)/shard_map/ppermute | solution.py:96
  83.0 13.1 %collective-permute-start.20 = (bf16[384,512]{1,0:T(8,128)(2,1)S(1)}, bf16[384,512]{1,0:T(8,128)(2,1)S(1)}, u32[]{:S(2)}, u32[]{:S(2)}) collective-permute-start(bf16[384,512]{1,0:T(8,128)(2,1)S(1)} %collective-permute-done.19), channel_id=1, source_target_pairs={{8,0},{10,2},{12,4},{14,6},{9,1},{11,3},{13,5},{15,7}} | collective-permute-start | bytes 1179656 | tf_op jit(solution)/shard_map/ppermute | solution.py:367
  85.0 13.1 %collective-permute-start.29 = (bf16[384,512]{1,0:T(8,128)(2,1)S(1)}, bf16[384,512]{1,0:T(8,128)(2,1)S(1)}, u32[]{:S(2)}, u32[]{:S(2)}) collective-permute-start(bf16[384,512]{1,0:T(8,128)(2,1)S(1)} %collective-permute-done.28.refs_6_), channel_id=1, source_target_pairs={{0,2},{2,0},{4,6},{6,4},{8,10},{10,8},{12,14},{14,12},{16,18},{18,... | collective-permute-start | bytes 1179656 | tf_op jit(solution)/shard_map/ppermute | solution.py:96
  96.1 11.6 %collective-permute-start.21 = (bf16[384,512]{1,0:T(8,128)(2,1)S(1)}, bf16[384,512]{1,0:T(8,128)(2,1)S(1)}, u32[]{:S(2)}, u32[]{:S(2)}) collective-permute-start(bf16[384,512]{1,0:T(8,128)(2,1)S(1)} %select_select_fusion.1.refs_0_), channel_id=1, source_target_pairs={{0,2},{2,0},{4,6},{6,4},{8,10},{10,8},{12,14},{14,12},{16,18},{18,... | collective-permute-start | bytes 1179656 | tf_op jit(solution)/shard_map/ppermute | solution.py:96
  96.2 11.5 %collective-permute-start.22 = (bf16[384,512]{1,0:T(8,128)(2,1)S(1)}, bf16[384,512]{1,0:T(8,128)(2,1)S(1)}, u32[]{:S(2)}, u32[]{:S(2)}) collective-permute-start(bf16[384,512]{1,0:T(8,128)(2,1)S(1)} %select_select_fusion.1.refs_0_), channel_id=1, source_target_pairs={{0,4},{2,6},{4,0},{6,2},{8,12},{10,14},{12,8},{14,10},{16,20},{18,... | collective-permute-start | bytes 1179656 | tf_op jit(solution)/shard_map/ppermute | solution.py:96
  96.8 11.8 %collective-permute-start.32 = (bf16[384,512]{1,0:T(8,128)(2,1)S(1)}, bf16[384,512]{1,0:T(8,128)(2,1)S(1)}, u32[]{:S(2)}, u32[]{:S(2)}) collective-permute-start(bf16[384,512]{1,0:T(8,128)(2,1)S(1)} %collective-permute-done.31.refs_10_), channel_id=1, source_target_pairs={{0,2},{2,0},{4,6},{6,4},{8,10},{10,8},{12,14},{14,12},{16,18},{18,... | collective-permute-start | bytes 1179656 | tf_op jit(solution)/shard_map/ppermute | solution.py:96
  110.7 7.0 %collective-permute-start.33 = (f32[3,128,128]{2,1,0:T(8,128)S(1)}, f32[3,128,128]{2,1,0:T(8,128)S(1)}, u32[]{:S(2)}, u32[]{:S(2)}) collective-permute-start(f32[3,128,128]{2,1,0:T(8,128)S(1)} %maximum_select_fusion), channel_id=1, source_target_pairs={{0,1},{1,0},{2,3},{3,2},{4,5},{5,4},{6,7},{7,6},{8,9},{9,8},{10,11... | collective-permute-start | bytes 589832 | tf_op jit(solution)/shard_map/ppermute | solution.py:96
  117.7 19.2 %collective-permute-start.34 = (f32[3,128,128]{2,1,0:T(8,128)S(1)}, f32[3,128,128]{2,1,0:T(8,128)S(1)}, u32[]{:S(2)}, u32[]{:S(2)}) collective-permute-start(f32[3,128,128]{2,1,0:T(8,128)S(1)} %fusion.71), channel_id=1, source_target_pairs={{0,2},{2,0},{4,6},{6,4},{8,10},{10,8},{12,14},{14,12},{16,18},{18,... | collective-permute-start | bytes 589832 | tf_op jit(solution)/shard_map/ppermute | solution.py:96
  145.6 25.8 %collective-permute-start.35 = (f32[1024,256]{1,0:T(8,128)}, f32[1024,256]{1,0:T(8,128)S(1)}, u32[]{:S(2)}, u32[]{:S(2)}) collective-permute-start(f32[1024,256]{1,0:T(8,128)} %get-tuple-element.28), channel_id=1, source_target_pairs={{0,1},{1,0},{2,3},{3,2},{4,5},{5,4},{6,7},{7,6},{8,9},{9,8},{10,11... | collective-permute-start | bytes 3145736 | tf_op jit(solution)/shard_map/ppermute | solution.py:96
  (25 other events, 98.5 us)
where the time goes:
time: 174 us
  waiting for transfers between devices  77.6 us (45%)
  starting transfers between devices  47.3 us (27%)
  Pallas kernels  26.9 us (15%)
  matrix products  13 us (7%)
  other arithmetic  6.5 us (4%)
    ppermute x30, waiting for transfers between devices, exchange(): return lax.ppermute(value, axis, [(i, i ^ bit) for i in range(size)])  44.9 us
    ppermute x30, starting transfers between devices, exchange(): return lax.ppermute(value, axis, [(i, i ^ bit) for i in range(size)])  35.2 us
    ppermute x3, waiting for transfers between devices, lined_panel(): up = lax.ppermute(up, 'wide', falling)  26.4 us
    pallas_call x2, Pallas kernels, accumulate(): pl.pallas_call(kernel, in_specs=[pl.BlockSpec(memory_space=pltpu.SMEM)] +...  19.1 us
    ppermute x3, starting transfers between devices, lined_panel(): down = lax.ppermute(down, 'wide', rising)  8.19 us
    pallas_call x1, Pallas kernels, recur(): pl.pallas_call(functools.partial(recur_kernel, blocks), in_specs=[pl.Bloc...  7.87 us
    ppermute x3, waiting for transfers between devices, lined_panel(): down = lax.ppermute(down, 'wide', rising)  6.35 us
    dot_general x2, matrix products, own_rows(): jnp.dot(chosen, source, preferred_element_type=jnp.float32)  6.04 us
  transfers between devices with their start and end apart: 36, of which 12 were waited for; matrix products, arithmetic and copies ran while one was open for 4% of the time, Pallas kernels for 11%

commit v1 on v0

v1 whole, which is shorter than its diff:
```python
import functools

import jax
import jax.numpy as jnp
from jax import lax
from jax.experimental import pallas as pl
from jax.experimental.pallas import tpu as pltpu
from jax.sharding import PartitionSpec as P


LANES = 128
SUBLANES = 16
GROUP = 4
ONE_CUT = True
SENDS = 2
TILES = 2
EXACT = lax.Precision.HIGHEST


def panel_factor(density, diag_block, inv_tiles):
    block_size = inv_tiles.shape[1]
    piv_parts = []
    new_parts = []
    for block_index in range(inv_tiles.shape[0]):
        low_edge = block_index * block_size
        high_edge = low_edge + block_size
        piv_rest = diag_block[:, low_edge:high_edge]
        new_rest = density[:, low_edge:high_edge]
        if block_index > 0:
            piv_left = jnp.concatenate(piv_parts, axis=1)
            new_left = jnp.concatenate(new_parts, axis=1)
            coupling = piv_left[low_edge:high_edge]
            piv_rest = piv_rest - jnp.dot(piv_left, coupling.T, precision=EXACT)
            new_rest = new_rest - jnp.dot(new_left, coupling.T, precision=EXACT)
        piv_parts.append(jnp.dot(piv_rest, inv_tiles[block_index], precision=EXACT))
        new_parts.append(jnp.dot(new_rest, inv_tiles[block_index], precision=EXACT))
    return jnp.concatenate(new_parts, axis=1)


def general(coeffs, earlier, inv_tiles, piv_local, piv_owner):
    owners = piv_owner[:, 0]
    panel_width = piv_local.shape[0]
    mine = owners == lax.axis_index("wide")
    capacity = 3 * panel_width // lax.axis_size("wide")
    positions = jnp.arange(panel_width, dtype=jnp.int32)
    same_owner = owners[:, None] == owners[None, :]
    before = positions[None, :] < positions[:, None]
    slot_rank = jnp.sum(same_owner & before, axis=1)
    slot_index = owners * capacity + slot_rank
    wanted = mine[None, :] & (slot_rank[None, :] == jnp.arange(capacity, dtype=jnp.int32)[:, None])
    local_rows = jnp.sum(jnp.where(wanted, piv_local[None, :], 0), axis=1)
    filled = jnp.any(wanted, axis=1)
    slots = [jnp.where(filled[:, None], source[local_rows], 0) for source in (coeffs, earlier)]
    pieces = [lax.all_gather(slot, "wide", axis=0, tiled=True) for slot in slots]
    select = slot_index[:, None] == jnp.arange(pieces[0].shape[0], dtype=jnp.int32)[None, :]
    select = select.astype(jnp.bfloat16)
    pivots = [
        jnp.dot(select, piece, preferred_element_type=jnp.float32).astype(jnp.bfloat16)
        for piece in pieces
    ]
    partial = [
        jnp.einsum("ro,po->rp", source, pivot, preferred_element_type=jnp.float32)
        for source, pivot in zip((coeffs, earlier), pivots)
    ]
    density = lax.psum_scatter(
        partial[0] - partial[1], "narrow", scatter_dimension=0, tiled=True
    )
    diag = [
        jnp.einsum("qo,po->qp", pivot, pivot, preferred_element_type=jnp.float32)
        for pivot in pivots
    ]
    diag_block = lax.psum(diag[0] - diag[1], "narrow")
    factor = panel_factor(density, diag_block, inv_tiles)
    return lax.all_to_all(factor, "narrow", split_axis=1, concat_axis=0, tiled=True)


def arrival_order(lines):
    tables = []
    for line in range(lines):
        order = []
        for hop in range(1, lines):
            sides = ("up", "down") if 2 * line < lines else ("down", "up")
            for side in sides:
                source = line + hop if side == "up" else line - hop
                if 0 <= source < lines:
                    order.append((side, hop, source))
        tables.append(order)
    return tables


def look_up(table, line):
    result = jnp.int32(table[-1])
    for index, entry in enumerate(table[:-1]):
        result = jnp.where(line == index, jnp.int32(entry), result)
    return result


def exchange(value, axis, bit, size):
    return lax.ppermute(value, axis, [(i, i ^ bit) for i in range(size)])


def lower_pairs(blocks):
    pairs = [(i, j) for i in range(blocks) for j in range(i)]
    half = len(pairs) // 2
    return pairs[:half], pairs[half:]


def near(values):
    return [pltpu.with_memory_space_constraint(value, pltpu.VMEM) for value in values]


def seat():
    me = lax.axis_index("wide")
    return lax.div(me, GROUP), lax.rem(me, GROUP)


def hold_copies(lane, pieces, held_ref, sems):
    width = pieces[0].shape[0]
    copies = []
    for index, piece in enumerate(pieces):
        start = pl.multiple_of((lane ^ index) * width, SUBLANES)
        target = held_ref.at[pl.ds(start, width), :]
        copies.append(pltpu.make_async_copy(piece, target, sems.at[index]))
    return copies


def add_lower(blocks, edge, lane, held_ref, old_ref, lower_ref):
    block = held_ref.shape[1] // blocks
    for parity, pairs in enumerate(lower_pairs(blocks)):

        @pl.when((lane & 1) == parity)
        def _():
            place = 0
            for i in sorted({pair[0] for pair in pairs}):
                picks = [pair[1] for pair in pairs if pair[0] == i]
                rows = slice(i * block, (i + 1) * block)
                columns = slice(picks[0] * block, (picks[-1] + 1) * block)
                terms = [
                    lax.dot_general(
                        held_ref[part, rows],
                        held_ref[part, columns],
                        (((0,), (0,)), ((), ())),
                        preferred_element_type=jnp.float32,
                    )
                    for part in (slice(0, edge), slice(edge, held_ref.shape[0]))
                ]
                total = terms[0] - terms[1]
                for index in range(len(picks)):
                    part = total[:, index * block : (index + 1) * block]
                    if old_ref is not None:
                        part = old_ref[place] + part
                    lower_ref[place] = part
                    place += 1


def lower_kernel(blocks, edge, bits, old_ref, *refs):
    pieces, lower_ref = refs[:-1], refs[-1]
    _, lane = seat()
    width, panel = pieces[0].shape
    block = panel // blocks
    signed = []
    for bit, piece in zip(bits, pieces):
        at = (lane ^ bit) * width + lax.broadcasted_iota(jnp.int32, (width, block), 0)
        signed.append(jnp.where(at < edge, 1.0, -1.0).astype(jnp.bfloat16))
    for parity, pairs in enumerate(lower_pairs(blocks)):

        @pl.when((lane & 1) == parity)
        def _():
            place = 0
            for i in sorted({pair[0] for pair in pairs}):
                picks = [pair[1] for pair in pairs if pair[0] == i]
                columns = slice(picks[0] * block, (picks[-1] + 1) * block)
                total = 0.0
                for sign, piece in zip(signed, pieces):
                    total = total + lax.dot_general(
                        piece[:, i * block : (i + 1) * block] * sign,
                        piece[:, columns],
                        (((0,), (0,)), ((), ())),
                        preferred_element_type=jnp.float32,
                    )
                for index in range(len(picks)):
                    part = total[:, index * block : (index + 1) * block]
                    lower_ref[place] = old_ref[place] + part
                    place += 1


def lower_only(blocks, edge, bits, old, pieces):
    vmem = pl.BlockSpec(memory_space=pltpu.VMEM)
    return pl.pallas_call(
        functools.partial(lower_kernel, blocks, edge, bits),
        in_specs=[vmem] * (1 + len(pieces)),
        out_specs=vmem,
        out_shape=jax.ShapeDtypeStruct(old.shape, jnp.float32),
        input_output_aliases={0: 0},
        name="lower",
    )(*near([old, *pieces]))


def accumulate_kernel(table, blocks, fresh, final, coeffs_ref, earlier_ref, *refs):
    pieces, refs = list(refs[:GROUP]), list(refs[GROUP:])
    old_sum_ref = None if fresh else refs.pop(0)
    old_lower_ref = None if fresh or final else refs.pop(0)
    sum_ref = refs.pop(0)
    lower_ref = None if final else refs.pop(0)
    held_ref, main_ref, sems = refs
    line, lane = seat()
    source = look_up(table, line)
    tile = main_ref.shape[0] // TILES
    depths = [ref.shape[1] // len(table) for ref in (coeffs_ref, earlier_ref)]
    holds = hold_copies(lane, pieces, held_ref, sems)
    loads = []
    for step in range(TILES):
        rows_at = pl.ds(step * tile, tile)
        place = 0
        for side, (ref, depth) in enumerate(zip((coeffs_ref, earlier_ref), depths)):
            base = pl.multiple_of(source * depth, LANES)
            loads.append(
                pltpu.make_async_copy(
                    ref.at[rows_at, pl.ds(base, depth)],
                    main_ref.at[rows_at, pl.ds(place, depth)],
                    sems.at[GROUP + 2 * step + side],
                )
            )
            place += depth
    for copy in holds + loads:
        copy.start()
    for copy in holds:
        copy.wait()
    if not final:
        add_lower(blocks, depths[0], lane, held_ref, old_lower_ref, lower_ref)
    for step in range(TILES):
        loads[2 * step].wait()
        loads[2 * step + 1].wait()
        rows_at = slice(step * tile, (step + 1) * tile)
        total = jnp.dot(main_ref[rows_at, :], held_ref[...], preferred_element_type=jnp.float32)
        sum_ref[rows_at, :] = total if fresh else old_sum_ref[rows_at, :] + total


def accumulate(table, blocks, coeffs, earlier, pieces, state, final):
    rows = coeffs.shape[0]
    width, panel = pieces[0].shape
    fresh = state is None
    block = panel // blocks
    shapes = [(rows, panel), (len(lower_pairs(blocks)[0]), block, block)]
    state = [] if fresh else list(state)
    if final:
        shapes, state = shapes[:1], state[:1]
    anywhere = pl.BlockSpec(memory_space=pl.ANY)
    vmem = pl.BlockSpec(memory_space=pltpu.VMEM)
    return pl.pallas_call(
        functools.partial(accumulate_kernel, table, blocks, fresh, final),
        in_specs=[anywhere] * (2 + GROUP) + [vmem] * len(state),
        out_specs=[vmem] * len(shapes),
        scratch_shapes=[
            pltpu.VMEM((width * GROUP, panel), jnp.bfloat16),
            pltpu.VMEM((rows, width * GROUP), jnp.bfloat16),
            pltpu.SemaphoreType.DMA((GROUP + 2 * TILES,)),
        ],
        out_shape=[jax.ShapeDtypeStruct(shape, jnp.float32) for shape in shapes],
        input_output_aliases={2 + GROUP + i: i for i in range(len(state))},
        cost_estimate=pl.CostEstimate(
            flops=2 * rows * panel * width * GROUP,
            bytes_accessed=2 * rows * width * GROUP,
            transcendentals=0,
        ),
        name="accumulate",
    )(coeffs, earlier, *pieces, *state)


def my_rows(capacity, owner_ref, local_ref):
    panel = owner_ref.shape[1]
    below = lax.broadcasted_iota(jnp.int32, (panel, panel), 0)
    across = lax.broadcasted_iota(jnp.int32, (panel, panel), 1)
    turned = owner_ref[...]
    owners = jnp.sum(jnp.where(below == across, turned, 0), axis=1, keepdims=True)
    same = (owners == turned) & (below < across)
    ranks = jnp.sum(jnp.where(same, 1, 0), axis=0, keepdims=True)
    slots = lax.broadcasted_iota(jnp.int32, (capacity, panel), 0)
    wanted = (ranks == slots) & (turned == lax.axis_index("wide"))
    return jnp.sum(jnp.where(wanted, local_ref[...] + 1, 0), axis=1, keepdims=True) - 1


def cut_kernel(hops, lines, owner_ref, local_ref, coeffs_ref, earlier_ref, *refs):
    outs, (main_ref, sems) = refs[:-2], refs[-2:]
    line, lane = seat()
    depths = [ref.shape[1] // lines for ref in (coeffs_ref, earlier_ref)]
    width = sum(depths) // GROUP
    copies = []
    for index, hop in enumerate(hops):
        place = 0
        for side, (ref, depth) in enumerate(zip((coeffs_ref, earlier_ref), depths)):
            base = pl.multiple_of((line ^ hop) * depth, LANES)
            source = ref.at[:, pl.ds(base, depth)]
            target = main_ref.at[index, :, pl.ds(place, depth)]
            copies.append(pltpu.make_async_copy(source, target, sems.at[index, side]))
            place += depth
    for copy in copies:
        copy.start()
    capacity = outs[0].shape[0]
    at = lax.broadcasted_iota(jnp.int32, (capacity, coeffs_ref.shape[0]), 1)
    select = my_rows(capacity, owner_ref, local_ref) == at
    select = jnp.where(select, 1.0, 0.0).astype(jnp.bfloat16)
    for index in range(len(hops)):
        copies[2 * index].wait()
        copies[2 * index + 1].wait()
        rows = jnp.dot(select, main_ref[index], preferred_element_type=jnp.float32)
        rows = jnp.concatenate([rows[:, : depths[0]], -rows[:, depths[0] :]], axis=1)
        rows = rows.astype(jnp.bfloat16)
        parts = [rows[:, i * width : (i + 1) * width] for i in range(GROUP)]
        for case in range(GROUP):

            @pl.when(lane == case)
            def _():
                for i, part in enumerate(parts):
                    outs[index * GROUP + (i ^ case)][...] = part


def cut(hops, lines, capacity, piv_owner, piv_local, coeffs, earlier):
    vmem = pl.BlockSpec(memory_space=pltpu.VMEM)
    anywhere = pl.BlockSpec(memory_space=pl.ANY)
    total = coeffs.shape[1] + earlier.shape[1]
    shape = jax.ShapeDtypeStruct((capacity, total // (lines * GROUP)), jnp.bfloat16)
    return pl.pallas_call(
        functools.partial(cut_kernel, hops, lines),
        in_specs=[vmem, vmem, anywhere, anywhere],
        out_specs=[vmem] * (len(hops) * GROUP),
        out_shape=[shape] * (len(hops) * GROUP),
        scratch_shapes=[
            pltpu.VMEM((len(hops), coeffs.shape[0], total // lines), jnp.bfloat16),
            pltpu.SemaphoreType.DMA((len(hops), 2)),
        ],
        name="cut",
    )(piv_owner.reshape(1, -1), piv_local[None, :], coeffs, earlier)


def choose(line, table, received):
    names = sorted(set(table))
    values = lax.optimization_barrier(tuple(received[name] for name in names))
    result = values[-1]
    for index, name in enumerate(names[:-1]):
        here = False
        for place, entry in enumerate(table):
            if entry == name:
                here = here | (line == place)
        result = jnp.where(here, values[index], result)
    return result


def split(value):
    high = value.astype(jnp.bfloat16)
    return high, (value - high.astype(jnp.float32)).astype(jnp.bfloat16)


def dot_split(left, right):
    left = jnp.concatenate([left[0], left[0], left[1]], axis=1)
    right = jnp.concatenate([right[0], right[1], right[0]], axis=0)
    return jnp.dot(left, right, preferred_element_type=jnp.float32)


def recur_kernel(blocks, partial_ref, mine_ref, other_ref, inv_ref, keep_ref, give_ref):
    block = inv_ref.shape[1]
    odd = (seat()[1] & 1) == 1
    right_side = lax.axis_index("narrow")
    lower = {}
    for parity, pairs in enumerate(lower_pairs(blocks)):
        here = odd if parity else jnp.logical_not(odd)
        for index, pair in enumerate(pairs):
            lower[pair] = jnp.where(here, mine_ref[index], other_ref[index])
    inverse = [split(inv_ref[j]) for j in range(blocks)]

    def stack(parts, axis):
        return tuple(jnp.concatenate(side, axis=axis) for side in zip(*parts))

    def flip(part):
        return tuple(jnp.transpose(side) for side in part)

    factor = {}
    for j in range(blocks - 1):
        rest = jnp.concatenate(
            [lower[i, j] for i in range(j + 1, blocks)], axis=0
        )
        if j:
            left = stack([stack([factor[i, k] for k in range(j)], 1) for i in range(j + 1, blocks)], 0)
            right = stack([flip(factor[j, k]) for k in range(j)], 0)
            rest = rest - dot_split(left, right)
        made = split(dot_split(split(rest), inverse[j]))
        for i in range(j + 1, blocks):
            rows = slice((i - j - 1) * block, (i - j) * block)
            factor[i, j] = (made[0][rows], made[1][rows])
    new = []
    for j in range(blocks):
        rest = partial_ref[:, j * block : (j + 1) * block]
        if j:
            right = stack([flip(factor[j, k]) for k in range(j)], 0)
            rest = rest - dot_split(stack(new, 1), right)
        result = dot_split(split(rest), inverse[j])
        new.append(split(result))
        half = blocks // 2
        mine = right_side == j // half
        place = pl.ds((j % half) * block, block)

        @pl.when(mine)
        def _():
            keep_ref[:, place] = result

        @pl.when(jnp.logical_not(mine))
        def _():
            give_ref[:, place] = result


def recur(index, partial, mine, other, inv_tiles):
    rows, panel = partial.shape
    blocks = inv_tiles.shape[0]
    rows = rows // SENDS
    half = jax.ShapeDtypeStruct((rows, panel // 2), jnp.float32)
    vmem = pl.BlockSpec(memory_space=pltpu.VMEM)
    return pl.pallas_call(
        functools.partial(recur_kernel, blocks),
        grid=(1,),
        in_specs=[pl.BlockSpec((rows, panel), lambda i: (index, 0)), vmem, vmem, vmem],
        out_specs=[vmem, vmem],
        out_shape=[half, half],
        name="recur",
    )(partial, mine, other, inv_tiles)


def finish_kernel(keep_ref, taken_ref, *refs):
    refs[-1][...] = keep_ref[...] + taken_ref[...]


def finish(index, keep, taken, result):
    rows, columns = keep.shape
    vmem = pl.BlockSpec(memory_space=pltpu.VMEM)
    anywhere = pl.BlockSpec(memory_space=pl.ANY)
    old = [] if result is None else [result]
    return pl.pallas_call(
        finish_kernel,
        grid=(1,),
        in_specs=[vmem, vmem] + [anywhere] * len(old),
        out_specs=pl.BlockSpec((rows, columns), lambda i: (index, 0)),
        out_shape=jax.ShapeDtypeStruct((rows * SENDS, columns), jnp.float32),
        input_output_aliases={2: 0} if old else {},
        name="finish",
    )(*near([keep, taken]), *old)


def lined(*args):
    return lined_panel(*args)


def lined_panel(coeffs, earlier, inv_tiles, piv_local, piv_owner):
    size = lax.axis_size("wide")
    lines = size // GROUP
    me = lax.axis_index("wide")
    line = me // GROUP
    panel = piv_local.shape[0]
    blocks = inv_tiles.shape[0]
    capacity = 3 * panel // size
    widths = [source.shape[1] // size for source in (coeffs, earlier)]
    edge = GROUP * widths[0]

    owners = piv_owner[:, 0]
    positions = jnp.arange(panel, dtype=jnp.int32)
    earlier_same = (owners[:, None] == owners[None, :]) & (positions[None, :] < positions[:, None])
    ranks = jnp.sum(earlier_same, axis=1, dtype=jnp.int32)
    hops = tuple(range(lines - 1, -1, -1))
    cuts = (hops,) if ONE_CUT else (hops[: lines // 2], hops[lines // 2 :])
    parts = {}
    for hops in cuts:
        made = cut(hops, lines, capacity, piv_owner, piv_local, coeffs, earlier)
        for index, hop in enumerate(hops):
            for bit in range(GROUP):
                parts[hop * GROUP + bit] = made[index * GROUP + bit]
    got = []
    for bit in range(size):
        got.append(exchange(parts[bit], "wide", bit, size) if bit else parts[bit])
    stacked = jnp.concatenate(got, axis=0)
    places = (owners ^ me) * capacity + ranks
    taken = places[:, None] == jnp.arange(size * capacity, dtype=jnp.int32)[None, :]
    own = lax.dot_general(
        stacked,
        taken.astype(jnp.bfloat16),
        (((0,), (1,)), ((), ())),
        preferred_element_type=jnp.float32,
    ).astype(jnp.bfloat16)

    up, down = own, own
    tables = arrival_order(lines)
    received = {}
    pieces = [own]
    sources = [tuple(range(lines))]
    for hop in range(1, lines):
        rising = [(i, i + GROUP) for i in range(size - GROUP) if i // GROUP >= hop - 1]
        falling = [(i, i - GROUP) for i in range(GROUP, size) if lines - 1 - i // GROUP >= hop - 1]
        down = lax.ppermute(down, "wide", rising)
        up = lax.ppermute(up, "wide", falling)
        received[("down", hop)] = down
        received[("up", hop)] = up
        pieces.append(choose(line, [tables[i][hop - 1][:2] for i in range(lines)], received))
        sources.append(tuple(tables[i][hop - 1][2] for i in range(lines)))

    groups = []
    for piece in pieces:
        across = exchange(piece, "wide", 2, size)
        beside = exchange(piece, "wide", 1, size)
        corner = exchange(across, "wide", 1, size)
        groups.append([piece, beside, across, corner])
    state = None
    for index, (source, group) in enumerate(zip(sources, groups)):
        final = index == lines - 1
        if final:
            mine = lower_only(blocks, edge, (0, 1), state[1], group[:2])
            mine = lower_only(blocks, edge, (2, 3), mine, group[2:])
        state = accumulate(source, blocks, coeffs, earlier, group, state, final)
    mine = mine + exchange(mine, "narrow", 1, 2)
    other = exchange(mine, "wide", 1, size)
    result = None
    for index in range(SENDS):
        keep, give = recur(index, state[0], mine, other, inv_tiles)
        taken = exchange(give, "narrow", 1, 2)
        result = finish(index, keep, taken, result)
    return result


def on_device(coeffs, earlier, inv_tiles, piv_local, piv_owner):
    chosen = lined if fits(coeffs, earlier, inv_tiles) else general
    return chosen(coeffs, earlier, inv_tiles, piv_local, piv_owner)


def fits(coeffs, earlier, inv_tiles):
    size = lax.axis_size("wide")
    lines = size // GROUP
    return (
        size == lines * GROUP
        and size & (size - 1) == 0
        and lines > 1
        and lax.axis_size("narrow") == 2
        and coeffs.shape[0] % (SUBLANES * TILES) == 0
        and coeffs.shape[1] % (lines * LANES) == 0
        and earlier.shape[1] % (lines * LANES) == 0
        and (coeffs.shape[1] + earlier.shape[1]) % (size * SUBLANES) == 0
        and inv_tiles.shape[0] % 4 == 0
    )


def solution(mesh):
    return jax.shard_map(
        on_device,
        mesh=mesh,
        in_specs=(P("wide", "narrow"), P("wide", "narrow"), P(), P(), P()),
        out_specs=P("wide", "narrow"),
        check_vma=False,
    )
```

time: 174 us -> 170 us (0.977)
  Pallas kernels: 26.9 us -> 46.2 us
  matrix products: 13 us -> 0.98 us
  waiting for transfers between devices: 77.6 us -> 67.8 us
  other arithmetic: 6.5 us -> 0.45 us
  starting transfers between devices: 47.3 us -> 49.6 us
  local copies, waits for them, and re-layouts: 1.37 us -> 3.67 us
    pallas_call x3 -> x11, Pallas kernels: 26.9 us -> 46.2 us  [the longest x4 25.5 us: accumulate(): pl.pallas_call(functools.partial(accumulate_kernel, table, blocks, fresh,...]
    dot_general x18 -> x0, matrix products: 12 us -> none  [the longest x2 6.04 us: own_rows(): jnp.dot(chosen, source, preferred_element_type=jnp.float32)]
    ppermute x3, waiting for transfers between devices: 26.4 us -> 20.6 us  [lined_panel(): up = lax.ppermute(up, 'wide', falling)]
    ppermute x30 -> x31, waiting for transfers between devices: 44.9 us -> 40.5 us  [exchange(): return lax.ppermute(value, axis, [(i, i ^ bit) for i in range(size)])]
    add x2 -> x0, other arithmetic: 3.01 us -> none  [the longest x1 2.33 us: lined_panel(): return keep + exchange(give, 'narrow', 1, 2)]
    ppermute x30 -> x31, starting transfers between devices: 35.2 us -> 37.9 us  [exchange(): return lax.ppermute(value, axis, [(i, i ^ bit) for i in range(size)])]
    unnamed x71 -> x57, local copies, waits for them, and re-layouts: 1.12 us -> 3.65 us
  transfers between devices with their start and end apart: 36 -> 37, of which waited for: 12 -> 11; matrix products, arithmetic and copies ran while one was open for 4% -> 1% of each run, Pallas kernels for 11% -> 19%
where the time goes in v1:
time: 170 us; the launch traced here: 169 us
  waiting for transfers between devices  67.8 us (40%)
  starting transfers between devices  49.6 us (29%)
  Pallas kernels  46.2 us (27%)
  local copies, waits for them, and re-layouts  3.67 us (2%)
    ppermute x31, waiting for transfers between devices, exchange(): return lax.ppermute(value, axis, [(i, i ^ bit) for i in range(size)])  40.5 us
    ppermute x31, starting transfers between devices, exchange(): return lax.ppermute(value, axis, [(i, i ^ bit) for i in range(size)])  37.9 us
    pallas_call x4, Pallas kernels, accumulate(): pl.pallas_call(functools.partial(accumulate_kernel, table, blocks, fresh,...  25.5 us
    ppermute x3, waiting for transfers between devices, lined_panel(): up = lax.ppermute(up, 'wide', falling)  20.6 us
    pallas_call x2, Pallas kernels, recur(): pl.pallas_call(functools.partial(recur_kernel, blocks), grid=(1,), in_spe...  11.3 us
    ppermute x3, starting transfers between devices, lined_panel(): down = lax.ppermute(down, 'wide', rising)  7.88 us
    pallas_call x1, Pallas kernels, cut(): pl.pallas_call(functools.partial(cut_kernel, hops, lines), in_specs=[vmem...  6.93 us
    ppermute x3, waiting for transfers between devices, lined_panel(): down = lax.ppermute(down, 'wide', rising)  6.62 us
  transfers between devices with their start and end apart: 37, of which 11 were waited for; matrix products, arithmetic and copies ran while one was open for 1% of the time, Pallas kernels for 19%

profile of v1, /device:TPU:0, one launch (start us, length us, event | category | flops | bytes accessed | tf_op | source)
XLA Modules:
  0.0 169.3 jit_solution(11162709640090113070)
XLA Ops:
  0.0 6.9 %cut.1 = (bf16[96,352]{1,0:T(8,128)(2,1)}, bf16[96,352]{1,0:T(8,128)(2,1)}, bf16[96,352]{1,0:T(8,128)(2,1)}, bf16[96,352]{1,0:T(8,128)(2,1)}, bf16[96,352]{1,0:T...) custom-call(s32[1,512]{1,0:T(1,128)} %bitcast.6, ...), custom_call_target="tpu_custom_call" | custom-call | tf_op jit(solution)/shard_map/cut/pallas_call | solution.py:323
  7.5 2.6 %collective-permute-start.1 = (bf16[96,352]{1,0:T(8,128)(2,1)}, bf16[96,352]{1,0:T(8,128)(2,1)S(1)}, u32[]{:S(2)}, u32[]{:S(2)}) collective-permute-start(bf16[96,352]{1,0:T(8,128)(2,1)} %get-tuple-element.43), channel_id=1, source_target_pairs={{0,4},{2,6},{4,0},{6,2},{8,12},{10,14},{12,8},{14,10},{16,20},{18,... | collective-permute-start | bytes 202760 | tf_op jit(solution)/shard_map/ppermute | solution.py:99
  10.1 1.8 %collective-permute-start.3 = (bf16[96,352]{1,0:T(8,128)(2,1)}, bf16[96,352]{1,0:T(8,128)(2,1)S(1)}, u32[]{:S(2)}, u32[]{:S(2)}) collective-permute-start(bf16[96,352]{1,0:T(8,128)(2,1)} %get-tuple-element.45), channel_id=1, source_target_pairs={{0,8},{2,10},{4,12},{6,14},{8,0},{10,2},{12,4},{14,6},{16,24},{18,... | collective-permute-start | bytes 202760 | tf_op jit(solution)/shard_map/ppermute | solution.py:99
  13.1 2.7 %collective-permute-start.5 = (bf16[96,352]{1,0:T(8,128)(2,1)}, bf16[96,352]{1,0:T(8,128)(2,1)S(1)}, u32[]{:S(2)}, u32[]{:S(2)}) collective-permute-start(bf16[96,352]{1,0:T(8,128)(2,1)} %get-tuple-element.47), channel_id=1, source_target_pairs={{0,12},{2,14},{4,8},{6,10},{8,4},{10,6},{12,0},{14,2},{16,28},{18,... | collective-permute-start | bytes 202760 | tf_op jit(solution)/shard_map/ppermute | solution.py:99
  16.0 2.7 %collective-permute-start.7 = (bf16[96,352]{1,0:T(8,128)(2,1)}, bf16[96,352]{1,0:T(8,128)(2,1)S(1)}, u32[]{:S(2)}, u32[]{:S(2)}) collective-permute-start(bf16[96,352]{1,0:T(8,128)(2,1)} %get-tuple-element.49), channel_id=1, source_target_pairs={{0,16},{2,18},{4,20},{6,22},{8,24},{10,26},{12,28},{14,30},{16,0},... | collective-permute-start | bytes 202760 | tf_op jit(solution)/shard_map/ppermute | solution.py:99
  19.0 3.5 %collective-permute-start.9 = (bf16[96,352]{1,0:T(8,128)(2,1)}, bf16[96,352]{1,0:T(8,128)(2,1)S(1)}, u32[]{:S(2)}, u32[]{:S(2)}) collective-permute-start(bf16[96,352]{1,0:T(8,128)(2,1)} %get-tuple-element.51), channel_id=1, source_target_pairs={{0,20},{2,22},{4,16},{6,18},{8,28},{10,30},{12,24},{14,26},{16,4},... | collective-permute-start | bytes 202760 | tf_op jit(solution)/shard_map/ppermute | solution.py:99
  22.7 3.6 %collective-permute-start.11 = (bf16[96,352]{1,0:T(8,128)(2,1)}, bf16[96,352]{1,0:T(8,128)(2,1)S(1)}, u32[]{:S(2)}, u32[]{:S(2)}) collective-permute-start(bf16[96,352]{1,0:T(8,128)(2,1)} %get-tuple-element.53), channel_id=1, source_target_pairs={{0,24},{2,26},{4,28},{6,30},{8,16},{10,18},{12,20},{14,22},{16,8},... | collective-permute-start | bytes 202760 | tf_op jit(solution)/shard_map/ppermute | solution.py:99
  26.4 6.4 %collective-permute-start.12 = (bf16[96,352]{1,0:T(8,128)(2,1)S(1)}, bf16[96,352]{1,0:T(8,128)(2,1)S(1)}, u32[]{:S(2)}, u32[]{:S(2)}) collective-permute-start(bf16[96,352]{1,0:T(8,128)(2,1)S(1)} %copy-done.20), channel_id=1, source_target_pairs={{0,26},{2,24},{4,30},{6,28},{8,18},{10,16},{12,22},{14,20},{16,10}... | collective-permute-start | bytes 202760 | tf_op jit(solution)/shard_map/ppermute | solution.py:99
  32.8 2.9 %collective-permute-start.13 = (bf16[96,352]{1,0:T(8,128)(2,1)S(1)}, bf16[96,352]{1,0:T(8,128)(2,1)S(1)}, u32[]{:S(2)}, u32[]{:S(2)}) collective-permute-start(bf16[96,352]{1,0:T(8,128)(2,1)S(1)} %copy-done.19), channel_id=1, source_target_pairs={{0,28},{2,30},{4,24},{6,26},{8,20},{10,22},{12,16},{14,18},{16,12}... | collective-permute-start | bytes 202760 | tf_op jit(solution)/shard_map/ppermute | solution.py:99
  35.7 2.3 %collective-permute-start.14 = (bf16[96,352]{1,0:T(8,128)(2,1)S(1)}, bf16[96,352]{1,0:T(8,128)(2,1)S(1)}, u32[]{:S(2)}, u32[]{:S(2)}) collective-permute-start(bf16[96,352]{1,0:T(8,128)(2,1)S(1)} %copy-done.18), channel_id=1, source_target_pairs={{0,30},{2,28},{4,26},{6,24},{8,22},{10,20},{12,18},{14,16},{16,14}... | collective-permute-start | bytes 202760 | tf_op jit(solution)/shard_map/ppermute | solution.py:99
  38.1 2.7 %collective-permute-done.13 = bf16[96,352]{1,0:T(8,128)(2,1)S(1)} collective-permute-done((bf16[96,352]{1,0:T(8,128)(2,1)S(1)}, bf16[96,352]{1,0:T(8,128)(2,1)S(1)}, u32[]{:S(2)}, u32[]{:S(2)}) %collective-permute-start.13) | collective-permute-done | bytes 67616 | tf_op jit(solution)/shard_map/ppermute | solution.py:99
  40.8 2.3 %collective-permute-done.14 = bf16[96,352]{1,0:T(8,128)(2,1)S(1)} collective-permute-done((bf16[96,352]{1,0:T(8,128)(2,1)S(1)}, bf16[96,352]{1,0:T(8,128)(2,1)S(1)}, u32[]{:S(2)}, u32[]{:S(2)}) %collective-permute-start.14) | collective-permute-done | bytes 67616 | tf_op jit(solution)/shard_map/ppermute | solution.py:99
  44.1 6.5 %collective-permute-start.15 = (bf16[352,512]{1,0:T(8,128)(2,1)S(1)}, bf16[352,512]{1,0:T(8,128)(2,1)S(1)}, u32[]{:S(2)}, u32[]{:S(2)}) collective-permute-start(bf16[352,512]{1,0:T(8,128)(2,1)S(1)} %fusion.2.refs_0_), channel_id=1, source_target_pairs={{0,8},{2,10},{4,12},{6,14},{8,16},{10,18},{12,20},{14,22},{16,24},... | collective-permute-start | bytes 1081352 | tf_op jit(solution)/shard_map/ppermute | solution.py:495
  50.7 1.3 collective-permute-start.18
  52.0 6.6 %collective-permute-done.15 = bf16[352,512]{1,0:T(8,128)(2,1)S(1)} collective-permute-done((bf16[352,512]{1,0:T(8,128)(2,1)S(1)}, bf16[352,512]{1,0:T(8,128)(2,1)S(1)}, u32[]{:S(2)}, u32[]{:S(2)}) %collective-permute-start.15) | collective-permute-done | bytes 360480 | tf_op jit(solution)/shard_map/ppermute | solution.py:495
  59.3 3.5 %collective-permute-done.18 = bf16[352,512]{1,0:T(8,128)(2,1)S(1)} collective-permute-done((bf16[352,512]{1,0:T(8,128)(2,1)S(1)}, bf16[352,512]{1,0:T(8,128)(2,1)S(1)}, u32[]{:S(2)}, u32[]{:S(2)}) %collective-permute-start.18) | collective-permute-done | bytes 360480 | tf_op jit(solution)/shard_map/ppermute | solution.py:496
  65.3 9.0 %collective-permute-done.19 = bf16[352,512]{1,0:T(8,128)(2,1)S(1)} collective-permute-done((bf16[352,512]{1,0:T(8,128)(2,1)S(1)}, bf16[352,512]{1,0:T(8,128)(2,1)S(1)}, u32[]{:S(2)}, u32[]{:S(2)}) %collective-permute-start.19) | collective-permute-done | bytes 360480 | tf_op jit(solution)/shard_map/ppermute | solution.py:496
  76.8 8.1 %collective-permute-done.20 = bf16[352,512]{1,0:T(8,128)(2,1)S(1)} collective-permute-done((bf16[352,512]{1,0:T(8,128)(2,1)S(1)}, bf16[352,512]{1,0:T(8,128)(2,1)S(1)}, u32[]{:S(2)}, u32[]{:S(2)}) %collective-permute-start.20) | collective-permute-done | bytes 360480 | tf_op jit(solution)/shard_map/ppermute | solution.py:496
  85.4 1.7 %collective-permute-start.22 = (bf16[352,512]{1,0:T(8,128)(2,1)S(1)}, bf16[352,512]{1,0:T(8,128)(2,1)S(1)}, u32[]{:S(2)}, u32[]{:S(2)}) collective-permute-start(bf16[352,512]{1,0:T(8,128)(2,1)S(1)} %select_select_fusion.1.refs_0_), channel_id=1, source_target_pairs={{0,4},{2,6},{4,0},{6,2},{8,12},{10,14},{12,8},{14,10},{16,20},{18,... | collective-permute-start | bytes 1081352 | tf_op jit(solution)/shard_map/ppermute | solution.py:99
  87.6 8.7 %collective-permute-done.25.refs_2_ = bf16[352,512]{1,0:T(8,128)(2,1)} collective-permute-done((bf16[352,512]{1,0:T(8,128)(2,1)S(1)}, bf16[352,512]{1,0:T(8,128)(2,1)}, u32[]{:S(2)}, u32[]{:S(2)}) %collective-permute-start.25) | collective-permute-done | bytes 360480 | tf_op jit(solution)/shard_map/ppermute | solution.py:99
  96.8 3.8 %collective-permute-done.22.refs_2_.refs_0_ = bf16[352,512]{1,0:T(8,128)(2,1)S(1)} collective-permute-done((bf16[352,512]{1,0:T(8,128)(2,1)S(1)}, bf16[352,512]{1,0:T(8,128)(2,1)S(1)}, u32[]{:S(2)}, u32[]{:S(2)}) %collective-permute-start.22) | collective-permute-done | bytes 360480 | tf_op jit(solution)/shard_map/ppermute | solution.py:99
  100.7 5.2 %accumulate.4 = (f32[1024,512]{1,0:T(8,128)}, f32[3,128,128]{2,1,0:T(8,128)}) custom-call(bf16[1024,4608]{1,0:T(8,128)(2,1)} %coeffs_ref.9, bf16[1024,1024]{1,0:T(8,128)(2,1)} %earlier_ref.9, bf16[352,512]{1,0:T(8,128)(2,1)} %copy-done.11, bf16[352,512]{1,0:T(8,128)(2,1)} %copy-done.13, bf16[352,512]{1,0:T(8,128)(2,1)} %copy-done.12, bf16[352,512]{1,0:T(8,128)(2,1)} %copy-done.14), custom_call_target="tpu_custom_call" | custom-call | flops 1476395008 | bytes 2883584 | tf_op jit(solution)/shard_map/accumulate/pallas_call | solution.py:250
  105.9 6.9 %accumulate.5 = (f32[1024,512]{1,0:T(8,128)}, f32[3,128,128]{2,1,0:T(8,128)}) custom-call(bf16[1024,4608]{1,0:T(8,128)(2,1)} %coeffs_ref.9, bf16[1024,1024]{1,0:T(8,128)(2,1)} %earlier_ref.9, bf16[352,512]{1,0:T(8,128)(2,1)} %copy-done.8, bf16[352,512]{1,0:T(8,128)(2,1)} %copy-done.15, ...), custom_call_target="tpu_custom_call", output_to_operand_aliasing={{0}: (6, {}), {1}: (7, {})} | custom-call | flops 1476395008 | bytes 2883584 | tf_op jit(solution)/shard_map/accumulate/pallas_call | solution.py:250
  113.5 6.7 %accumulate.6 = (f32[1024,512]{1,0:T(8,128)}, f32[3,128,128]{2,1,0:T(8,128)}) custom-call(bf16[1024,4608]{1,0:T(8,128)(2,1)} %coeffs_ref.9, bf16[1024,1024]{1,0:T(8,128)(2,1)} %earlier_ref.9, bf16[352,512]{1,0:T(8,128)(2,1)} %copy-done.9, bf16[352,512]{1,0:T(8,128)(2,1)} %copy-done.16, ...), custom_call_target="tpu_custom_call", output_to_operand_aliasing={{0}: (6, {}), {1}: (7, {})} | custom-call | flops 1476395008 | bytes 2883584 | tf_op jit(solution)/shard_map/accumulate/pallas_call | solution.py:250
  122.2 1.6 collective-permute-start.33
  123.8 5.7 %collective-permute-done.33 = f32[3,128,128]{2,1,0:T(8,128)S(1)} collective-permute-done((f32[3,128,128]{2,1,0:T(8,128)S(1)}, f32[3,128,128]{2,1,0:T(8,128)S(1)}, u32[]{:S(2)}, u32[]{:S(2)}) %collective-permute-start.33) | collective-permute-done | bytes 196640 | tf_op jit(solution)/shard_map/ppermute | solution.py:99
  129.7 6.7 %accumulate.7.partial_ref = f32[1024,512]{1,0:T(8,128)} custom-call(bf16[1024,4608]{1,0:T(8,128)(2,1)} %coeffs_ref.9, bf16[1024,1024]{1,0:T(8,128)(2,1)} %earlier_ref.9, bf16[352,512]{1,0:T(8,128)(2,1)} %copy-done.1, bf16[352,512]{1,0:T(8,128)(2,1)} %copy-done.3, bf16[352,512]{1,0:T(8,128)(2,1)} %copy-done.2, ...), custom_call_target="tpu_custom_call", output_to_operand_aliasing={{}: (6, {})} | custom-call | flops 1476395008 | bytes 2883584 | tf_op jit(solution)/shard_map/accumulate/pallas_call | solution.py:250
  137.1 5.6 %recur.3 = (f32[512,256]{1,0:T(8,128)}, f32[512,256]{1,0:T(8,128)}) custom-call(f32[1024,512]{1,0:T(8,128)} %accumulate.7.partial_ref, f32[3,128,128]{2,1,0:T(8,128)} %copy-done.7, f32[3,128,128]{2,1,0:T(8,128)} %copy-done.10, f32[4,128,128]{2,1,0:T(8,128)} %inv_ref.3), custom_call_target="tpu_custom_call" | custom-call | tf_op jit(solution)/shard_map/recur/pallas_call | solution.py:417
  142.7 1.5 collective-permute-start.36
  144.2 5.6 %recur.2 = (f32[512,256]{1,0:T(8,128)}, f32[512,256]{1,0:T(8,128)}) custom-call(f32[1024,512]{1,0:T(8,128)} %accumulate.7.partial_ref, f32[3,128,128]{2,1,0:T(8,128)} %copy-done.7, f32[3,128,128]{2,1,0:T(8,128)} %copy-done.10, f32[4,128,128]{2,1,0:T(8,128)} %inv_ref.3), custom_call_target="tpu_custom_call" | custom-call | tf_op jit(solution)/shard_map/recur/pallas_call | solution.py:417
  150.4 7.3 %collective-permute-done.36.taken_ref = f32[512,256]{1,0:T(8,128)S(1)} collective-permute-done((f32[512,256]{1,0:T(8,128)}, f32[512,256]{1,0:T(8,128)S(1)}, u32[]{:S(2)}, u32[]{:S(2)}) %collective-permute-start.36) | collective-permute-done | bytes 524320 | tf_op jit(solution)/shard_map/ppermute | solution.py:99
  158.6 9.9 %collective-permute-done.35.taken_ref = f32[512,256]{1,0:T(8,128)S(1)} collective-permute-done((f32[512,256]{1,0:T(8,128)}, f32[512,256]{1,0:T(8,128)S(1)}, u32[]{:S(2)}, u32[]{:S(2)}) %collective-permute-start.35) | collective-permute-done | bytes 524320 | tf_op jit(solution)/shard_map/ppermute | solution.py:99
  (118 shorter events, 16.2 us)
Async XLA Ops:
  7.5 8.3 %collective-permute-start.1 = (bf16[96,352]{1,0:T(8,128)(2,1)}, bf16[96,352]{1,0:T(8,128)(2,1)S(1)}, u32[]{:S(2)}, u32[]{:S(2)}) collective-permute-start(bf16[96,352]{1,0:T(8,128)(2,1)} %get-tuple-element.43), channel_id=1, source_target_pairs={{0,4},{2,6},{4,0},{6,2},{8,12},{10,14},{12,8},{14,10},{16,20},{18,... | collective-permute-start | bytes 202760 | tf_op jit(solution)/shard_map/ppermute | solution.py:99
  10.1 8.6 %collective-permute-start.3 = (bf16[96,352]{1,0:T(8,128)(2,1)}, bf16[96,352]{1,0:T(8,128)(2,1)S(1)}, u32[]{:S(2)}, u32[]{:S(2)}) collective-permute-start(bf16[96,352]{1,0:T(8,128)(2,1)} %get-tuple-element.45), channel_id=1, source_target_pairs={{0,8},{2,10},{4,12},{6,14},{8,0},{10,2},{12,4},{14,6},{16,24},{18,... | collective-permute-start | bytes 202760 | tf_op jit(solution)/shard_map/ppermute | solution.py:99
  11.9 7.1 %collective-permute-start.4 = (bf16[96,352]{1,0:T(8,128)(2,1)}, bf16[96,352]{1,0:T(8,128)(2,1)S(1)}, u32[]{:S(2)}, u32[]{:S(2)}) collective-permute-start(bf16[96,352]{1,0:T(8,128)(2,1)} %get-tuple-element.46), channel_id=1, source_target_pairs={{0,10},{2,8},{4,14},{6,12},{8,2},{10,0},{12,6},{14,4},{16,26},{18,... | collective-permute-start | bytes 202760 | tf_op jit(solution)/shard_map/ppermute | solution.py:99
  13.1 9.4 %collective-permute-start.5 = (bf16[96,352]{1,0:T(8,128)(2,1)}, bf16[96,352]{1,0:T(8,128)(2,1)S(1)}, u32[]{:S(2)}, u32[]{:S(2)}) collective-permute-start(bf16[96,352]{1,0:T(8,128)(2,1)} %get-tuple-element.47), channel_id=1, source_target_pairs={{0,12},{2,14},{4,8},{6,10},{8,4},{10,6},{12,0},{14,2},{16,28},{18,... | collective-permute-start | bytes 202760 | tf_op jit(solution)/shard_map/ppermute | solution.py:99
  16.0 10.3 %collective-permute-start.7 = (bf16[96,352]{1,0:T(8,128)(2,1)}, bf16[96,352]{1,0:T(8,128)(2,1)S(1)}, u32[]{:S(2)}, u32[]{:S(2)}) collective-permute-start(bf16[96,352]{1,0:T(8,128)(2,1)} %get-tuple-element.49), channel_id=1, source_target_pairs={{0,16},{2,18},{4,20},{6,22},{8,24},{10,26},{12,28},{14,30},{16,0},... | collective-permute-start | bytes 202760 | tf_op jit(solution)/shard_map/ppermute | solution.py:99
  18.8 14.0 %collective-permute-start.8 = (bf16[96,352]{1,0:T(8,128)(2,1)}, bf16[96,352]{1,0:T(8,128)(2,1)S(1)}, u32[]{:S(2)}, u32[]{:S(2)}) collective-permute-start(bf16[96,352]{1,0:T(8,128)(2,1)} %get-tuple-element.50), channel_id=1, source_target_pairs={{0,18},{2,16},{4,22},{6,20},{8,26},{10,24},{12,30},{14,28},{16,2},... | collective-permute-start | bytes 202760 | tf_op jit(solution)/shard_map/ppermute | solution.py:99
  19.0 16.7 %collective-permute-start.9 = (bf16[96,352]{1,0:T(8,128)(2,1)}, bf16[96,352]{1,0:T(8,128)(2,1)S(1)}, u32[]{:S(2)}, u32[]{:S(2)}) collective-permute-start(bf16[96,352]{1,0:T(8,128)(2,1)} %get-tuple-element.51), channel_id=1, source_target_pairs={{0,20},{2,22},{4,16},{6,18},{8,28},{10,30},{12,24},{14,26},{16,4},... | collective-permute-start | bytes 202760 | tf_op jit(solution)/shard_map/ppermute | solution.py:99
  22.5 15.5 %collective-permute-start.10 = (bf16[96,352]{1,0:T(8,128)(2,1)}, bf16[96,352]{1,0:T(8,128)(2,1)S(1)}, u32[]{:S(2)}, u32[]{:S(2)}) collective-permute-start(bf16[96,352]{1,0:T(8,128)(2,1)} %get-tuple-element.52), channel_id=1, source_target_pairs={{0,22},{2,20},{4,18},{6,16},{8,30},{10,28},{12,26},{14,24},{16,6},... | collective-permute-start | bytes 202760 | tf_op jit(solution)/shard_map/ppermute | solution.py:99
  22.7 15.3 %collective-permute-start.11 = (bf16[96,352]{1,0:T(8,128)(2,1)}, bf16[96,352]{1,0:T(8,128)(2,1)S(1)}, u32[]{:S(2)}, u32[]{:S(2)}) collective-permute-start(bf16[96,352]{1,0:T(8,128)(2,1)} %get-tuple-element.53), channel_id=1, source_target_pairs={{0,24},{2,26},{4,28},{6,30},{8,16},{10,18},{12,20},{14,22},{16,8},... | collective-permute-start | bytes 202760 | tf_op jit(solution)/shard_map/ppermute | solution.py:99
  26.4 11.7 %collective-permute-start.12 = (bf16[96,352]{1,0:T(8,128)(2,1)S(1)}, bf16[96,352]{1,0:T(8,128)(2,1)S(1)}, u32[]{:S(2)}, u32[]{:S(2)}) collective-permute-start(bf16[96,352]{1,0:T(8,128)(2,1)S(1)} %copy-done.20), channel_id=1, source_target_pairs={{0,26},{2,24},{4,30},{6,28},{8,18},{10,16},{12,22},{14,20},{16,10}... | collective-permute-start | bytes 202760 | tf_op jit(solution)/shard_map/ppermute | solution.py:99
  32.8 8.0 %collective-permute-start.13 = (bf16[96,352]{1,0:T(8,128)(2,1)S(1)}, bf16[96,352]{1,0:T(8,128)(2,1)S(1)}, u32[]{:S(2)}, u32[]{:S(2)}) collective-permute-start(bf16[96,352]{1,0:T(8,128)(2,1)S(1)} %copy-done.19), channel_id=1, source_target_pairs={{0,28},{2,30},{4,24},{6,26},{8,20},{10,22},{12,16},{14,18},{16,12}... | collective-permute-start | bytes 202760 | tf_op jit(solution)/shard_map/ppermute | solution.py:99
  35.7 7.4 %collective-permute-start.14 = (bf16[96,352]{1,0:T(8,128)(2,1)S(1)}, bf16[96,352]{1,0:T(8,128)(2,1)S(1)}, u32[]{:S(2)}, u32[]{:S(2)}) collective-permute-start(bf16[96,352]{1,0:T(8,128)(2,1)S(1)} %copy-done.18), channel_id=1, source_target_pairs={{0,30},{2,28},{4,26},{6,24},{8,22},{10,20},{12,18},{14,16},{16,14}... | collective-permute-start | bytes 202760 | tf_op jit(solution)/shard_map/ppermute | solution.py:99
  44.1 14.5 %collective-permute-start.15 = (bf16[352,512]{1,0:T(8,128)(2,1)S(1)}, bf16[352,512]{1,0:T(8,128)(2,1)S(1)}, u32[]{:S(2)}, u32[]{:S(2)}) collective-permute-start(bf16[352,512]{1,0:T(8,128)(2,1)S(1)} %fusion.2.refs_0_), channel_id=1, source_target_pairs={{0,8},{2,10},{4,12},{6,14},{8,16},{10,18},{12,20},{14,22},{16,24},... | collective-permute-start | bytes 1081352 | tf_op jit(solution)/shard_map/ppermute | solution.py:495
  50.7 12.1 %collective-permute-start.18 = (bf16[352,512]{1,0:T(8,128)(2,1)S(1)}, bf16[352,512]{1,0:T(8,128)(2,1)S(1)}, u32[]{:S(2)}, u32[]{:S(2)}) collective-permute-start(bf16[352,512]{1,0:T(8,128)(2,1)S(1)} %fusion.2.refs_0_), channel_id=1, source_target_pairs={{8,0},{10,2},{12,4},{14,6},{16,8},{18,10},{20,12},{22,14},{24,16},... | collective-permute-start | bytes 1081352 | tf_op jit(solution)/shard_map/ppermute | solution.py:496
  62.8 11.5 %collective-permute-start.19 = (bf16[352,512]{1,0:T(8,128)(2,1)S(1)}, bf16[352,512]{1,0:T(8,128)(2,1)S(1)}, u32[]{:S(2)}, u32[]{:S(2)}) collective-permute-start(bf16[352,512]{1,0:T(8,128)(2,1)S(1)} %collective-permute-done.18), channel_id=1, source_target_pairs={{8,0},{10,2},{12,4},{14,6},{16,8},{18,10},{20,12},{22,14},{9,1},{1... | collective-permute-start | bytes 1081352 | tf_op jit(solution)/shard_map/ppermute | solution.py:496
  64.1 12.1 %collective-permute-start.31 = (bf16[352,512]{1,0:T(8,128)(2,1)S(1)}, bf16[352,512]{1,0:T(8,128)(2,1)S(1)}, u32[]{:S(2)}, u32[]{:S(2)}) collective-permute-start(bf16[352,512]{1,0:T(8,128)(2,1)S(1)} %fusion.2.refs_0_), channel_id=1, source_target_pairs={{0,4},{2,6},{4,0},{6,2},{8,12},{10,14},{12,8},{14,10},{16,20},{18,... | collective-permute-start | bytes 1081352 | tf_op jit(solution)/shard_map/ppermute | solution.py:99
  64.6 20.7 %collective-permute-start.30 = (bf16[352,512]{1,0:T(8,128)(2,1)S(1)}, bf16[352,512]{1,0:T(8,128)(2,1)S(1)}, u32[]{:S(2)}, u32[]{:S(2)}) collective-permute-start(bf16[352,512]{1,0:T(8,128)(2,1)S(1)} %fusion.2.refs_0_), channel_id=1, source_target_pairs={{0,2},{2,0},{4,6},{6,4},{8,10},{10,8},{12,14},{14,12},{16,18},{18,... | collective-permute-start | bytes 1081352 | tf_op jit(solution)/shard_map/ppermute | solution.py:99
  64.6 11.7 %collective-permute-start.17 = (bf16[352,512]{1,0:T(8,128)(2,1)S(1)}, bf16[352,512]{1,0:T(8,128)(2,1)S(1)}, u32[]{:S(2)}, u32[]{:S(2)}) collective-permute-start(bf16[352,512]{1,0:T(8,128)(2,1)S(1)} %collective-permute-done.16), channel_id=1, source_target_pairs={{16,24},{18,26},{20,28},{22,30},{17,25},{19,27},{21,29},{23,31}} | collective-permute-start | bytes 1081352 | tf_op jit(solution)/shard_map/ppermute | solution.py:495
  74.3 10.6 %collective-permute-start.20 = (bf16[352,512]{1,0:T(8,128)(2,1)S(1)}, bf16[352,512]{1,0:T(8,128)(2,1)S(1)}, u32[]{:S(2)}, u32[]{:S(2)}) collective-permute-start(bf16[352,512]{1,0:T(8,128)(2,1)S(1)} %collective-permute-done.19), channel_id=1, source_target_pairs={{8,0},{10,2},{12,4},{14,6},{9,1},{11,3},{13,5},{15,7}} | collective-permute-start | bytes 1081352 | tf_op jit(solution)/shard_map/ppermute | solution.py:496
  75.6 11.5 %collective-permute-start.28 = (bf16[352,512]{1,0:T(8,128)(2,1)S(1)}, bf16[352,512]{1,0:T(8,128)(2,1)}, u32[]{:S(2)}, u32[]{:S(2)}) collective-permute-start(bf16[352,512]{1,0:T(8,128)(2,1)S(1)} %broadcast_select_fusion.refs_0_), channel_id=1, source_target_pairs={{0,4},{2,6},{4,0},{6,2},{8,12},{10,14},{12,8},{14,10},{16,20},{18,... | collective-permute-start | bytes 1081352 | tf_op jit(solution)/shard_map/ppermute | solution.py:99
  76.2 20.1 %collective-permute-start.27 = (bf16[352,512]{1,0:T(8,128)(2,1)S(1)}, bf16[352,512]{1,0:T(8,128)(2,1)S(1)}, u32[]{:S(2)}, u32[]{:S(2)}) collective-permute-start(bf16[352,512]{1,0:T(8,128)(2,1)S(1)} %broadcast_select_fusion.refs_0_), channel_id=1, source_target_pairs={{0,2},{2,0},{4,6},{6,4},{8,10},{10,8},{12,14},{14,12},{16,18},{18,... | collective-permute-start | bytes 1081352 | tf_op jit(solution)/shard_map/ppermute | solution.py:99
  76.3 10.8 %collective-permute-start.32 = (bf16[352,512]{1,0:T(8,128)(2,1)S(1)}, bf16[352,512]{1,0:T(8,128)(2,1)S(1)}, u32[]{:S(2)}, u32[]{:S(2)}) collective-permute-start(bf16[352,512]{1,0:T(8,128)(2,1)S(1)} %collective-permute-done.31.refs_2_), channel_id=1, source_target_pairs={{0,2},{2,0},{4,6},{6,4},{8,10},{10,8},{12,14},{14,12},{16,18},{18,... | collective-permute-start | bytes 1081352 | tf_op jit(solution)/shard_map/ppermute | solution.py:99
  84.9 11.4 %collective-permute-start.25 = (bf16[352,512]{1,0:T(8,128)(2,1)S(1)}, bf16[352,512]{1,0:T(8,128)(2,1)}, u32[]{:S(2)}, u32[]{:S(2)}) collective-permute-start(bf16[352,512]{1,0:T(8,128)(2,1)S(1)} %select_select_fusion.refs_0_), channel_id=1, source_target_pairs={{0,4},{2,6},{4,0},{6,2},{8,12},{10,14},{12,8},{14,10},{16,20},{18,... | collective-permute-start | bytes 1081352 | tf_op jit(solution)/shard_map/ppermute | solution.py:99
  85.4 15.2 %collective-permute-start.22 = (bf16[352,512]{1,0:T(8,128)(2,1)S(1)}, bf16[352,512]{1,0:T(8,128)(2,1)S(1)}, u32[]{:S(2)}, u32[]{:S(2)}) collective-permute-start(bf16[352,512]{1,0:T(8,128)(2,1)S(1)} %select_select_fusion.1.refs_0_), channel_id=1, source_target_pairs={{0,4},{2,6},{4,0},{6,2},{8,12},{10,14},{12,8},{14,10},{16,20},{18,... | collective-permute-start | bytes 1081352 | tf_op jit(solution)/shard_map/ppermute | solution.py:99
  87.1 18.8 %collective-permute-start.29 = (bf16[352,512]{1,0:T(8,128)(2,1)}, bf16[352,512]{1,0:T(8,128)(2,1)}, u32[]{:S(2)}, u32[]{:S(2)}) collective-permute-start(bf16[352,512]{1,0:T(8,128)(2,1)} %collective-permute-done.28.refs_2_), channel_id=1, source_target_pairs={{0,2},{2,0},{4,6},{6,4},{8,10},{10,8},{12,14},{14,12},{16,18},{18,... | collective-permute-start | bytes 1081352 | tf_op jit(solution)/shard_map/ppermute | solution.py:99
  87.1 25.7 %collective-permute-start.24 = (bf16[352,512]{1,0:T(8,128)(2,1)S(1)}, bf16[352,512]{1,0:T(8,128)(2,1)S(1)}, u32[]{:S(2)}, u32[]{:S(2)}) collective-permute-start(bf16[352,512]{1,0:T(8,128)(2,1)S(1)} %select_select_fusion.refs_0_), channel_id=1, source_target_pairs={{0,2},{2,0},{4,6},{6,4},{8,10},{10,8},{12,14},{14,12},{16,18},{18,... | collective-permute-start | bytes 1081352 | tf_op jit(solution)/shard_map/ppermute | solution.py:99
  96.3 16.5 %collective-permute-start.26 = (bf16[352,512]{1,0:T(8,128)(2,1)}, bf16[352,512]{1,0:T(8,128)(2,1)}, u32[]{:S(2)}, u32[]{:S(2)}) collective-permute-start(bf16[352,512]{1,0:T(8,128)(2,1)} %collective-permute-done.25.refs_2_), channel_id=1, source_target_pairs={{0,2},{2,0},{4,6},{6,4},{8,10},{10,8},{12,14},{14,12},{16,18},{18,... | collective-permute-start | bytes 1081352 | tf_op jit(solution)/shard_map/ppermute | solution.py:99
  96.3 24.0 %collective-permute-start.21 = (bf16[352,512]{1,0:T(8,128)(2,1)S(1)}, bf16[352,512]{1,0:T(8,128)(2,1)S(1)}, u32[]{:S(2)}, u32[]{:S(2)}) collective-permute-start(bf16[352,512]{1,0:T(8,128)(2,1)S(1)} %select_select_fusion.1.refs_0_), channel_id=1, source_target_pairs={{0,2},{2,0},{4,6},{6,4},{8,10},{10,8},{12,14},{14,12},{16,18},{18,... | collective-permute-start | bytes 1081352 | tf_op jit(solution)/shard_map/ppermute | solution.py:99
  100.6 21.2 %collective-permute-start.23 = (bf16[352,512]{1,0:T(8,128)(2,1)S(1)}, bf16[352,512]{1,0:T(8,128)(2,1)S(1)}, u32[]{:S(2)}, u32[]{:S(2)}) collective-permute-start(bf16[352,512]{1,0:T(8,128)(2,1)S(1)} %collective-permute-done.22.refs_2_.refs_0_), channel_id=1, source_target_pairs={{0,2},{2,0},{4,6},{6,4},{8,10},{10,8},{12,14},{14,12},{16,18},{18,... | collective-permute-start | bytes 1081352 | tf_op jit(solution)/shard_map/ppermute | solution.py:99
  122.2 7.3 %collective-permute-start.33 = (f32[3,128,128]{2,1,0:T(8,128)S(1)}, f32[3,128,128]{2,1,0:T(8,128)S(1)}, u32[]{:S(2)}, u32[]{:S(2)}) collective-permute-start(f32[3,128,128]{2,1,0:T(8,128)S(1)} %lower.3), channel_id=1, source_target_pairs={{0,1},{1,0},{2,3},{3,2},{4,5},{5,4},{6,7},{7,6},{8,9},{9,8},{10,11... | collective-permute-start | bytes 589832 | tf_op jit(solution)/shard_map/ppermute | solution.py:99
  142.7 15.0 %collective-permute-start.36 = (f32[512,256]{1,0:T(8,128)}, f32[512,256]{1,0:T(8,128)S(1)}, u32[]{:S(2)}, u32[]{:S(2)}) collective-permute-start(f32[512,256]{1,0:T(8,128)} %get-tuple-element.76), channel_id=1, source_target_pairs={{0,1},{1,0},{2,3},{3,2},{4,5},{5,4},{6,7},{7,6},{8,9},{9,8},{10,11... | collective-permute-start | bytes 1572872 | tf_op jit(solution)/shard_map/ppermute | solution.py:99
  149.9 18.6 %collective-permute-start.35 = (f32[512,256]{1,0:T(8,128)}, f32[512,256]{1,0:T(8,128)S(1)}, u32[]{:S(2)}, u32[]{:S(2)}) collective-permute-start(f32[512,256]{1,0:T(8,128)} %get-tuple-element.74), channel_id=1, source_target_pairs={{0,1},{1,0},{2,3},{3,2},{4,5},{5,4},{6,7},{7,6},{8,9},{9,8},{10,11... | collective-permute-start | bytes 1572872 | tf_op jit(solution)/shard_map/ppermute | solution.py:99
  (26 other events, 363.0 us)

commit v2 on v1

--- a/solution.py
+++ b/solution.py
@@ -109,6 +109,10 @@
     return [pltpu.with_memory_space_constraint(value, pltpu.VMEM) for value in values]
 
 
+def away(values):
+    return [pltpu.with_memory_space_constraint(value, pltpu.HBM) for value in values]
+
+
 def seat():
     me = lax.axis_index("wide")
     return lax.div(me, GROUP), lax.rem(me, GROUP)
@@ -192,11 +196,12 @@
         out_specs=vmem,
         out_shape=jax.ShapeDtypeStruct(old.shape, jnp.float32),
         input_output_aliases={0: 0},
+        compiler_params=pltpu.CompilerParams(vmem_limit_bytes=8 << 20),
         name="lower",
     )(*near([old, *pieces]))
 
 
-def accumulate_kernel(table, blocks, fresh, final, coeffs_ref, earlier_ref, *refs):
+def accumulate_kernel(table, blocks, fresh, final, tick_ref, coeffs_ref, earlier_ref, *refs):
     pieces, refs = list(refs[:GROUP]), list(refs[GROUP:])
     old_sum_ref = None if fresh else refs.pop(0)
     old_lower_ref = None if fresh or final else refs.pop(0)
@@ -236,7 +241,7 @@
         sum_ref[rows_at, :] = total if fresh else old_sum_ref[rows_at, :] + total
 
 
-def accumulate(table, blocks, coeffs, earlier, pieces, state, final):
+def accumulate(table, blocks, ticked, coeffs, earlier, pieces, state, final):
     rows = coeffs.shape[0]
     width, panel = pieces[0].shape
     fresh = state is None
@@ -249,7 +254,9 @@
     vmem = pl.BlockSpec(memory_space=pltpu.VMEM)
     return pl.pallas_call(
         functools.partial(accumulate_kernel, table, blocks, fresh, final),
-        in_specs=[anywhere] * (2 + GROUP) + [vmem] * len(state),
+        in_specs=[pl.BlockSpec(memory_space=pltpu.SMEM)]
+        + [anywhere] * 2
+        + [vmem] * (GROUP + len(state)),
         out_specs=[vmem] * len(shapes),
         scratch_shapes=[
             pltpu.VMEM((width * GROUP, panel), jnp.bfloat16),
@@ -257,14 +264,15 @@
             pltpu.SemaphoreType.DMA((GROUP + 2 * TILES,)),
         ],
         out_shape=[jax.ShapeDtypeStruct(shape, jnp.float32) for shape in shapes],
-        input_output_aliases={2 + GROUP + i: i for i in range(len(state))},
+        input_output_aliases={3 + GROUP + i: i for i in range(len(state))},
         cost_estimate=pl.CostEstimate(
             flops=2 * rows * panel * width * GROUP,
             bytes_accessed=2 * rows * width * GROUP,
             transcendentals=0,
         ),
+        compiler_params=pltpu.CompilerParams(vmem_limit_bytes=16 << 20),
         name="accumulate",
-    )(coeffs, earlier, *pieces, *state)
+    )(ticked, *away([coeffs, earlier]), *near([*pieces, *state]))
 
 
 def my_rows(capacity, owner_ref, local_ref):
@@ -329,8 +337,23 @@
             pltpu.VMEM((len(hops), coeffs.shape[0], total // lines), jnp.bfloat16),
             pltpu.SemaphoreType.DMA((len(hops), 2)),
         ],
+        compiler_params=pltpu.CompilerParams(vmem_limit_bytes=24 << 20),
         name="cut",
-    )(piv_owner.reshape(1, -1), piv_local[None, :], coeffs, earlier)
+    )(piv_owner.reshape(1, -1), piv_local[None, :], *away([coeffs, earlier]))
+
+
+def tick_kernel(local_ref, out_ref):
+    out_ref[0, 0] = local_ref[0, 0]
+
+
+def tick(local):
+    smem = pl.BlockSpec(memory_space=pltpu.SMEM)
+    return pl.pallas_call(
+        tick_kernel,
+        in_specs=[smem],
+        out_specs=smem,
+        out_shape=jax.ShapeDtypeStruct((1, 1), jnp.int32),
+    )(local)
 
 
 def choose(line, table, received):
@@ -420,8 +443,9 @@
         in_specs=[pl.BlockSpec((rows, panel), lambda i: (index, 0)), vmem, vmem, vmem],
         out_specs=[vmem, vmem],
         out_shape=[half, half],
+        compiler_params=pltpu.CompilerParams(vmem_limit_bytes=20 << 20),
         name="recur",
-    )(partial, mine, other, inv_tiles)
+    )(*near([partial, mine, other]), inv_tiles)
 
 
 def finish_kernel(keep_ref, taken_ref, *refs):
@@ -440,6 +464,7 @@
         out_specs=pl.BlockSpec((rows, columns), lambda i: (index, 0)),
         out_shape=jax.ShapeDtypeStruct((rows * SENDS, columns), jnp.float32),
         input_output_aliases={2: 0} if old else {},
+        compiler_params=pltpu.CompilerParams(vmem_limit_bytes=8 << 20),
         name="finish",
     )(*near([keep, taken]), *old)
 
@@ -505,13 +530,15 @@
         beside = exchange(piece, "wide", 1, size)
         corner = exchange(across, "wide", 1, size)
         groups.append([piece, beside, across, corner])
+    ticks = {hop: tick(piv_local[:1, None]) for hop in range(1, lines - 1)}
     state = None
     for index, (source, group) in enumerate(zip(sources, groups)):
         final = index == lines - 1
         if final:
             mine = lower_only(blocks, edge, (0, 1), state[1], group[:2])
             mine = lower_only(blocks, edge, (2, 3), mine, group[2:])
-        state = accumulate(source, blocks, coeffs, earlier, group, state, final)
+        ticked = ticks[min(max(index, 1), lines - 2)]
+        state = accumulate(source, blocks, ticked, coeffs, earlier, group, state, final)
     mine = mine + exchange(mine, "narrow", 1, 2)
     other = exchange(mine, "wide", 1, size)
     result = None

time: 170 us -> 158 us (0.929)
  Pallas kernels: 46.2 us -> 36.1 us
    pallas_call x4, Pallas kernels: 25.5 us -> 20.6 us  [accumulate(): pl.pallas_call(functools.partial(accumulate_kernel, table, blocks, fresh,...]
    pallas_call x2, Pallas kernels: 11.3 us -> 6.47 us  [recur(): pl.pallas_call(functools.partial(recur_kernel, blocks), grid=(1,), in_spe...]
    unnamed x57 -> x23, local copies, waits for them, and re-layouts: 3.65 us -> 1.61 us
  transfers between devices with their start and end apart: 37 -> 37, of which waited for: 11 -> 13; matrix products, arithmetic and copies ran while one was open for 1% -> 2% of each run, Pallas kernels for 19% -> 17%
where the time goes in v2:
time: 158 us
  waiting for transfers between devices  66.5 us (42%)
  starting transfers between devices  49.4 us (31%)
  Pallas kernels  36.1 us (23%)
  local copies, waits for them, and re-layouts  2.82 us (2%)
    ppermute x31, waiting for transfers between devices, exchange(): return lax.ppermute(value, axis, [(i, i ^ bit) for i in range(size)])  40.9 us
    ppermute x31, starting transfers between devices, exchange(): return lax.ppermute(value, axis, [(i, i ^ bit) for i in range(size)])  37.3 us
    pallas_call x4, Pallas kernels, accumulate(): pl.pallas_call(functools.partial(accumulate_kernel, table, blocks, fresh,...  20.6 us
    ppermute x3, waiting for transfers between devices, lined_panel(): up = lax.ppermute(up, 'wide', falling)  19.1 us
    ppermute x3, starting transfers between devices, lined_panel(): down = lax.ppermute(down, 'wide', rising)  8.29 us
    ppermute x3, waiting for transfers between devices, lined_panel(): down = lax.ppermute(down, 'wide', rising)  6.62 us
    pallas_call x2, Pallas kernels, recur(): pl.pallas_call(functools.partial(recur_kernel, blocks), grid=(1,), in_spe...  6.47 us
    pallas_call x1, Pallas kernels, cut(): pl.pallas_call(functools.partial(cut_kernel, hops, lines), in_specs=[vmem...  5.35 us
  transfers between devices with their start and end apart: 37, of which 13 were waited for; matrix products, arithmetic and copies ran while one was open for 2% of the time, Pallas kernels for 17%

profile of v2, /device:TPU:0, one launch (start us, length us, event | category | flops | bytes accessed | tf_op | source)
XLA Modules:
  0.0 157.7 jit_solution(3154933639080405268)
XLA Ops:
  1.4 5.3 %cut.1 = (bf16[96,352]{1,0:T(8,128)(2,1)S(1)}, bf16[96,352]{1,0:T(8,128)(2,1)S(1)}, bf16[96,352]{1,0:T(8,128)(2,1)S(1)}, bf16[96,352]{1,0:T(8,128)(2,1)S(1)}, bf...) custom-call(s32[1,512]{1,0:T(1,128)S(1)} %bitcast.7, ...), custom_call_target="tpu_custom_call" | custom-call | tf_op jit(solution)/shard_map/cut/pallas_call | solution.py:331
  7.3 2.6 %collective-permute-start.1 = (bf16[96,352]{1,0:T(8,128)(2,1)S(1)}, bf16[96,352]{1,0:T(8,128)(2,1)S(1)}, u32[]{:S(2)}, u32[]{:S(2)}) collective-permute-start(bf16[96,352]{1,0:T(8,128)(2,1)S(1)} %get-tuple-element.43), channel_id=1, source_target_pairs={{0,4},{2,6},{4,0},{6,2},{8,12},{10,14},{12,8},{14,10},{16,20},{18,... | collective-permute-start | bytes 202760 | tf_op jit(solution)/shard_map/ppermute | solution.py:99
  9.9 1.8 %collective-permute-start.3 = (bf16[96,352]{1,0:T(8,128)(2,1)S(1)}, bf16[96,352]{1,0:T(8,128)(2,1)S(1)}, u32[]{:S(2)}, u32[]{:S(2)}) collective-permute-start(bf16[96,352]{1,0:T(8,128)(2,1)S(1)} %get-tuple-element.45), channel_id=1, source_target_pairs={{0,8},{2,10},{4,12},{6,14},{8,0},{10,2},{12,4},{14,6},{16,24},{18,... | collective-permute-start | bytes 202760 | tf_op jit(solution)/shard_map/ppermute | solution.py:99
  12.0 2.7 %collective-permute-start.5 = (bf16[96,352]{1,0:T(8,128)(2,1)S(1)}, bf16[96,352]{1,0:T(8,128)(2,1)S(1)}, u32[]{:S(2)}, u32[]{:S(2)}) collective-permute-start(bf16[96,352]{1,0:T(8,128)(2,1)S(1)} %get-tuple-element.47), channel_id=1, source_target_pairs={{0,12},{2,14},{4,8},{6,10},{8,4},{10,6},{12,0},{14,2},{16,28},{18,... | collective-permute-start | bytes 202760 | tf_op jit(solution)/shard_map/ppermute | solution.py:99
  14.9 2.8 %collective-permute-start.7 = (bf16[96,352]{1,0:T(8,128)(2,1)S(1)}, bf16[96,352]{1,0:T(8,128)(2,1)S(1)}, u32[]{:S(2)}, u32[]{:S(2)}) collective-permute-start(bf16[96,352]{1,0:T(8,128)(2,1)S(1)} %get-tuple-element.49), channel_id=1, source_target_pairs={{0,16},{2,18},{4,20},{6,22},{8,24},{10,26},{12,28},{14,30},{16,0},... | collective-permute-start | bytes 202760 | tf_op jit(solution)/shard_map/ppermute | solution.py:99
  18.6 2.8 %collective-permute-start.9 = (bf16[96,352]{1,0:T(8,128)(2,1)S(1)}, bf16[96,352]{1,0:T(8,128)(2,1)S(1)}, u32[]{:S(2)}, u32[]{:S(2)}) collective-permute-start(bf16[96,352]{1,0:T(8,128)(2,1)S(1)} %get-tuple-element.51), channel_id=1, source_target_pairs={{0,20},{2,22},{4,16},{6,18},{8,28},{10,30},{12,24},{14,26},{16,4},... | collective-permute-start | bytes 202760 | tf_op jit(solution)/shard_map/ppermute | solution.py:99
  22.0 3.2 %collective-permute-start.11 = (bf16[96,352]{1,0:T(8,128)(2,1)S(1)}, bf16[96,352]{1,0:T(8,128)(2,1)S(1)}, u32[]{:S(2)}, u32[]{:S(2)}) collective-permute-start(bf16[96,352]{1,0:T(8,128)(2,1)S(1)} %get-tuple-element.53), channel_id=1, source_target_pairs={{0,24},{2,26},{4,28},{6,30},{8,16},{10,18},{12,20},{14,22},{16,8},... | collective-permute-start | bytes 202760 | tf_op jit(solution)/shard_map/ppermute | solution.py:99
  25.2 4.3 %collective-permute-start.12 = (bf16[96,352]{1,0:T(8,128)(2,1)S(1)}, bf16[96,352]{1,0:T(8,128)(2,1)S(1)}, u32[]{:S(2)}, u32[]{:S(2)}) collective-permute-start(bf16[96,352]{1,0:T(8,128)(2,1)S(1)} %get-tuple-element.54), channel_id=1, source_target_pairs={{0,26},{2,24},{4,30},{6,28},{8,18},{10,16},{12,22},{14,20},{16,10}... | collective-permute-start | bytes 202760 | tf_op jit(solution)/shard_map/ppermute | solution.py:99
  29.6 1.2 collective-permute-done.8
  30.8 3.4 %collective-permute-start.13 = (bf16[96,352]{1,0:T(8,128)(2,1)S(1)}, bf16[96,352]{1,0:T(8,128)(2,1)S(1)}, u32[]{:S(2)}, u32[]{:S(2)}) collective-permute-start(bf16[96,352]{1,0:T(8,128)(2,1)S(1)} %get-tuple-element.55), channel_id=1, source_target_pairs={{0,28},{2,30},{4,24},{6,26},{8,20},{10,22},{12,16},{14,18},{16,12}... | collective-permute-start | bytes 202760 | tf_op jit(solution)/shard_map/ppermute | solution.py:99
  34.4 2.6 %collective-permute-start.14 = (bf16[96,352]{1,0:T(8,128)(2,1)S(1)}, bf16[96,352]{1,0:T(8,128)(2,1)S(1)}, u32[]{:S(2)}, u32[]{:S(2)}) collective-permute-start(bf16[96,352]{1,0:T(8,128)(2,1)S(1)} %get-tuple-element.56), channel_id=1, source_target_pairs={{0,30},{2,28},{4,26},{6,24},{8,22},{10,20},{12,18},{14,16},{16,14}... | collective-permute-start | bytes 202760 | tf_op jit(solution)/shard_map/ppermute | solution.py:99
  37.9 3.6 %collective-permute-done.14 = bf16[96,352]{1,0:T(8,128)(2,1)S(1)} collective-permute-done((bf16[96,352]{1,0:T(8,128)(2,1)S(1)}, bf16[96,352]{1,0:T(8,128)(2,1)S(1)}, u32[]{:S(2)}, u32[]{:S(2)}) %collective-permute-start.14) | collective-permute-done | bytes 67616 | tf_op jit(solution)/shard_map/ppermute | solution.py:99
  42.5 6.9 %collective-permute-start.15 = (bf16[352,512]{1,0:T(8,128)(2,1)S(1)}, bf16[352,512]{1,0:T(8,128)(2,1)S(1)}, u32[]{:S(2)}, u32[]{:S(2)}) collective-permute-start(bf16[352,512]{1,0:T(8,128)(2,1)S(1)} %fusion.2.refs_0_), channel_id=1, source_target_pairs={{0,8},{2,10},{4,12},{6,14},{8,16},{10,18},{12,20},{14,22},{16,24},... | collective-permute-start | bytes 1081352 | tf_op jit(solution)/shard_map/ppermute | solution.py:520
  49.4 1.3 collective-permute-start.18
  50.7 6.6 %collective-permute-done.15 = bf16[352,512]{1,0:T(8,128)(2,1)S(1)} collective-permute-done((bf16[352,512]{1,0:T(8,128)(2,1)S(1)}, bf16[352,512]{1,0:T(8,128)(2,1)S(1)}, u32[]{:S(2)}, u32[]{:S(2)}) %collective-permute-start.15) | collective-permute-done | bytes 360480 | tf_op jit(solution)/shard_map/ppermute | solution.py:520
  58.0 3.5 %collective-permute-done.18 = bf16[352,512]{1,0:T(8,128)(2,1)S(1)} collective-permute-done((bf16[352,512]{1,0:T(8,128)(2,1)S(1)}, bf16[352,512]{1,0:T(8,128)(2,1)S(1)}, u32[]{:S(2)}, u32[]{:S(2)}) %collective-permute-start.18) | collective-permute-done | bytes 360480 | tf_op jit(solution)/shard_map/ppermute | solution.py:521
  61.5 1.3 collective-permute-start.19
  64.1 8.8 %collective-permute-done.19 = bf16[352,512]{1,0:T(8,128)(2,1)} collective-permute-done((bf16[352,512]{1,0:T(8,128)(2,1)S(1)}, bf16[352,512]{1,0:T(8,128)(2,1)}, u32[]{:S(2)}, u32[]{:S(2)}) %collective-permute-start.19) | collective-permute-done | bytes 360480 | tf_op jit(solution)/shard_map/ppermute | solution.py:521
  72.9 1.3 collective-permute-start.20
  76.8 6.8 %collective-permute-done.20 = bf16[352,512]{1,0:T(8,128)(2,1)S(1)} collective-permute-done((bf16[352,512]{1,0:T(8,128)(2,1)}, bf16[352,512]{1,0:T(8,128)(2,1)S(1)}, u32[]{:S(2)}, u32[]{:S(2)}) %collective-permute-start.20) | collective-permute-done | bytes 360480 | tf_op jit(solution)/shard_map/ppermute | solution.py:521
  86.2 8.7 %collective-permute-done.25.refs_2_ = bf16[352,512]{1,0:T(8,128)(2,1)} collective-permute-done((bf16[352,512]{1,0:T(8,128)(2,1)S(1)}, bf16[352,512]{1,0:T(8,128)(2,1)}, u32[]{:S(2)}, u32[]{:S(2)}) %collective-permute-start.25) | collective-permute-done | bytes 360480 | tf_op jit(solution)/shard_map/ppermute | solution.py:99
  99.0 4.6 %accumulate.4 = (f32[1024,512]{1,0:T(8,128)S(1)}, f32[3,128,128]{2,1,0:T(8,128)S(1)}) custom-call(s32[1,1]{1,0:T(1,128)} %shard_map.55.tick_ref, bf16[1024,4608]{1,0:T(8,128)(2,1)} %coeffs_ref.9, bf16[1024,1024]{1,0:T(8,128)(2,1)} %earlier_ref.9, bf16[352,512]{1,0:T(8,128)(2,1)S(1)} %fusion.2.refs_0_, bf16[352,512]{1,0:T(8,128)(2,1)S(1)} %collective-permute-done.30.refs_1_, ...), custom_call_target="tpu_custom_call" | custom-call | flops 1476395008 | bytes 2883584 | tf_op jit(solution)/shard_map/accumulate/pallas_call | solution.py:255
  103.6 5.7 %accumulate.5 = (f32[1024,512]{1,0:T(8,128)S(1)}, f32[3,128,128]{2,1,0:T(8,128)S(1)}) custom-call(s32[1,1]{1,0:T(1,128)} %shard_map.55.tick_ref, bf16[1024,4608]{1,0:T(8,128)(2,1)} %coeffs_ref.9, bf16[1024,1024]{1,0:T(8,128)(2,1)} %earlier_ref.9, bf16[352,512]{1,0:T(8,128)(2,1)S(1)} %broadcast_select_fusion.refs_0_, ...), custom_call_target="tpu_custom_call", output_to_operand_aliasing={{0}: (7, {}), {1}: (8, {})} | custom-call | flops 1476395008 | bytes 2883584 | tf_op jit(solution)/shard_map/accumulate/pallas_call | solution.py:255
  109.3 5.8 %accumulate.6 = (f32[1024,512]{1,0:T(8,128)S(1)}, f32[3,128,128]{2,1,0:T(8,128)S(1)}) custom-call(s32[1,1]{1,0:T(1,128)} %shard_map.55.tick_ref, bf16[1024,4608]{1,0:T(8,128)(2,1)} %coeffs_ref.9, bf16[1024,1024]{1,0:T(8,128)(2,1)} %earlier_ref.9, bf16[352,512]{1,0:T(8,128)(2,1)S(1)} %select_select_fusion.refs_0_, ...), custom_call_target="tpu_custom_call", output_to_operand_aliasing={{0}: (7, {}), {1}: (8, {})} | custom-call | flops 1476395008 | bytes 2883584 | tf_op jit(solution)/shard_map/accumulate/pallas_call | solution.py:255
  115.9 1.6 collective-permute-start.33
  117.5 5.8 %collective-permute-done.33 = f32[3,128,128]{2,1,0:T(8,128)S(1)} collective-permute-done((f32[3,128,128]{2,1,0:T(8,128)S(1)}, f32[3,128,128]{2,1,0:T(8,128)S(1)}, u32[]{:S(2)}, u32[]{:S(2)}) %collective-permute-start.33) | collective-permute-done | bytes 196640 | tf_op jit(solution)/shard_map/ppermute | solution.py:99
  123.4 4.6 %accumulate.7.partial_ref = f32[1024,512]{1,0:T(8,128)S(1)} custom-call(s32[1,1]{1,0:T(1,128)} %shard_map.55.tick_ref, bf16[1024,4608]{1,0:T(8,128)(2,1)} %coeffs_ref.9, bf16[1024,1024]{1,0:T(8,128)(2,1)} %earlier_ref.9, bf16[352,512]{1,0:T(8,128)(2,1)S(1)} %select_select_fusion.1.refs_0_, ...), custom_call_target="tpu_custom_call", output_to_operand_aliasing={{}: (7, {})} | custom-call | flops 1476395008 | bytes 2883584 | tf_op jit(solution)/shard_map/accumulate/pallas_call | solution.py:255
  128.0 3.2 %recur.3 = (f32[512,256]{1,0:T(8,128)S(1)}, f32[512,256]{1,0:T(8,128)S(1)}) custom-call(f32[1024,512]{1,0:T(8,128)S(1)} %accumulate.7.partial_ref, f32[3,128,128]{2,1,0:T(8,128)S(1)} %add.9.mine_ref, f32[3,128,128]{2,1,0:T(8,128)S(1)} %collective-permute-done.34.other_ref, f32[4,128,128]{2,1,0:T(8,128)S(1)} %copy-done), custom_call_target="tpu_custom_call" | custom-call | tf_op jit(solution)/shard_map/recur/pallas_call | solution.py:440
  131.3 1.6 collective-permute-start.36
  132.8 3.2 %recur.2 = (f32[512,256]{1,0:T(8,128)S(1)}, f32[512,256]{1,0:T(8,128)S(1)}) custom-call(f32[1024,512]{1,0:T(8,128)S(1)} %accumulate.7.partial_ref, f32[3,128,128]{2,1,0:T(8,128)S(1)} %add.9.mine_ref, f32[3,128,128]{2,1,0:T(8,128)S(1)} %collective-permute-done.34.other_ref, f32[4,128,128]{2,1,0:T(8,128)S(1)} %copy-done), custom_call_target="tpu_custom_call" | custom-call | tf_op jit(solution)/shard_map/recur/pallas_call | solution.py:440
  136.7 9.5 %collective-permute-done.36.taken_ref = f32[512,256]{1,0:T(8,128)S(1)} collective-permute-done((f32[512,256]{1,0:T(8,128)S(1)}, f32[512,256]{1,0:T(8,128)S(1)}, u32[]{:S(2)}, u32[]{:S(2)}) %collective-permute-start.36) | collective-permute-done | bytes 524320 | tf_op jit(solution)/shard_map/ppermute | solution.py:99
  147.0 9.9 %collective-permute-done.35.taken_ref = f32[512,256]{1,0:T(8,128)S(1)} collective-permute-done((f32[512,256]{1,0:T(8,128)S(1)}, f32[512,256]{1,0:T(8,128)S(1)}, u32[]{:S(2)}, u32[]{:S(2)}) %collective-permute-start.35) | collective-permute-done | bytes 524320 | tf_op jit(solution)/shard_map/ppermute | solution.py:99
  (86 shorter events, 20.5 us)
Async XLA Ops:
  7.3 7.5 %collective-permute-start.1 = (bf16[96,352]{1,0:T(8,128)(2,1)S(1)}, bf16[96,352]{1,0:T(8,128)(2,1)S(1)}, u32[]{:S(2)}, u32[]{:S(2)}) collective-permute-start(bf16[96,352]{1,0:T(8,128)(2,1)S(1)} %get-tuple-element.43), channel_id=1, source_target_pairs={{0,4},{2,6},{4,0},{6,2},{8,12},{10,14},{12,8},{14,10},{16,20},{18,... | collective-permute-start | bytes 202760 | tf_op jit(solution)/shard_map/ppermute | solution.py:99
  9.9 7.8 %collective-permute-start.3 = (bf16[96,352]{1,0:T(8,128)(2,1)S(1)}, bf16[96,352]{1,0:T(8,128)(2,1)S(1)}, u32[]{:S(2)}, u32[]{:S(2)}) collective-permute-start(bf16[96,352]{1,0:T(8,128)(2,1)S(1)} %get-tuple-element.45), channel_id=1, source_target_pairs={{0,8},{2,10},{4,12},{6,14},{8,0},{10,2},{12,4},{14,6},{16,24},{18,... | collective-permute-start | bytes 202760 | tf_op jit(solution)/shard_map/ppermute | solution.py:99
  12.0 9.4 %collective-permute-start.5 = (bf16[96,352]{1,0:T(8,128)(2,1)S(1)}, bf16[96,352]{1,0:T(8,128)(2,1)S(1)}, u32[]{:S(2)}, u32[]{:S(2)}) collective-permute-start(bf16[96,352]{1,0:T(8,128)(2,1)S(1)} %get-tuple-element.47), channel_id=1, source_target_pairs={{0,12},{2,14},{4,8},{6,10},{8,4},{10,6},{12,0},{14,2},{16,28},{18,... | collective-permute-start | bytes 202760 | tf_op jit(solution)/shard_map/ppermute | solution.py:99
  14.8 7.2 %collective-permute-start.6 = (bf16[96,352]{1,0:T(8,128)(2,1)S(1)}, bf16[96,352]{1,0:T(8,128)(2,1)S(1)}, u32[]{:S(2)}, u32[]{:S(2)}) collective-permute-start(bf16[96,352]{1,0:T(8,128)(2,1)S(1)} %get-tuple-element.48), channel_id=1, source_target_pairs={{0,14},{2,12},{4,10},{6,8},{8,6},{10,4},{12,2},{14,0},{16,30},{18,... | collective-permute-start | bytes 202760 | tf_op jit(solution)/shard_map/ppermute | solution.py:99
  14.9 10.3 %collective-permute-start.7 = (bf16[96,352]{1,0:T(8,128)(2,1)S(1)}, bf16[96,352]{1,0:T(8,128)(2,1)S(1)}, u32[]{:S(2)}, u32[]{:S(2)}) collective-permute-start(bf16[96,352]{1,0:T(8,128)(2,1)S(1)} %get-tuple-element.49), channel_id=1, source_target_pairs={{0,16},{2,18},{4,20},{6,22},{8,24},{10,26},{12,28},{14,30},{16,0},... | collective-permute-start | bytes 202760 | tf_op jit(solution)/shard_map/ppermute | solution.py:99
  17.7 13.1 %collective-permute-start.8 = (bf16[96,352]{1,0:T(8,128)(2,1)S(1)}, bf16[96,352]{1,0:T(8,128)(2,1)S(1)}, u32[]{:S(2)}, u32[]{:S(2)}) collective-permute-start(bf16[96,352]{1,0:T(8,128)(2,1)S(1)} %get-tuple-element.50), channel_id=1, source_target_pairs={{0,18},{2,16},{4,22},{6,20},{8,26},{10,24},{12,30},{14,28},{16,2},... | collective-permute-start | bytes 202760 | tf_op jit(solution)/shard_map/ppermute | solution.py:99
  18.6 15.8 %collective-permute-start.9 = (bf16[96,352]{1,0:T(8,128)(2,1)S(1)}, bf16[96,352]{1,0:T(8,128)(2,1)S(1)}, u32[]{:S(2)}, u32[]{:S(2)}) collective-permute-start(bf16[96,352]{1,0:T(8,128)(2,1)S(1)} %get-tuple-element.51), channel_id=1, source_target_pairs={{0,20},{2,22},{4,16},{6,18},{8,28},{10,30},{12,24},{14,26},{16,4},... | collective-permute-start | bytes 202760 | tf_op jit(solution)/shard_map/ppermute | solution.py:99
  21.4 15.5 %collective-permute-start.10 = (bf16[96,352]{1,0:T(8,128)(2,1)S(1)}, bf16[96,352]{1,0:T(8,128)(2,1)S(1)}, u32[]{:S(2)}, u32[]{:S(2)}) collective-permute-start(bf16[96,352]{1,0:T(8,128)(2,1)S(1)} %get-tuple-element.52), channel_id=1, source_target_pairs={{0,22},{2,20},{4,18},{6,16},{8,30},{10,28},{12,26},{14,24},{16,6},... | collective-permute-start | bytes 202760 | tf_op jit(solution)/shard_map/ppermute | solution.py:99
  22.0 15.0 %collective-permute-start.11 = (bf16[96,352]{1,0:T(8,128)(2,1)S(1)}, bf16[96,352]{1,0:T(8,128)(2,1)S(1)}, u32[]{:S(2)}, u32[]{:S(2)}) collective-permute-start(bf16[96,352]{1,0:T(8,128)(2,1)S(1)} %get-tuple-element.53), channel_id=1, source_target_pairs={{0,24},{2,26},{4,28},{6,30},{8,16},{10,18},{12,20},{14,22},{16,8},... | collective-permute-start | bytes 202760 | tf_op jit(solution)/shard_map/ppermute | solution.py:99
  25.2 11.8 %collective-permute-start.12 = (bf16[96,352]{1,0:T(8,128)(2,1)S(1)}, bf16[96,352]{1,0:T(8,128)(2,1)S(1)}, u32[]{:S(2)}, u32[]{:S(2)}) collective-permute-start(bf16[96,352]{1,0:T(8,128)(2,1)S(1)} %get-tuple-element.54), channel_id=1, source_target_pairs={{0,26},{2,24},{4,30},{6,28},{8,18},{10,16},{12,22},{14,20},{16,10}... | collective-permute-start | bytes 202760 | tf_op jit(solution)/shard_map/ppermute | solution.py:99
  30.8 7.2 %collective-permute-start.13 = (bf16[96,352]{1,0:T(8,128)(2,1)S(1)}, bf16[96,352]{1,0:T(8,128)(2,1)S(1)}, u32[]{:S(2)}, u32[]{:S(2)}) collective-permute-start(bf16[96,352]{1,0:T(8,128)(2,1)S(1)} %get-tuple-element.55), channel_id=1, source_target_pairs={{0,28},{2,30},{4,24},{6,26},{8,20},{10,22},{12,16},{14,18},{16,12}... | collective-permute-start | bytes 202760 | tf_op jit(solution)/shard_map/ppermute | solution.py:99
  34.4 7.1 %collective-permute-start.14 = (bf16[96,352]{1,0:T(8,128)(2,1)S(1)}, bf16[96,352]{1,0:T(8,128)(2,1)S(1)}, u32[]{:S(2)}, u32[]{:S(2)}) collective-permute-start(bf16[96,352]{1,0:T(8,128)(2,1)S(1)} %get-tuple-element.56), channel_id=1, source_target_pairs={{0,30},{2,28},{4,26},{6,24},{8,22},{10,20},{12,18},{14,16},{16,14}... | collective-permute-start | bytes 202760 | tf_op jit(solution)/shard_map/ppermute | solution.py:99
  42.5 14.9 %collective-permute-start.15 = (bf16[352,512]{1,0:T(8,128)(2,1)S(1)}, bf16[352,512]{1,0:T(8,128)(2,1)S(1)}, u32[]{:S(2)}, u32[]{:S(2)}) collective-permute-start(bf16[352,512]{1,0:T(8,128)(2,1)S(1)} %fusion.2.refs_0_), channel_id=1, source_target_pairs={{0,8},{2,10},{4,12},{6,14},{8,16},{10,18},{12,20},{14,22},{16,24},... | collective-permute-start | bytes 1081352 | tf_op jit(solution)/shard_map/ppermute | solution.py:520
  49.4 12.0 %collective-permute-start.18 = (bf16[352,512]{1,0:T(8,128)(2,1)S(1)}, bf16[352,512]{1,0:T(8,128)(2,1)S(1)}, u32[]{:S(2)}, u32[]{:S(2)}) collective-permute-start(bf16[352,512]{1,0:T(8,128)(2,1)S(1)} %fusion.2.refs_0_), channel_id=1, source_target_pairs={{8,0},{10,2},{12,4},{14,6},{16,8},{18,10},{20,12},{22,14},{24,16},... | collective-permute-start | bytes 1081352 | tf_op jit(solution)/shard_map/ppermute | solution.py:521
  61.5 11.4 %collective-permute-start.19 = (bf16[352,512]{1,0:T(8,128)(2,1)S(1)}, bf16[352,512]{1,0:T(8,128)(2,1)}, u32[]{:S(2)}, u32[]{:S(2)}) collective-permute-start(bf16[352,512]{1,0:T(8,128)(2,1)S(1)} %collective-permute-done.18), channel_id=1, source_target_pairs={{8,0},{10,2},{12,4},{14,6},{16,8},{18,10},{20,12},{22,14},{9,1},{1... | collective-permute-start | bytes 1081352 | tf_op jit(solution)/shard_map/ppermute | solution.py:521
  62.8 13.4 %collective-permute-start.31 = (bf16[352,512]{1,0:T(8,128)(2,1)S(1)}, bf16[352,512]{1,0:T(8,128)(2,1)S(1)}, u32[]{:S(2)}, u32[]{:S(2)}) collective-permute-start(bf16[352,512]{1,0:T(8,128)(2,1)S(1)} %fusion.2.refs_0_), channel_id=1, source_target_pairs={{0,4},{2,6},{4,0},{6,2},{8,12},{10,14},{12,8},{14,10},{16,20},{18,... | collective-permute-start | bytes 1081352 | tf_op jit(solution)/shard_map/ppermute | solution.py:99
  63.4 21.4 %collective-permute-start.30 = (bf16[352,512]{1,0:T(8,128)(2,1)S(1)}, bf16[352,512]{1,0:T(8,128)(2,1)S(1)}, u32[]{:S(2)}, u32[]{:S(2)}) collective-permute-start(bf16[352,512]{1,0:T(8,128)(2,1)S(1)} %fusion.2.refs_0_), channel_id=1, source_target_pairs={{0,2},{2,0},{4,6},{6,4},{8,10},{10,8},{12,14},{14,12},{16,18},{18,... | collective-permute-start | bytes 1081352 | tf_op jit(solution)/shard_map/ppermute | solution.py:99
  63.4 12.9 %collective-permute-start.17 = (bf16[352,512]{1,0:T(8,128)(2,1)S(1)}, bf16[352,512]{1,0:T(8,128)(2,1)S(1)}, u32[]{:S(2)}, u32[]{:S(2)}) collective-permute-start(bf16[352,512]{1,0:T(8,128)(2,1)S(1)} %collective-permute-done.16), channel_id=1, source_target_pairs={{16,24},{18,26},{20,28},{22,30},{17,25},{19,27},{21,29},{23,31}} | collective-permute-start | bytes 1081352 | tf_op jit(solution)/shard_map/ppermute | solution.py:520
  72.9 10.7 %collective-permute-start.20 = (bf16[352,512]{1,0:T(8,128)(2,1)}, bf16[352,512]{1,0:T(8,128)(2,1)S(1)}, u32[]{:S(2)}, u32[]{:S(2)}) collective-permute-start(bf16[352,512]{1,0:T(8,128)(2,1)} %collective-permute-done.19), channel_id=1, source_target_pairs={{8,0},{10,2},{12,4},{14,6},{9,1},{11,3},{13,5},{15,7}} | collective-permute-start | bytes 1081352 | tf_op jit(solution)/shard_map/ppermute | solution.py:521
  74.2 11.5 %collective-permute-start.28 = (bf16[352,512]{1,0:T(8,128)(2,1)S(1)}, bf16[352,512]{1,0:T(8,128)(2,1)S(1)}, u32[]{:S(2)}, u32[]{:S(2)}) collective-permute-start(bf16[352,512]{1,0:T(8,128)(2,1)S(1)} %broadcast_select_fusion.refs_0_), channel_id=1, source_target_pairs={{0,4},{2,6},{4,0},{6,2},{8,12},{10,14},{12,8},{14,10},{16,20},{18,... | collective-permute-start | bytes 1081352 | tf_op jit(solution)/shard_map/ppermute | solution.py:99
  76.2 21.1 %collective-permute-start.27 = (bf16[352,512]{1,0:T(8,128)(2,1)S(1)}, bf16[352,512]{1,0:T(8,128)(2,1)}, u32[]{:S(2)}, u32[]{:S(2)}) collective-permute-start(bf16[352,512]{1,0:T(8,128)(2,1)S(1)} %broadcast_select_fusion.refs_0_), channel_id=1, source_target_pairs={{0,2},{2,0},{4,6},{6,4},{8,10},{10,8},{12,14},{14,12},{16,18},{18,... | collective-permute-start | bytes 1081352 | tf_op jit(solution)/shard_map/ppermute | solution.py:99
  76.3 9.4 %collective-permute-start.32 = (bf16[352,512]{1,0:T(8,128)(2,1)S(1)}, bf16[352,512]{1,0:T(8,128)(2,1)S(1)}, u32[]{:S(2)}, u32[]{:S(2)}) collective-permute-start(bf16[352,512]{1,0:T(8,128)(2,1)S(1)} %collective-permute-done.31.refs_2_), channel_id=1, source_target_pairs={{0,2},{2,0},{4,6},{6,4},{8,10},{10,8},{12,14},{14,12},{16,18},{18,... | collective-permute-start | bytes 1081352 | tf_op jit(solution)/shard_map/ppermute | solution.py:99
  83.6 11.4 %collective-permute-start.25 = (bf16[352,512]{1,0:T(8,128)(2,1)S(1)}, bf16[352,512]{1,0:T(8,128)(2,1)}, u32[]{:S(2)}, u32[]{:S(2)}) collective-permute-start(bf16[352,512]{1,0:T(8,128)(2,1)S(1)} %select_select_fusion.refs_0_), channel_id=1, source_target_pairs={{0,4},{2,6},{4,0},{6,2},{8,12},{10,14},{12,8},{14,10},{16,20},{18,... | collective-permute-start | bytes 1081352 | tf_op jit(solution)/shard_map/ppermute | solution.py:99
  84.8 14.2 %collective-permute-start.22 = (bf16[352,512]{1,0:T(8,128)(2,1)S(1)}, bf16[352,512]{1,0:T(8,128)(2,1)S(1)}, u32[]{:S(2)}, u32[]{:S(2)}) collective-permute-start(bf16[352,512]{1,0:T(8,128)(2,1)S(1)} %select_select_fusion.1.refs_0_), channel_id=1, source_target_pairs={{0,4},{2,6},{4,0},{6,2},{8,12},{10,14},{12,8},{14,10},{16,20},{18,... | collective-permute-start | bytes 1081352 | tf_op jit(solution)/shard_map/ppermute | solution.py:99
  85.7 17.8 %collective-permute-start.29 = (bf16[352,512]{1,0:T(8,128)(2,1)S(1)}, bf16[352,512]{1,0:T(8,128)(2,1)}, u32[]{:S(2)}, u32[]{:S(2)}) collective-permute-start(bf16[352,512]{1,0:T(8,128)(2,1)S(1)} %collective-permute-done.28.refs_2_), channel_id=1, source_target_pairs={{0,2},{2,0},{4,6},{6,4},{8,10},{10,8},{12,14},{14,12},{16,18},{18,... | collective-permute-start | bytes 1081352 | tf_op jit(solution)/shard_map/ppermute | solution.py:99
  85.7 23.5 %collective-permute-start.24 = (bf16[352,512]{1,0:T(8,128)(2,1)S(1)}, bf16[352,512]{1,0:T(8,128)(2,1)}, u32[]{:S(2)}, u32[]{:S(2)}) collective-permute-start(bf16[352,512]{1,0:T(8,128)(2,1)S(1)} %select_select_fusion.refs_0_), channel_id=1, source_target_pairs={{0,2},{2,0},{4,6},{6,4},{8,10},{10,8},{12,14},{14,12},{16,18},{18,... | collective-permute-start | bytes 1081352 | tf_op jit(solution)/shard_map/ppermute | solution.py:99
  94.9 14.3 %collective-permute-start.26 = (bf16[352,512]{1,0:T(8,128)(2,1)}, bf16[352,512]{1,0:T(8,128)(2,1)}, u32[]{:S(2)}, u32[]{:S(2)}) collective-permute-start(bf16[352,512]{1,0:T(8,128)(2,1)} %collective-permute-done.25.refs_2_), channel_id=1, source_target_pairs={{0,2},{2,0},{4,6},{6,4},{8,10},{10,8},{12,14},{14,12},{16,18},{18,... | collective-permute-start | bytes 1081352 | tf_op jit(solution)/shard_map/ppermute | solution.py:99
  97.3 17.7 %collective-permute-start.21 = (bf16[352,512]{1,0:T(8,128)(2,1)S(1)}, bf16[352,512]{1,0:T(8,128)(2,1)S(1)}, u32[]{:S(2)}, u32[]{:S(2)}) collective-permute-start(bf16[352,512]{1,0:T(8,128)(2,1)S(1)} %select_select_fusion.1.refs_0_), channel_id=1, source_target_pairs={{0,2},{2,0},{4,6},{6,4},{8,10},{10,8},{12,14},{14,12},{16,18},{18,... | collective-permute-start | bytes 1081352 | tf_op jit(solution)/shard_map/ppermute | solution.py:99
  99.0 16.5 %collective-permute-start.23 = (bf16[352,512]{1,0:T(8,128)(2,1)S(1)}, bf16[352,512]{1,0:T(8,128)(2,1)S(1)}, u32[]{:S(2)}, u32[]{:S(2)}) collective-permute-start(bf16[352,512]{1,0:T(8,128)(2,1)S(1)} %collective-permute-done.22.refs_2_.refs_0_), channel_id=1, source_target_pairs={{0,2},{2,0},{4,6},{6,4},{8,10},{10,8},{12,14},{14,12},{16,18},{18,... | collective-permute-start | bytes 1081352 | tf_op jit(solution)/shard_map/ppermute | solution.py:99
  115.9 7.4 %collective-permute-start.33 = (f32[3,128,128]{2,1,0:T(8,128)S(1)}, f32[3,128,128]{2,1,0:T(8,128)S(1)}, u32[]{:S(2)}, u32[]{:S(2)}) collective-permute-start(f32[3,128,128]{2,1,0:T(8,128)S(1)} %lower.3), channel_id=1, source_target_pairs={{0,1},{1,0},{2,3},{3,2},{4,5},{5,4},{6,7},{7,6},{8,9},{9,8},{10,11... | collective-permute-start | bytes 589832 | tf_op jit(solution)/shard_map/ppermute | solution.py:99
  131.3 14.9 %collective-permute-start.36 = (f32[512,256]{1,0:T(8,128)S(1)}, f32[512,256]{1,0:T(8,128)S(1)}, u32[]{:S(2)}, u32[]{:S(2)}) collective-permute-start(f32[512,256]{1,0:T(8,128)S(1)} %get-tuple-element.76), channel_id=1, source_target_pairs={{0,1},{1,0},{2,3},{3,2},{4,5},{5,4},{6,7},{7,6},{8,9},{9,8},{10,11... | collective-permute-start | bytes 1572872 | tf_op jit(solution)/shard_map/ppermute | solution.py:99
  136.1 20.8 %collective-permute-start.35 = (f32[512,256]{1,0:T(8,128)S(1)}, f32[512,256]{1,0:T(8,128)S(1)}, u32[]{:S(2)}, u32[]{:S(2)}) collective-permute-start(f32[512,256]{1,0:T(8,128)S(1)} %get-tuple-element.74), channel_id=1, source_target_pairs={{0,1},{1,0},{2,3},{3,2},{4,5},{5,4},{6,7},{7,6},{8,9},{9,8},{10,11... | collective-permute-start | bytes 1572872 | tf_op jit(solution)/shard_map/ppermute | solution.py:99
  (9 other events, 44.3 us)

commit v3 on v2

--- a/solution.py
+++ b/solution.py
@@ -12,7 +12,7 @@
 SUBLANES = 16
 GROUP = 4
 ONE_CUT = True
-SENDS = 2
+SENDS = 4
 TILES = 2
 EXACT = lax.Precision.HIGHEST
 
@@ -254,8 +254,7 @@
     vmem = pl.BlockSpec(memory_space=pltpu.VMEM)
     return pl.pallas_call(
         functools.partial(accumulate_kernel, table, blocks, fresh, final),
-        in_specs=[pl.BlockSpec(memory_space=pltpu.SMEM)]
-        + [anywhere] * 2
+        in_specs=[anywhere] * 3
         + [vmem] * (GROUP + len(state)),
         out_specs=[vmem] * len(shapes),
         scratch_shapes=[
@@ -275,20 +274,20 @@
     )(ticked, *away([coeffs, earlier]), *near([*pieces, *state]))
 
 
-def my_rows(capacity, owner_ref, local_ref):
-    panel = owner_ref.shape[1]
+def my_rows(capacity, pivot_ref):
+    panel = pivot_ref.shape[1]
     below = lax.broadcasted_iota(jnp.int32, (panel, panel), 0)
     across = lax.broadcasted_iota(jnp.int32, (panel, panel), 1)
-    turned = owner_ref[...]
+    turned = pivot_ref[0:1, :]
     owners = jnp.sum(jnp.where(below == across, turned, 0), axis=1, keepdims=True)
     same = (owners == turned) & (below < across)
     ranks = jnp.sum(jnp.where(same, 1, 0), axis=0, keepdims=True)
     slots = lax.broadcasted_iota(jnp.int32, (capacity, panel), 0)
     wanted = (ranks == slots) & (turned == lax.axis_index("wide"))
-    return jnp.sum(jnp.where(wanted, local_ref[...] + 1, 0), axis=1, keepdims=True) - 1
-
-
-def cut_kernel(hops, lines, owner_ref, local_ref, coeffs_ref, earlier_ref, *refs):
+    return jnp.sum(jnp.where(wanted, pivot_ref[1:2, :] + 1, 0), axis=1, keepdims=True) - 1
+
+
+def cut_kernel(hops, lines, pivot_ref, coeffs_ref, earlier_ref, *refs):
     outs, (main_ref, sems) = refs[:-2], refs[-2:]
     line, lane = seat()
     depths = [ref.shape[1] // lines for ref in (coeffs_ref, earlier_ref)]
@@ -306,7 +305,7 @@
         copy.start()
     capacity = outs[0].shape[0]
     at = lax.broadcasted_iota(jnp.int32, (capacity, coeffs_ref.shape[0]), 1)
-    select = my_rows(capacity, owner_ref, local_ref) == at
+    select = my_rows(capacity, pivot_ref) == at
     select = jnp.where(select, 1.0, 0.0).astype(jnp.bfloat16)
     for index in range(len(hops)):
         copies[2 * index].wait()
@@ -327,10 +326,12 @@
     vmem = pl.BlockSpec(memory_space=pltpu.VMEM)
     anywhere = pl.BlockSpec(memory_space=pl.ANY)
     total = coeffs.shape[1] + earlier.shape[1]
+    pivots = jnp.concatenate([piv_owner.reshape(1, -1), piv_local[None, :]], axis=0)
+    pivots = near([pivots])[0]
     shape = jax.ShapeDtypeStruct((capacity, total // (lines * GROUP)), jnp.bfloat16)
     return pl.pallas_call(
         functools.partial(cut_kernel, hops, lines),
-        in_specs=[vmem, vmem, anywhere, anywhere],
+        in_specs=[vmem, anywhere, anywhere],
         out_specs=[vmem] * (len(hops) * GROUP),
         out_shape=[shape] * (len(hops) * GROUP),
         scratch_shapes=[
@@ -339,34 +340,34 @@
         ],
         compiler_params=pltpu.CompilerParams(vmem_limit_bytes=24 << 20),
         name="cut",
-    )(piv_owner.reshape(1, -1), piv_local[None, :], *away([coeffs, earlier]))
-
-
-def tick_kernel(local_ref, out_ref):
-    out_ref[0, 0] = local_ref[0, 0]
-
-
-def tick(local):
-    smem = pl.BlockSpec(memory_space=pltpu.SMEM)
+    )(pivots, *away([coeffs, earlier]))
+
+
+def tick(local, hop):
+    return local * (hop + 2) + hop
+
+
+def choose_kernel(order, *refs):
+    which = look_up(order, seat()[0])
+    for index, source in enumerate(refs[:-1]):
+
+        @pl.when(which == index)
+        def _():
+            refs[-1][...] = source[...]
+
+
+def choose(table, received):
+    names = sorted(set(table))
+    vmem = pl.BlockSpec(memory_space=pltpu.VMEM)
+    sources = [received[name] for name in names]
     return pl.pallas_call(
-        tick_kernel,
-        in_specs=[smem],
-        out_specs=smem,
-        out_shape=jax.ShapeDtypeStruct((1, 1), jnp.int32),
-    )(local)
-
-
-def choose(line, table, received):
-    names = sorted(set(table))
-    values = lax.optimization_barrier(tuple(received[name] for name in names))
-    result = values[-1]
-    for index, name in enumerate(names[:-1]):
-        here = False
-        for place, entry in enumerate(table):
-            if entry == name:
-                here = here | (line == place)
-        result = jnp.where(here, values[index], result)
-    return result
+        functools.partial(choose_kernel, tuple(names.index(name) for name in table)),
+        in_specs=[vmem] * len(names),
+        out_specs=vmem,
+        out_shape=jax.ShapeDtypeStruct(sources[0].shape, sources[0].dtype),
+        compiler_params=pltpu.CompilerParams(vmem_limit_bytes=4 << 20),
+        name="choose",
+    )(*near(sources))
 
 
 def split(value):
@@ -477,7 +478,6 @@
     size = lax.axis_size("wide")
     lines = size // GROUP
     me = lax.axis_index("wide")
-    line = me // GROUP
     panel = piv_local.shape[0]
     blocks = inv_tiles.shape[0]
     capacity = 3 * panel // size
@@ -521,7 +521,7 @@
         up = lax.ppermute(up, "wide", falling)
         received[("down", hop)] = down
         received[("up", hop)] = up
-        pieces.append(choose(line, [tables[i][hop - 1][:2] for i in range(lines)], received))
+        pieces.append(choose([tables[i][hop - 1][:2] for i in range(lines)], received))
         sources.append(tuple(tables[i][hop - 1][2] for i in range(lines)))
 
     groups = []
@@ -530,7 +530,7 @@
         beside = exchange(piece, "wide", 1, size)
         corner = exchange(across, "wide", 1, size)
         groups.append([piece, beside, across, corner])
-    ticks = {hop: tick(piv_local[:1, None]) for hop in range(1, lines - 1)}
+    ticks = {hop: tick(owners if hop % 2 else piv_local, hop) for hop in range(1, lines - 1)}
     state = None
     for index, (source, group) in enumerate(zip(sources, groups)):
         final = index == lines - 1

time: 158 us -> 153 us (0.968)
  local copies, waits for them, and re-layouts: 2.82 us -> 0.27 us
  starting transfers between devices: 49.4 us -> 51.8 us
  waiting for transfers between devices: 66.5 us -> 64.2 us
  Pallas kernels: 36.1 us -> 34.2 us
    pallas_call x4, Pallas kernels: 20.6 us -> 15.8 us  [accumulate(): pl.pallas_call(functools.partial(accumulate_kernel, table, blocks, fresh,...]
    pallas_call x2 -> x4, Pallas kernels: 6.47 us -> 9.21 us  [recur(): pl.pallas_call(functools.partial(recur_kernel, blocks), grid=(1,), in_spe...]
    ppermute x31 -> x33, starting transfers between devices: 37.3 us -> 39.6 us  [exchange(): return lax.ppermute(value, axis, [(i, i ^ bit) for i in range(size)])]
    ppermute x31 -> x33, waiting for transfers between devices: 40.9 us -> 39 us  [exchange(): return lax.ppermute(value, axis, [(i, i ^ bit) for i in range(size)])]
  transfers between devices with their start and end apart: 37 -> 39, of which waited for: 13 -> 15; matrix products, arithmetic and copies ran while one was open for 2% -> 0% of each run, Pallas kernels for 17% -> 17%
where the time goes in v3:
time: 153 us
  waiting for transfers between devices  64.2 us (42%)
  starting transfers between devices  51.8 us (34%)
  Pallas kernels  34.2 us (22%)
    ppermute x33, starting transfers between devices, exchange(): return lax.ppermute(value, axis, [(i, i ^ bit) for i in range(size)])  39.6 us
    ppermute x33, waiting for transfers between devices, exchange(): return lax.ppermute(value, axis, [(i, i ^ bit) for i in range(size)])  39 us
    ppermute x3, waiting for transfers between devices, lined_panel(): up = lax.ppermute(up, 'wide', falling)  18.5 us
    pallas_call x4, Pallas kernels, accumulate(): pl.pallas_call(functools.partial(accumulate_kernel, table, blocks, fresh,...  15.8 us
    pallas_call x4, Pallas kernels, recur(): pl.pallas_call(functools.partial(recur_kernel, blocks), grid=(1,), in_spe...  9.21 us
    ppermute x3, starting transfers between devices, lined_panel(): down = lax.ppermute(down, 'wide', rising)  8.3 us
    ppermute x3, waiting for transfers between devices, lined_panel(): down = lax.ppermute(down, 'wide', rising)  6.62 us
    pallas_call x1, Pallas kernels, cut(): pl.pallas_call(functools.partial(cut_kernel, hops, lines), in_specs=[vmem...  5.34 us
  transfers between devices with their start and end apart: 39, of which 15 were waited for; matrix products, arithmetic and copies ran while one was open for 0% of the time, Pallas kernels for 17%

profile of v3, /device:TPU:0, one launch (start us, length us, event | category | flops | bytes accessed | tf_op | source)
XLA Modules:
  0.0 152.8 jit_solution(5173569559838921205)
XLA Ops:
  0.7 5.3 %cut.1 = (bf16[96,352]{1,0:T(8,128)(2,1)S(1)}, bf16[96,352]{1,0:T(8,128)(2,1)S(1)}, bf16[96,352]{1,0:T(8,128)(2,1)S(1)}, bf16[96,352]{1,0:T(8,128)(2,1)S(1)}, bf...) custom-call(s32[2,512]{1,0:T(2,128)S(1)} %pad_add_fusion.pivot_ref, ...), custom_call_target="tpu_custom_call" | custom-call | tf_op jit(solution)/shard_map/cut/pallas_call | solution.py:332
  6.6 2.6 %collective-permute-start.1 = (bf16[96,352]{1,0:T(8,128)(2,1)S(1)}, bf16[96,352]{1,0:T(8,128)(2,1)S(1)}, u32[]{:S(2)}, u32[]{:S(2)}) collective-permute-start(bf16[96,352]{1,0:T(8,128)(2,1)S(1)} %get-tuple-element.37), channel_id=1, source_target_pairs={{0,4},{2,6},{4,0},{6,2},{8,12},{10,14},{12,8},{14,10},{16,20},{18,... | collective-permute-start | bytes 202760 | tf_op jit(solution)/shard_map/ppermute | solution.py:99
  9.2 1.8 %collective-permute-start.3 = (bf16[96,352]{1,0:T(8,128)(2,1)S(1)}, bf16[96,352]{1,0:T(8,128)(2,1)S(1)}, u32[]{:S(2)}, u32[]{:S(2)}) collective-permute-start(bf16[96,352]{1,0:T(8,128)(2,1)S(1)} %get-tuple-element.39), channel_id=1, source_target_pairs={{0,8},{2,10},{4,12},{6,14},{8,0},{10,2},{12,4},{14,6},{16,24},{18,... | collective-permute-start | bytes 202760 | tf_op jit(solution)/shard_map/ppermute | solution.py:99
  11.3 2.7 %collective-permute-start.5 = (bf16[96,352]{1,0:T(8,128)(2,1)S(1)}, bf16[96,352]{1,0:T(8,128)(2,1)S(1)}, u32[]{:S(2)}, u32[]{:S(2)}) collective-permute-start(bf16[96,352]{1,0:T(8,128)(2,1)S(1)} %get-tuple-element.41), channel_id=1, source_target_pairs={{0,12},{2,14},{4,8},{6,10},{8,4},{10,6},{12,0},{14,2},{16,28},{18,... | collective-permute-start | bytes 202760 | tf_op jit(solution)/shard_map/ppermute | solution.py:99
  14.2 2.7 %collective-permute-start.7 = (bf16[96,352]{1,0:T(8,128)(2,1)S(1)}, bf16[96,352]{1,0:T(8,128)(2,1)S(1)}, u32[]{:S(2)}, u32[]{:S(2)}) collective-permute-start(bf16[96,352]{1,0:T(8,128)(2,1)S(1)} %get-tuple-element.43), channel_id=1, source_target_pairs={{0,16},{2,18},{4,20},{6,22},{8,24},{10,26},{12,28},{14,30},{16,0},... | collective-permute-start | bytes 202760 | tf_op jit(solution)/shard_map/ppermute | solution.py:99
  17.9 2.8 %collective-permute-start.9 = (bf16[96,352]{1,0:T(8,128)(2,1)S(1)}, bf16[96,352]{1,0:T(8,128)(2,1)S(1)}, u32[]{:S(2)}, u32[]{:S(2)}) collective-permute-start(bf16[96,352]{1,0:T(8,128)(2,1)S(1)} %get-tuple-element.45), channel_id=1, source_target_pairs={{0,20},{2,22},{4,16},{6,18},{8,28},{10,30},{12,24},{14,26},{16,4},... | collective-permute-start | bytes 202760 | tf_op jit(solution)/shard_map/ppermute | solution.py:99
  21.3 3.2 %collective-permute-start.11 = (bf16[96,352]{1,0:T(8,128)(2,1)S(1)}, bf16[96,352]{1,0:T(8,128)(2,1)S(1)}, u32[]{:S(2)}, u32[]{:S(2)}) collective-permute-start(bf16[96,352]{1,0:T(8,128)(2,1)S(1)} %get-tuple-element.47), channel_id=1, source_target_pairs={{0,24},{2,26},{4,28},{6,30},{8,16},{10,18},{12,20},{14,22},{16,8},... | collective-permute-start | bytes 202760 | tf_op jit(solution)/shard_map/ppermute | solution.py:99
  24.6 4.3 %collective-permute-start.12 = (bf16[96,352]{1,0:T(8,128)(2,1)S(1)}, bf16[96,352]{1,0:T(8,128)(2,1)S(1)}, u32[]{:S(2)}, u32[]{:S(2)}) collective-permute-start(bf16[96,352]{1,0:T(8,128)(2,1)S(1)} %get-tuple-element.48), channel_id=1, source_target_pairs={{0,26},{2,24},{4,30},{6,28},{8,18},{10,16},{12,22},{14,20},{16,10}... | collective-permute-start | bytes 202760 | tf_op jit(solution)/shard_map/ppermute | solution.py:99
  30.1 3.4 %collective-permute-start.13 = (bf16[96,352]{1,0:T(8,128)(2,1)S(1)}, bf16[96,352]{1,0:T(8,128)(2,1)S(1)}, u32[]{:S(2)}, u32[]{:S(2)}) collective-permute-start(bf16[96,352]{1,0:T(8,128)(2,1)S(1)} %get-tuple-element.49), channel_id=1, source_target_pairs={{0,28},{2,30},{4,24},{6,26},{8,20},{10,22},{12,16},{14,18},{16,12}... | collective-permute-start | bytes 202760 | tf_op jit(solution)/shard_map/ppermute | solution.py:99
  33.7 2.6 %collective-permute-start.14 = (bf16[96,352]{1,0:T(8,128)(2,1)S(1)}, bf16[96,352]{1,0:T(8,128)(2,1)S(1)}, u32[]{:S(2)}, u32[]{:S(2)}) collective-permute-start(bf16[96,352]{1,0:T(8,128)(2,1)S(1)} %get-tuple-element.50), channel_id=1, source_target_pairs={{0,30},{2,28},{4,26},{6,24},{8,22},{10,20},{12,18},{14,16},{16,14}... | collective-permute-start | bytes 202760 | tf_op jit(solution)/shard_map/ppermute | solution.py:99
  37.3 3.5 %collective-permute-done.14 = bf16[96,352]{1,0:T(8,128)(2,1)S(1)} collective-permute-done((bf16[96,352]{1,0:T(8,128)(2,1)S(1)}, bf16[96,352]{1,0:T(8,128)(2,1)S(1)}, u32[]{:S(2)}, u32[]{:S(2)}) %collective-permute-start.14) | collective-permute-done | bytes 67616 | tf_op jit(solution)/shard_map/ppermute | solution.py:99
  41.8 7.0 %collective-permute-start.15 = (bf16[352,512]{1,0:T(8,128)(2,1)S(1)}, bf16[352,512]{1,0:T(8,128)(2,1)S(1)}, u32[]{:S(2)}, u32[]{:S(2)}) collective-permute-start(bf16[352,512]{1,0:T(8,128)(2,1)S(1)} %fusion.2.refs_0_), channel_id=1, source_target_pairs={{0,8},{2,10},{4,12},{6,14},{8,16},{10,18},{12,20},{14,22},{16,24},... | collective-permute-start | bytes 1081352 | tf_op jit(solution)/shard_map/ppermute | solution.py:520
  50.1 6.6 %collective-permute-done.15.refs_0_ = bf16[352,512]{1,0:T(8,128)(2,1)S(1)} collective-permute-done((bf16[352,512]{1,0:T(8,128)(2,1)S(1)}, bf16[352,512]{1,0:T(8,128)(2,1)S(1)}, u32[]{:S(2)}, u32[]{:S(2)}) %collective-permute-start.15) | collective-permute-done | bytes 360480 | tf_op jit(solution)/shard_map/ppermute | solution.py:520
  57.4 3.5 %collective-permute-done.18.refs_2_.refs_1_ = bf16[352,512]{1,0:T(8,128)(2,1)S(1)} collective-permute-done((bf16[352,512]{1,0:T(8,128)(2,1)S(1)}, bf16[352,512]{1,0:T(8,128)(2,1)S(1)}, u32[]{:S(2)}, u32[]{:S(2)}) %collective-permute-start.18) | collective-permute-done | bytes 360480 | tf_op jit(solution)/shard_map/ppermute | solution.py:521
  63.4 8.7 %collective-permute-done.19.refs_2_.refs_3_ = bf16[352,512]{1,0:T(8,128)(2,1)S(1)} collective-permute-done((bf16[352,512]{1,0:T(8,128)(2,1)S(1)}, bf16[352,512]{1,0:T(8,128)(2,1)S(1)}, u32[]{:S(2)}, u32[]{:S(2)}) %collective-permute-start.19) | collective-permute-done | bytes 360480 | tf_op jit(solution)/shard_map/ppermute | solution.py:521
  76.2 6.3 %collective-permute-done.20.refs_3_ = bf16[352,512]{1,0:T(8,128)(2,1)S(1)} collective-permute-done((bf16[352,512]{1,0:T(8,128)(2,1)S(1)}, bf16[352,512]{1,0:T(8,128)(2,1)S(1)}, u32[]{:S(2)}, u32[]{:S(2)}) %collective-permute-start.20) | collective-permute-done | bytes 360480 | tf_op jit(solution)/shard_map/ppermute | solution.py:521
  85.4 7.7 %collective-permute-done.25.refs_2_ = bf16[352,512]{1,0:T(8,128)(2,1)S(1)} collective-permute-done((bf16[352,512]{1,0:T(8,128)(2,1)S(1)}, bf16[352,512]{1,0:T(8,128)(2,1)S(1)}, u32[]{:S(2)}, u32[]{:S(2)}) %collective-permute-start.25) | collective-permute-done | bytes 360480 | tf_op jit(solution)/shard_map/ppermute | solution.py:99
  93.7 6.2 %collective-permute-done.22.refs_2_.refs_0_ = bf16[352,512]{1,0:T(8,128)(2,1)S(1)} collective-permute-done((bf16[352,512]{1,0:T(8,128)(2,1)S(1)}, bf16[352,512]{1,0:T(8,128)(2,1)S(1)}, u32[]{:S(2)}, u32[]{:S(2)}) %collective-permute-start.22) | collective-permute-done | bytes 360480 | tf_op jit(solution)/shard_map/ppermute | solution.py:99
  99.9 3.9 %accumulate.4 = (f32[1024,512]{1,0:T(8,128)S(1)}, f32[3,128,128]{2,1,0:T(8,128)S(1)}) custom-call(s32[512]{0:T(512)S(1)} %multiply_add_fusion.tick_ref, bf16[1024,4608]{1,0:T(8,128)(2,1)} %coeffs_ref.9, bf16[1024,1024]{1,0:T(8,128)(2,1)} %earlier_ref.9, bf16[352,512]{1,0:T(8,128)(2,1)S(1)} %fusion.2.refs_0_, ...), custom_call_target="tpu_custom_call" | custom-call | flops 1476395008 | bytes 2883584 | tf_op jit(solution)/shard_map/accumulate/pallas_call | solution.py:255
  103.9 4.0 %accumulate.5 = (f32[1024,512]{1,0:T(8,128)S(1)}, f32[3,128,128]{2,1,0:T(8,128)S(1)}) custom-call(s32[512]{0:T(512)S(1)} %multiply_add_fusion.tick_ref, bf16[1024,4608]{1,0:T(8,128)(2,1)} %coeffs_ref.9, bf16[1024,1024]{1,0:T(8,128)(2,1)} %earlier_ref.9, bf16[352,512]{1,0:T(8,128)(2,1)S(1)} %choose.5.refs_0_, ...), custom_call_target="tpu_custom_call", output_to_operand_aliasing={{0}: (7, {}), {1}: (8, {})} | custom-call | flops 1476395008 | bytes 2883584 | tf_op jit(solution)/shard_map/accumulate/pallas_call | solution.py:255
  107.9 4.0 %accumulate.6 = (f32[1024,512]{1,0:T(8,128)S(1)}, f32[3,128,128]{2,1,0:T(8,128)S(1)}) custom-call(s32[512]{0:T(512)S(1)} %multiply_add_fusion.2.tick_ref, bf16[1024,4608]{1,0:T(8,128)(2,1)} %coeffs_ref.9, bf16[1024,1024]{1,0:T(8,128)(2,1)} %earlier_ref.9, bf16[352,512]{1,0:T(8,128)(2,1)S(1)} %choose.4.refs_0_, ...), custom_call_target="tpu_custom_call", output_to_operand_aliasing={{0}: (7, {}), {1}: (8, {})} | custom-call | flops 1476395008 | bytes 2883584 | tf_op jit(solution)/shard_map/accumulate/pallas_call | solution.py:255
  114.2 5.8 %collective-permute-done.33 = f32[3,128,128]{2,1,0:T(8,128)S(1)} collective-permute-done((f32[3,128,128]{2,1,0:T(8,128)S(1)}, f32[3,128,128]{2,1,0:T(8,128)S(1)}, u32[]{:S(2)}, u32[]{:S(2)}) %collective-permute-start.33) | collective-permute-done | bytes 196640 | tf_op jit(solution)/shard_map/ppermute | solution.py:99
  120.1 4.0 %accumulate.7.partial_ref = f32[1024,512]{1,0:T(8,128)S(1)} custom-call(s32[512]{0:T(512)S(1)} %multiply_add_fusion.2.tick_ref, bf16[1024,4608]{1,0:T(8,128)(2,1)} %coeffs_ref.9, bf16[1024,1024]{1,0:T(8,128)(2,1)} %earlier_ref.9, bf16[352,512]{1,0:T(8,128)(2,1)S(1)} %choose.3.refs_0_, ...), custom_call_target="tpu_custom_call", output_to_operand_aliasing={{}: (7, {})} | custom-call | flops 1476395008 | bytes 2883584 | tf_op jit(solution)/shard_map/accumulate/pallas_call | solution.py:255
  124.1 2.3 %recur.7 = (f32[256,256]{1,0:T(8,128)S(1)}, f32[256,256]{1,0:T(8,128)S(1)}) custom-call(f32[1024,512]{1,0:T(8,128)S(1)} %accumulate.7.partial_ref, f32[3,128,128]{2,1,0:T(8,128)S(1)} %add.24.mine_ref, f32[3,128,128]{2,1,0:T(8,128)S(1)} %collective-permute-done.34.other_ref, f32[4,128,128]{2,1,0:T(8,128)S(1)} %copy-done), custom_call_target="tpu_custom_call" | custom-call | tf_op jit(solution)/shard_map/recur/pallas_call | solution.py:441
  126.4 1.6 %collective-permute-start.38 = (f32[256,256]{1,0:T(8,128)S(1)}, f32[256,256]{1,0:T(8,128)S(1)}, u32[]{:S(2)}, u32[]{:S(2)}) collective-permute-start(f32[256,256]{1,0:T(8,128)S(1)} %get-tuple-element.64), channel_id=1, source_target_pairs={{0,1},{1,0},{2,3},{3,2},{4,5},{5,4},{6,7},{7,6},{8,9},{9,8},{10,11... | collective-permute-start | bytes 786440 | tf_op jit(solution)/shard_map/ppermute | solution.py:99
  128.0 2.3 %recur.6 = (f32[256,256]{1,0:T(8,128)S(1)}, f32[256,256]{1,0:T(8,128)S(1)}) custom-call(f32[1024,512]{1,0:T(8,128)S(1)} %accumulate.7.partial_ref, f32[3,128,128]{2,1,0:T(8,128)S(1)} %add.24.mine_ref, f32[3,128,128]{2,1,0:T(8,128)S(1)} %collective-permute-done.34.other_ref, f32[4,128,128]{2,1,0:T(8,128)S(1)} %copy-done), custom_call_target="tpu_custom_call" | custom-call | tf_op jit(solution)/shard_map/recur/pallas_call | solution.py:441
  130.9 2.3 %recur.5 = (f32[256,256]{1,0:T(8,128)S(1)}, f32[256,256]{1,0:T(8,128)S(1)}) custom-call(f32[1024,512]{1,0:T(8,128)S(1)} %accumulate.7.partial_ref, f32[3,128,128]{2,1,0:T(8,128)S(1)} %add.24.mine_ref, f32[3,128,128]{2,1,0:T(8,128)S(1)} %collective-permute-done.34.other_ref, f32[4,128,128]{2,1,0:T(8,128)S(1)} %copy-done), custom_call_target="tpu_custom_call" | custom-call | tf_op jit(solution)/shard_map/recur/pallas_call | solution.py:441
  133.2 1.6 %collective-permute-start.36 = (f32[256,256]{1,0:T(8,128)S(1)}, f32[256,256]{1,0:T(8,128)S(1)}, u32[]{:S(2)}, u32[]{:S(2)}) collective-permute-start(f32[256,256]{1,0:T(8,128)S(1)} %get-tuple-element.60), channel_id=1, source_target_pairs={{0,1},{1,0},{2,3},{3,2},{4,5},{5,4},{6,7},{7,6},{8,9},{9,8},{10,11... | collective-permute-start | bytes 786440 | tf_op jit(solution)/shard_map/ppermute | solution.py:99
  134.8 2.3 %recur.4 = (f32[256,256]{1,0:T(8,128)S(1)}, f32[256,256]{1,0:T(8,128)S(1)}) custom-call(f32[1024,512]{1,0:T(8,128)S(1)} %accumulate.7.partial_ref, f32[3,128,128]{2,1,0:T(8,128)S(1)} %add.24.mine_ref, f32[3,128,128]{2,1,0:T(8,128)S(1)} %collective-permute-done.34.other_ref, f32[4,128,128]{2,1,0:T(8,128)S(1)} %copy-done), custom_call_target="tpu_custom_call" | custom-call | tf_op jit(solution)/shard_map/recur/pallas_call | solution.py:441
  138.4 2.9 %collective-permute-done.37.taken_ref = f32[256,256]{1,0:T(8,128)S(1)} collective-permute-done((f32[256,256]{1,0:T(8,128)S(1)}, f32[256,256]{1,0:T(8,128)S(1)}, u32[]{:S(2)}, u32[]{:S(2)}) %collective-permute-start.37) | collective-permute-done | bytes 262176 | tf_op jit(solution)/shard_map/ppermute | solution.py:99
  142.0 4.9 %collective-permute-done.36.taken_ref = f32[256,256]{1,0:T(8,128)S(1)} collective-permute-done((f32[256,256]{1,0:T(8,128)S(1)}, f32[256,256]{1,0:T(8,128)S(1)}, u32[]{:S(2)}, u32[]{:S(2)}) %collective-permute-start.36) | collective-permute-done | bytes 262176 | tf_op jit(solution)/shard_map/ppermute | solution.py:99
  147.7 4.4 %collective-permute-done.35.taken_ref = f32[256,256]{1,0:T(8,128)S(1)} collective-permute-done((f32[256,256]{1,0:T(8,128)S(1)}, f32[256,256]{1,0:T(8,128)S(1)}, u32[]{:S(2)}, u32[]{:S(2)}) %collective-permute-start.35) | collective-permute-done | bytes 262176 | tf_op jit(solution)/shard_map/ppermute | solution.py:99
  (93 shorter events, 25.2 us)
Async XLA Ops:
  6.6 7.5 %collective-permute-start.1 = (bf16[96,352]{1,0:T(8,128)(2,1)S(1)}, bf16[96,352]{1,0:T(8,128)(2,1)S(1)}, u32[]{:S(2)}, u32[]{:S(2)}) collective-permute-start(bf16[96,352]{1,0:T(8,128)(2,1)S(1)} %get-tuple-element.37), channel_id=1, source_target_pairs={{0,4},{2,6},{4,0},{6,2},{8,12},{10,14},{12,8},{14,10},{16,20},{18,... | collective-permute-start | bytes 202760 | tf_op jit(solution)/shard_map/ppermute | solution.py:99
  9.2 7.8 %collective-permute-start.3 = (bf16[96,352]{1,0:T(8,128)(2,1)S(1)}, bf16[96,352]{1,0:T(8,128)(2,1)S(1)}, u32[]{:S(2)}, u32[]{:S(2)}) collective-permute-start(bf16[96,352]{1,0:T(8,128)(2,1)S(1)} %get-tuple-element.39), channel_id=1, source_target_pairs={{0,8},{2,10},{4,12},{6,14},{8,0},{10,2},{12,4},{14,6},{16,24},{18,... | collective-permute-start | bytes 202760 | tf_op jit(solution)/shard_map/ppermute | solution.py:99
  11.3 9.4 %collective-permute-start.5 = (bf16[96,352]{1,0:T(8,128)(2,1)S(1)}, bf16[96,352]{1,0:T(8,128)(2,1)S(1)}, u32[]{:S(2)}, u32[]{:S(2)}) collective-permute-start(bf16[96,352]{1,0:T(8,128)(2,1)S(1)} %get-tuple-element.41), channel_id=1, source_target_pairs={{0,12},{2,14},{4,8},{6,10},{8,4},{10,6},{12,0},{14,2},{16,28},{18,... | collective-permute-start | bytes 202760 | tf_op jit(solution)/shard_map/ppermute | solution.py:99
  14.1 7.2 %collective-permute-start.6 = (bf16[96,352]{1,0:T(8,128)(2,1)S(1)}, bf16[96,352]{1,0:T(8,128)(2,1)S(1)}, u32[]{:S(2)}, u32[]{:S(2)}) collective-permute-start(bf16[96,352]{1,0:T(8,128)(2,1)S(1)} %get-tuple-element.42), channel_id=1, source_target_pairs={{0,14},{2,12},{4,10},{6,8},{8,6},{10,4},{12,2},{14,0},{16,30},{18,... | collective-permute-start | bytes 202760 | tf_op jit(solution)/shard_map/ppermute | solution.py:99
  14.2 10.3 %collective-permute-start.7 = (bf16[96,352]{1,0:T(8,128)(2,1)S(1)}, bf16[96,352]{1,0:T(8,128)(2,1)S(1)}, u32[]{:S(2)}, u32[]{:S(2)}) collective-permute-start(bf16[96,352]{1,0:T(8,128)(2,1)S(1)} %get-tuple-element.43), channel_id=1, source_target_pairs={{0,16},{2,18},{4,20},{6,22},{8,24},{10,26},{12,28},{14,30},{16,0},... | collective-permute-start | bytes 202760 | tf_op jit(solution)/shard_map/ppermute | solution.py:99
  17.0 13.1 %collective-permute-start.8 = (bf16[96,352]{1,0:T(8,128)(2,1)S(1)}, bf16[96,352]{1,0:T(8,128)(2,1)S(1)}, u32[]{:S(2)}, u32[]{:S(2)}) collective-permute-start(bf16[96,352]{1,0:T(8,128)(2,1)S(1)} %get-tuple-element.44), channel_id=1, source_target_pairs={{0,18},{2,16},{4,22},{6,20},{8,26},{10,24},{12,30},{14,28},{16,2},... | collective-permute-start | bytes 202760 | tf_op jit(solution)/shard_map/ppermute | solution.py:99
  17.9 15.8 %collective-permute-start.9 = (bf16[96,352]{1,0:T(8,128)(2,1)S(1)}, bf16[96,352]{1,0:T(8,128)(2,1)S(1)}, u32[]{:S(2)}, u32[]{:S(2)}) collective-permute-start(bf16[96,352]{1,0:T(8,128)(2,1)S(1)} %get-tuple-element.45), channel_id=1, source_target_pairs={{0,20},{2,22},{4,16},{6,18},{8,28},{10,30},{12,24},{14,26},{16,4},... | collective-permute-start | bytes 202760 | tf_op jit(solution)/shard_map/ppermute | solution.py:99
  20.8 15.5 %collective-permute-start.10 = (bf16[96,352]{1,0:T(8,128)(2,1)S(1)}, bf16[96,352]{1,0:T(8,128)(2,1)S(1)}, u32[]{:S(2)}, u32[]{:S(2)}) collective-permute-start(bf16[96,352]{1,0:T(8,128)(2,1)S(1)} %get-tuple-element.46), channel_id=1, source_target_pairs={{0,22},{2,20},{4,18},{6,16},{8,30},{10,28},{12,26},{14,24},{16,6},... | collective-permute-start | bytes 202760 | tf_op jit(solution)/shard_map/ppermute | solution.py:99
  21.3 15.0 %collective-permute-start.11 = (bf16[96,352]{1,0:T(8,128)(2,1)S(1)}, bf16[96,352]{1,0:T(8,128)(2,1)S(1)}, u32[]{:S(2)}, u32[]{:S(2)}) collective-permute-start(bf16[96,352]{1,0:T(8,128)(2,1)S(1)} %get-tuple-element.47), channel_id=1, source_target_pairs={{0,24},{2,26},{4,28},{6,30},{8,16},{10,18},{12,20},{14,22},{16,8},... | collective-permute-start | bytes 202760 | tf_op jit(solution)/shard_map/ppermute | solution.py:99
  24.6 11.8 %collective-permute-start.12 = (bf16[96,352]{1,0:T(8,128)(2,1)S(1)}, bf16[96,352]{1,0:T(8,128)(2,1)S(1)}, u32[]{:S(2)}, u32[]{:S(2)}) collective-permute-start(bf16[96,352]{1,0:T(8,128)(2,1)S(1)} %get-tuple-element.48), channel_id=1, source_target_pairs={{0,26},{2,24},{4,30},{6,28},{8,18},{10,16},{12,22},{14,20},{16,10}... | collective-permute-start | bytes 202760 | tf_op jit(solution)/shard_map/ppermute | solution.py:99
  41.8 14.9 %collective-permute-start.15 = (bf16[352,512]{1,0:T(8,128)(2,1)S(1)}, bf16[352,512]{1,0:T(8,128)(2,1)S(1)}, u32[]{:S(2)}, u32[]{:S(2)}) collective-permute-start(bf16[352,512]{1,0:T(8,128)(2,1)S(1)} %fusion.2.refs_0_), channel_id=1, source_target_pairs={{0,8},{2,10},{4,12},{6,14},{8,16},{10,18},{12,20},{14,22},{16,24},... | collective-permute-start | bytes 1081352 | tf_op jit(solution)/shard_map/ppermute | solution.py:520
  48.8 12.1 %collective-permute-start.18 = (bf16[352,512]{1,0:T(8,128)(2,1)S(1)}, bf16[352,512]{1,0:T(8,128)(2,1)S(1)}, u32[]{:S(2)}, u32[]{:S(2)}) collective-permute-start(bf16[352,512]{1,0:T(8,128)(2,1)S(1)} %fusion.2.refs_0_), channel_id=1, source_target_pairs={{8,0},{10,2},{12,4},{14,6},{16,8},{18,10},{20,12},{22,14},{24,16},... | collective-permute-start | bytes 1081352 | tf_op jit(solution)/shard_map/ppermute | solution.py:521
  60.8 11.3 %collective-permute-start.19 = (bf16[352,512]{1,0:T(8,128)(2,1)S(1)}, bf16[352,512]{1,0:T(8,128)(2,1)S(1)}, u32[]{:S(2)}, u32[]{:S(2)}) collective-permute-start(bf16[352,512]{1,0:T(8,128)(2,1)S(1)} %collective-permute-done.18.refs_2_.refs_1_), channel_id=1, source_target_pairs={{8,0},{10,2},{12,4},{14,6},{16,8},{18,10},{20,12},{22,14},{9,1},{1... | collective-permute-start | bytes 1081352 | tf_op jit(solution)/shard_map/ppermute | solution.py:521
  62.1 11.4 %collective-permute-start.31 = (bf16[352,512]{1,0:T(8,128)(2,1)S(1)}, bf16[352,512]{1,0:T(8,128)(2,1)S(1)}, u32[]{:S(2)}, u32[]{:S(2)}) collective-permute-start(bf16[352,512]{1,0:T(8,128)(2,1)S(1)} %fusion.2.refs_0_), channel_id=1, source_target_pairs={{0,4},{2,6},{4,0},{6,2},{8,12},{10,14},{12,8},{14,10},{16,20},{18,... | collective-permute-start | bytes 1081352 | tf_op jit(solution)/shard_map/ppermute | solution.py:99
  62.7 12.3 %collective-permute-start.17 = (bf16[352,512]{1,0:T(8,128)(2,1)S(1)}, bf16[352,512]{1,0:T(8,128)(2,1)S(1)}, u32[]{:S(2)}, u32[]{:S(2)}) collective-permute-start(bf16[352,512]{1,0:T(8,128)(2,1)S(1)} %collective-permute-done.16.refs_0_.refs_1_), channel_id=1, source_target_pairs={{16,24},{18,26},{20,28},{22,30},{17,25},{19,27},{21,29},{23,31}} | collective-permute-start | bytes 1081352 | tf_op jit(solution)/shard_map/ppermute | solution.py:520
  72.1 10.4 %collective-permute-start.20 = (bf16[352,512]{1,0:T(8,128)(2,1)S(1)}, bf16[352,512]{1,0:T(8,128)(2,1)S(1)}, u32[]{:S(2)}, u32[]{:S(2)}) collective-permute-start(bf16[352,512]{1,0:T(8,128)(2,1)S(1)} %collective-permute-done.19.refs_2_.refs_3_), channel_id=1, source_target_pairs={{8,0},{10,2},{12,4},{14,6},{9,1},{11,3},{13,5},{15,7}} | collective-permute-start | bytes 1081352 | tf_op jit(solution)/shard_map/ppermute | solution.py:521
  73.4 9.2 %collective-permute-start.30 = (bf16[352,512]{1,0:T(8,128)(2,1)S(1)}, bf16[352,512]{1,0:T(8,128)(2,1)S(1)}, u32[]{:S(2)}, u32[]{:S(2)}) collective-permute-start(bf16[352,512]{1,0:T(8,128)(2,1)S(1)} %fusion.2.refs_0_), channel_id=1, source_target_pairs={{0,2},{2,0},{4,6},{6,4},{8,10},{10,8},{12,14},{14,12},{16,18},{18,... | collective-permute-start | bytes 1081352 | tf_op jit(solution)/shard_map/ppermute | solution.py:99
  73.6 10.3 %collective-permute-start.32 = (bf16[352,512]{1,0:T(8,128)(2,1)S(1)}, bf16[352,512]{1,0:T(8,128)(2,1)S(1)}, u32[]{:S(2)}, u32[]{:S(2)}) collective-permute-start(bf16[352,512]{1,0:T(8,128)(2,1)S(1)} %collective-permute-done.31.refs_2_), channel_id=1, source_target_pairs={{0,2},{2,0},{4,6},{6,4},{8,10},{10,8},{12,14},{14,12},{16,18},{18,... | collective-permute-start | bytes 1081352 | tf_op jit(solution)/shard_map/ppermute | solution.py:99
  74.1 11.3 %collective-permute-start.28 = (bf16[352,512]{1,0:T(8,128)(2,1)S(1)}, bf16[352,512]{1,0:T(8,128)(2,1)S(1)}, u32[]{:S(2)}, u32[]{:S(2)}) collective-permute-start(bf16[352,512]{1,0:T(8,128)(2,1)S(1)} %choose.5.refs_0_), channel_id=1, source_target_pairs={{0,4},{2,6},{4,0},{6,2},{8,12},{10,14},{12,8},{14,10},{16,20},{18,... | collective-permute-start | bytes 1081352 | tf_op jit(solution)/shard_map/ppermute | solution.py:99
  75.0 18.1 %collective-permute-start.25 = (bf16[352,512]{1,0:T(8,128)(2,1)S(1)}, bf16[352,512]{1,0:T(8,128)(2,1)S(1)}, u32[]{:S(2)}, u32[]{:S(2)}) collective-permute-start(bf16[352,512]{1,0:T(8,128)(2,1)S(1)} %choose.4.refs_0_), channel_id=1, source_target_pairs={{0,4},{2,6},{4,0},{6,2},{8,12},{10,14},{12,8},{14,10},{16,20},{18,... | collective-permute-start | bytes 1081352 | tf_op jit(solution)/shard_map/ppermute | solution.py:99
  82.6 10.6 %collective-permute-start.27 = (bf16[352,512]{1,0:T(8,128)(2,1)S(1)}, bf16[352,512]{1,0:T(8,128)(2,1)S(1)}, u32[]{:S(2)}, u32[]{:S(2)}) collective-permute-start(bf16[352,512]{1,0:T(8,128)(2,1)S(1)} %choose.5.refs_0_), channel_id=1, source_target_pairs={{0,2},{2,0},{4,6},{6,4},{8,10},{10,8},{12,14},{14,12},{16,18},{18,... | collective-permute-start | bytes 1081352 | tf_op jit(solution)/shard_map/ppermute | solution.py:99
  82.6 17.3 %collective-permute-start.22 = (bf16[352,512]{1,0:T(8,128)(2,1)S(1)}, bf16[352,512]{1,0:T(8,128)(2,1)S(1)}, u32[]{:S(2)}, u32[]{:S(2)}) collective-permute-start(bf16[352,512]{1,0:T(8,128)(2,1)S(1)} %choose.3.refs_0_), channel_id=1, source_target_pairs={{0,4},{2,6},{4,0},{6,2},{8,12},{10,14},{12,8},{14,10},{16,20},{18,... | collective-permute-start | bytes 1081352 | tf_op jit(solution)/shard_map/ppermute | solution.py:99
  83.9 24.0 %collective-permute-start.24 = (bf16[352,512]{1,0:T(8,128)(2,1)S(1)}, bf16[352,512]{1,0:T(8,128)(2,1)S(1)}, u32[]{:S(2)}, u32[]{:S(2)}) collective-permute-start(bf16[352,512]{1,0:T(8,128)(2,1)S(1)} %choose.4.refs_0_), channel_id=1, source_target_pairs={{0,2},{2,0},{4,6},{6,4},{8,10},{10,8},{12,14},{14,12},{16,18},{18,... | collective-permute-start | bytes 1081352 | tf_op jit(solution)/shard_map/ppermute | solution.py:99
  85.4 18.5 %collective-permute-start.29 = (bf16[352,512]{1,0:T(8,128)(2,1)S(1)}, bf16[352,512]{1,0:T(8,128)(2,1)S(1)}, u32[]{:S(2)}, u32[]{:S(2)}) collective-permute-start(bf16[352,512]{1,0:T(8,128)(2,1)S(1)} %collective-permute-done.28.refs_2_), channel_id=1, source_target_pairs={{0,2},{2,0},{4,6},{6,4},{8,10},{10,8},{12,14},{14,12},{16,18},{18,... | collective-permute-start | bytes 1081352 | tf_op jit(solution)/shard_map/ppermute | solution.py:99
  93.1 14.7 %collective-permute-start.26 = (bf16[352,512]{1,0:T(8,128)(2,1)S(1)}, bf16[352,512]{1,0:T(8,128)(2,1)S(1)}, u32[]{:S(2)}, u32[]{:S(2)}) collective-permute-start(bf16[352,512]{1,0:T(8,128)(2,1)S(1)} %collective-permute-done.25.refs_2_), channel_id=1, source_target_pairs={{0,2},{2,0},{4,6},{6,4},{8,10},{10,8},{12,14},{14,12},{16,18},{18,... | collective-permute-start | bytes 1081352 | tf_op jit(solution)/shard_map/ppermute | solution.py:99
  93.1 18.7 %collective-permute-start.21 = (bf16[352,512]{1,0:T(8,128)(2,1)S(1)}, bf16[352,512]{1,0:T(8,128)(2,1)S(1)}, u32[]{:S(2)}, u32[]{:S(2)}) collective-permute-start(bf16[352,512]{1,0:T(8,128)(2,1)S(1)} %choose.3.refs_0_), channel_id=1, source_target_pairs={{0,2},{2,0},{4,6},{6,4},{8,10},{10,8},{12,14},{14,12},{16,18},{18,... | collective-permute-start | bytes 1081352 | tf_op jit(solution)/shard_map/ppermute | solution.py:99
  99.9 12.3 %collective-permute-start.23 = (bf16[352,512]{1,0:T(8,128)(2,1)S(1)}, bf16[352,512]{1,0:T(8,128)(2,1)S(1)}, u32[]{:S(2)}, u32[]{:S(2)}) collective-permute-start(bf16[352,512]{1,0:T(8,128)(2,1)S(1)} %collective-permute-done.22.refs_2_.refs_0_), channel_id=1, source_target_pairs={{0,2},{2,0},{4,6},{6,4},{8,10},{10,8},{12,14},{14,12},{16,18},{18,... | collective-permute-start | bytes 1081352 | tf_op jit(solution)/shard_map/ppermute | solution.py:99
  112.7 7.3 %collective-permute-start.33 = (f32[3,128,128]{2,1,0:T(8,128)S(1)}, f32[3,128,128]{2,1,0:T(8,128)S(1)}, u32[]{:S(2)}, u32[]{:S(2)}) collective-permute-start(f32[3,128,128]{2,1,0:T(8,128)S(1)} %lower.3), channel_id=1, source_target_pairs={{0,1},{1,0},{2,3},{3,2},{4,5},{5,4},{6,7},{7,6},{8,9},{9,8},{10,11... | collective-permute-start | bytes 589832 | tf_op jit(solution)/shard_map/ppermute | solution.py:99
  126.4 11.3 %collective-permute-start.38 = (f32[256,256]{1,0:T(8,128)S(1)}, f32[256,256]{1,0:T(8,128)S(1)}, u32[]{:S(2)}, u32[]{:S(2)}) collective-permute-start(f32[256,256]{1,0:T(8,128)S(1)} %get-tuple-element.64), channel_id=1, source_target_pairs={{0,1},{1,0},{2,3},{3,2},{4,5},{5,4},{6,7},{7,6},{8,9},{9,8},{10,11... | collective-permute-start | bytes 786440 | tf_op jit(solution)/shard_map/ppermute | solution.py:99
  130.3 11.0 %collective-permute-start.37 = (f32[256,256]{1,0:T(8,128)S(1)}, f32[256,256]{1,0:T(8,128)S(1)}, u32[]{:S(2)}, u32[]{:S(2)}) collective-permute-start(f32[256,256]{1,0:T(8,128)S(1)} %get-tuple-element.62), channel_id=1, source_target_pairs={{0,1},{1,0},{2,3},{3,2},{4,5},{5,4},{6,7},{7,6},{8,9},{9,8},{10,11... | collective-permute-start | bytes 786440 | tf_op jit(solution)/shard_map/ppermute | solution.py:99
  133.2 13.7 %collective-permute-start.36 = (f32[256,256]{1,0:T(8,128)S(1)}, f32[256,256]{1,0:T(8,128)S(1)}, u32[]{:S(2)}, u32[]{:S(2)}) collective-permute-start(f32[256,256]{1,0:T(8,128)S(1)} %get-tuple-element.60), channel_id=1, source_target_pairs={{0,1},{1,0},{2,3},{3,2},{4,5},{5,4},{6,7},{7,6},{8,9},{9,8},{10,11... | collective-permute-start | bytes 786440 | tf_op jit(solution)/shard_map/ppermute | solution.py:99
  137.1 14.9 %collective-permute-start.35 = (f32[256,256]{1,0:T(8,128)S(1)}, f32[256,256]{1,0:T(8,128)S(1)}, u32[]{:S(2)}, u32[]{:S(2)}) collective-permute-start(f32[256,256]{1,0:T(8,128)S(1)} %get-tuple-element.58), channel_id=1, source_target_pairs={{0,1},{1,0},{2,3},{3,2},{4,5},{5,4},{6,7},{7,6},{8,9},{9,8},{10,11... | collective-permute-start | bytes 786440 | tf_op jit(solution)/shard_map/ppermute | solution.py:99
  (10 other events, 74.0 us)

commit v4 on v3

--- a/solution.py
+++ b/solution.py
@@ -72,20 +72,6 @@
     diag_block = lax.psum(diag[0] - diag[1], "narrow")
     factor = panel_factor(density, diag_block, inv_tiles)
     return lax.all_to_all(factor, "narrow", split_axis=1, concat_axis=0, tiled=True)
-
-
-def arrival_order(lines):
-    tables = []
-    for line in range(lines):
-        order = []
-        for hop in range(1, lines):
-            sides = ("up", "down") if 2 * line < lines else ("down", "up")
-            for side in sides:
-                source = line + hop if side == "up" else line - hop
-                if 0 <= source < lines:
-                    order.append((side, hop, source))
-        tables.append(order)
-    return tables
 
 
 def look_up(table, line):
@@ -509,20 +495,24 @@
         preferred_element_type=jnp.float32,
     ).astype(jnp.bfloat16)
 
-    up, down = own, own
-    tables = arrival_order(lines)
-    received = {}
-    pieces = [own]
-    sources = [tuple(range(lines))]
-    for hop in range(1, lines):
-        rising = [(i, i + GROUP) for i in range(size - GROUP) if i // GROUP >= hop - 1]
-        falling = [(i, i - GROUP) for i in range(GROUP, size) if lines - 1 - i // GROUP >= hop - 1]
-        down = lax.ppermute(down, "wide", rising)
-        up = lax.ppermute(up, "wide", falling)
-        received[("down", hop)] = down
-        received[("up", hop)] = up
-        pieces.append(choose([tables[i][hop - 1][:2] for i in range(lines)], received))
-        sources.append(tuple(tables[i][hop - 1][2] for i in range(lines)))
+    def swap_middle(value):
+        pairs = [(i, i ^ (3 * GROUP)) for i in range(size) if i // GROUP in (1, 2)]
+        return lax.ppermute(value, "wide", pairs)
+
+    def send_out(value):
+        pairs = [(i, i ^ GROUP) for i in range(size) if i // GROUP in (1, 2)]
+        return lax.ppermute(value, "wide", pairs)
+
+    pair = exchange(own, "wide", GROUP, size)
+    middle = swap_middle(own)
+    farther = swap_middle(pair)
+    out = send_out(middle)
+    last_out = send_out(farther)
+    table = ["out", "middle", "middle", "out"]
+    third = choose(table, {"out": out, "middle": middle})
+    fourth = choose(table, {"out": last_out, "middle": farther})
+    pieces = [own, pair, third, fourth]
+    sources = [(0, 1, 2, 3), (1, 0, 3, 2), (2, 2, 1, 1), (3, 3, 0, 0)]
 
     groups = []
     for piece in pieces:
@@ -560,7 +550,7 @@
     return (
         size == lines * GROUP
         and size & (size - 1) == 0
-        and lines > 1
+        and lines == 4
         and lax.axis_size("narrow") == 2
         and coeffs.shape[0] % (SUBLANES * TILES) == 0
         and coeffs.shape[1] % (lines * LANES) == 0

time: 153 us -> 147 us (0.961)
  waiting for transfers between devices: 64.2 us -> 60.3 us
  starting transfers between devices: 51.8 us -> 48.3 us
    ppermute x6 -> x4, waiting for transfers between devices: 25.2 us -> 9.67 us  [the longest x2 9.67 us: send_out(): return lax.ppermute(value, 'wide', pairs)]
    ppermute x33 -> x34, waiting for transfers between devices: 39 us -> 50.6 us  [exchange(): return lax.ppermute(value, axis, [(i, i ^ bit) for i in range(size)])]
    ppermute x6 -> x4, starting transfers between devices: 12.2 us -> 3.92 us  [the longest x2 2.57 us: send_out(): return lax.ppermute(value, 'wide', pairs)]
    ppermute x33 -> x34, starting transfers between devices: 39.6 us -> 44.4 us  [exchange(): return lax.ppermute(value, axis, [(i, i ^ bit) for i in range(size)])]
  transfers between devices with their start and end apart: 39 -> 38, of which waited for: 15 -> 14; matrix products, arithmetic and copies ran while one was open for 0% -> 0% of each run, Pallas kernels for 17% -> 17%
where the time goes in v4:
time: 147 us; the launch traced here: 145 us
  waiting for transfers between devices  60.3 us (41%)
  starting transfers between devices  48.3 us (33%)
  Pallas kernels  34.1 us (23%)
    ppermute x34, waiting for transfers between devices, exchange(): return lax.ppermute(value, axis, [(i, i ^ bit) for i in range(size)])  50.6 us
    ppermute x34, starting transfers between devices, exchange(): return lax.ppermute(value, axis, [(i, i ^ bit) for i in range(size)])  44.4 us
    pallas_call x4, Pallas kernels, accumulate(): pl.pallas_call(functools.partial(accumulate_kernel, table, blocks, fresh,...  15.8 us
    ppermute x2, waiting for transfers between devices, send_out(): return lax.ppermute(value, 'wide', pairs)  9.67 us
    pallas_call x4, Pallas kernels, recur(): pl.pallas_call(functools.partial(recur_kernel, blocks), grid=(1,), in_spe...  9.21 us
    pallas_call x1, Pallas kernels, cut(): pl.pallas_call(functools.partial(cut_kernel, hops, lines), in_specs=[vmem...  5.34 us
  transfers between devices with their start and end apart: 38, of which 14 were waited for; matrix products, arithmetic and copies ran while one was open for 0% of the time, Pallas kernels for 17%

profile of v4, /device:TPU:0, one launch (start us, length us, event | category | flops | bytes accessed | tf_op | source)
XLA Modules:
  0.0 145.3 jit_solution(5436943711538704887)
XLA Ops:
  0.7 5.3 %cut.1 = (bf16[96,352]{1,0:T(8,128)(2,1)S(1)}, bf16[96,352]{1,0:T(8,128)(2,1)S(1)}, bf16[96,352]{1,0:T(8,128)(2,1)S(1)}, bf16[96,352]{1,0:T(8,128)(2,1)S(1)}, bf...) custom-call(s32[2,512]{1,0:T(2,128)S(1)} %pad_add_fusion.pivot_ref, ...), custom_call_target="tpu_custom_call" | custom-call | tf_op jit(solution)/shard_map/cut/pallas_call | solution.py:318
  6.6 2.6 %collective-permute-start.1 = (bf16[96,352]{1,0:T(8,128)(2,1)S(1)}, bf16[96,352]{1,0:T(8,128)(2,1)S(1)}, u32[]{:S(2)}, u32[]{:S(2)}) collective-permute-start(bf16[96,352]{1,0:T(8,128)(2,1)S(1)} %get-tuple-element.37), channel_id=1, source_target_pairs={{0,4},{2,6},{4,0},{6,2},{8,12},{10,14},{12,8},{14,10},{16,20},{18,... | collective-permute-start | bytes 202760 | tf_op jit(solution)/shard_map/ppermute | solution.py:85
  9.2 1.8 %collective-permute-start.3 = (bf16[96,352]{1,0:T(8,128)(2,1)S(1)}, bf16[96,352]{1,0:T(8,128)(2,1)S(1)}, u32[]{:S(2)}, u32[]{:S(2)}) collective-permute-start(bf16[96,352]{1,0:T(8,128)(2,1)S(1)} %get-tuple-element.39), channel_id=1, source_target_pairs={{0,8},{2,10},{4,12},{6,14},{8,0},{10,2},{12,4},{14,6},{16,24},{18,... | collective-permute-start | bytes 202760 | tf_op jit(solution)/shard_map/ppermute | solution.py:85
  11.3 2.7 %collective-permute-start.5 = (bf16[96,352]{1,0:T(8,128)(2,1)S(1)}, bf16[96,352]{1,0:T(8,128)(2,1)S(1)}, u32[]{:S(2)}, u32[]{:S(2)}) collective-permute-start(bf16[96,352]{1,0:T(8,128)(2,1)S(1)} %get-tuple-element.41), channel_id=1, source_target_pairs={{0,12},{2,14},{4,8},{6,10},{8,4},{10,6},{12,0},{14,2},{16,28},{18,... | collective-permute-start | bytes 202760 | tf_op jit(solution)/shard_map/ppermute | solution.py:85
  14.2 2.7 %collective-permute-start.7 = (bf16[96,352]{1,0:T(8,128)(2,1)S(1)}, bf16[96,352]{1,0:T(8,128)(2,1)S(1)}, u32[]{:S(2)}, u32[]{:S(2)}) collective-permute-start(bf16[96,352]{1,0:T(8,128)(2,1)S(1)} %get-tuple-element.43), channel_id=1, source_target_pairs={{0,16},{2,18},{4,20},{6,22},{8,24},{10,26},{12,28},{14,30},{16,0},... | collective-permute-start | bytes 202760 | tf_op jit(solution)/shard_map/ppermute | solution.py:85
  17.9 2.8 %collective-permute-start.9 = (bf16[96,352]{1,0:T(8,128)(2,1)S(1)}, bf16[96,352]{1,0:T(8,128)(2,1)S(1)}, u32[]{:S(2)}, u32[]{:S(2)}) collective-permute-start(bf16[96,352]{1,0:T(8,128)(2,1)S(1)} %get-tuple-element.45), channel_id=1, source_target_pairs={{0,20},{2,22},{4,16},{6,18},{8,28},{10,30},{12,24},{14,26},{16,4},... | collective-permute-start | bytes 202760 | tf_op jit(solution)/shard_map/ppermute | solution.py:85
  21.3 3.2 %collective-permute-start.11 = (bf16[96,352]{1,0:T(8,128)(2,1)S(1)}, bf16[96,352]{1,0:T(8,128)(2,1)S(1)}, u32[]{:S(2)}, u32[]{:S(2)}) collective-permute-start(bf16[96,352]{1,0:T(8,128)(2,1)S(1)} %get-tuple-element.47), channel_id=1, source_target_pairs={{0,24},{2,26},{4,28},{6,30},{8,16},{10,18},{12,20},{14,22},{16,8},... | collective-permute-start | bytes 202760 | tf_op jit(solution)/shard_map/ppermute | solution.py:85
  24.6 4.3 %collective-permute-start.12 = (bf16[96,352]{1,0:T(8,128)(2,1)S(1)}, bf16[96,352]{1,0:T(8,128)(2,1)S(1)}, u32[]{:S(2)}, u32[]{:S(2)}) collective-permute-start(bf16[96,352]{1,0:T(8,128)(2,1)S(1)} %get-tuple-element.48), channel_id=1, source_target_pairs={{0,26},{2,24},{4,30},{6,28},{8,18},{10,16},{12,22},{14,20},{16,10}... | collective-permute-start | bytes 202760 | tf_op jit(solution)/shard_map/ppermute | solution.py:85
  30.1 3.4 %collective-permute-start.13 = (bf16[96,352]{1,0:T(8,128)(2,1)S(1)}, bf16[96,352]{1,0:T(8,128)(2,1)S(1)}, u32[]{:S(2)}, u32[]{:S(2)}) collective-permute-start(bf16[96,352]{1,0:T(8,128)(2,1)S(1)} %get-tuple-element.49), channel_id=1, source_target_pairs={{0,28},{2,30},{4,24},{6,26},{8,20},{10,22},{12,16},{14,18},{16,12}... | collective-permute-start | bytes 202760 | tf_op jit(solution)/shard_map/ppermute | solution.py:85
  33.7 2.6 %collective-permute-start.14 = (bf16[96,352]{1,0:T(8,128)(2,1)S(1)}, bf16[96,352]{1,0:T(8,128)(2,1)S(1)}, u32[]{:S(2)}, u32[]{:S(2)}) collective-permute-start(bf16[96,352]{1,0:T(8,128)(2,1)S(1)} %get-tuple-element.50), channel_id=1, source_target_pairs={{0,30},{2,28},{4,26},{6,24},{8,22},{10,20},{12,18},{14,16},{16,14}... | collective-permute-start | bytes 202760 | tf_op jit(solution)/shard_map/ppermute | solution.py:85
  37.3 3.5 %collective-permute-done.14 = bf16[96,352]{1,0:T(8,128)(2,1)S(1)} collective-permute-done((bf16[96,352]{1,0:T(8,128)(2,1)S(1)}, bf16[96,352]{1,0:T(8,128)(2,1)S(1)}, u32[]{:S(2)}, u32[]{:S(2)}) %collective-permute-start.14) | collective-permute-done | bytes 67616 | tf_op jit(solution)/shard_map/ppermute | solution.py:85
  41.8 5.1 %collective-permute-start.15 = (bf16[352,512]{1,0:T(8,128)(2,1)S(1)}, bf16[352,512]{1,0:T(8,128)(2,1)S(1)}, u32[]{:S(2)}, u32[]{:S(2)}) collective-permute-start(bf16[352,512]{1,0:T(8,128)(2,1)S(1)} %fusion.2.refs_0_), channel_id=1, source_target_pairs={{0,8},{2,10},{4,12},{6,14},{8,0},{10,2},{12,4},{14,6},{16,24},{18,... | collective-permute-start | bytes 1081352 | tf_op jit(solution)/shard_map/ppermute | solution.py:85
  47.6 8.0 %collective-permute-done.15.refs_0_ = bf16[352,512]{1,0:T(8,128)(2,1)S(1)} collective-permute-done((bf16[352,512]{1,0:T(8,128)(2,1)S(1)}, bf16[352,512]{1,0:T(8,128)(2,1)S(1)}, u32[]{:S(2)}, u32[]{:S(2)}) %collective-permute-start.15) | collective-permute-done | bytes 360480 | tf_op jit(solution)/shard_map/ppermute | solution.py:85
  59.6 6.7 %collective-permute-done.30.refs_2_ = bf16[352,512]{1,0:T(8,128)(2,1)S(1)} collective-permute-done((bf16[352,512]{1,0:T(8,128)(2,1)S(1)}, bf16[352,512]{1,0:T(8,128)(2,1)S(1)}, u32[]{:S(2)}, u32[]{:S(2)}) %collective-permute-start.30) | collective-permute-done | bytes 360480 | tf_op jit(solution)/shard_map/ppermute | solution.py:85
  66.7 4.5 %collective-permute-done.22.refs_1_ = bf16[352,512]{1,0:T(8,128)(2,1)S(1)} collective-permute-done((bf16[352,512]{1,0:T(8,128)(2,1)S(1)}, bf16[352,512]{1,0:T(8,128)(2,1)S(1)}, u32[]{:S(2)}, u32[]{:S(2)}) %collective-permute-start.22) | collective-permute-done | bytes 360480 | tf_op jit(solution)/shard_map/ppermute | solution.py:504
  71.2 1.6 %collective-permute-start.24 = (bf16[352,512]{1,0:T(8,128)(2,1)S(1)}, bf16[352,512]{1,0:T(8,128)(2,1)S(1)}, u32[]{:S(2)}, u32[]{:S(2)}) collective-permute-start(bf16[352,512]{1,0:T(8,128)(2,1)S(1)} %choose.3.refs_0_), channel_id=1, source_target_pairs={{0,4},{2,6},{4,0},{6,2},{8,12},{10,14},{12,8},{14,10},{16,20},{18,... | collective-permute-start | bytes 1081352 | tf_op jit(solution)/shard_map/ppermute | solution.py:85
  72.8 5.2 %collective-permute-done.17.refs_1_ = bf16[352,512]{1,0:T(8,128)(2,1)S(1)} collective-permute-done((bf16[352,512]{1,0:T(8,128)(2,1)S(1)}, bf16[352,512]{1,0:T(8,128)(2,1)S(1)}, u32[]{:S(2)}, u32[]{:S(2)}) %collective-permute-start.17) | collective-permute-done | bytes 360480 | tf_op jit(solution)/shard_map/ppermute | solution.py:504
  79.8 5.4 %collective-permute-done.24.refs_2_ = bf16[352,512]{1,0:T(8,128)(2,1)S(1)} collective-permute-done((bf16[352,512]{1,0:T(8,128)(2,1)S(1)}, bf16[352,512]{1,0:T(8,128)(2,1)S(1)}, u32[]{:S(2)}, u32[]{:S(2)}) %collective-permute-start.24) | collective-permute-done | bytes 360480 | tf_op jit(solution)/shard_map/ppermute | solution.py:85
  85.8 6.7 %collective-permute-done.19.refs_2_.refs_0_ = bf16[352,512]{1,0:T(8,128)(2,1)S(1)} collective-permute-done((bf16[352,512]{1,0:T(8,128)(2,1)S(1)}, bf16[352,512]{1,0:T(8,128)(2,1)S(1)}, u32[]{:S(2)}, u32[]{:S(2)}) %collective-permute-start.19) | collective-permute-done | bytes 360480 | tf_op jit(solution)/shard_map/ppermute | solution.py:85
  92.5 3.9 %accumulate.4 = (f32[1024,512]{1,0:T(8,128)S(1)}, f32[3,128,128]{2,1,0:T(8,128)S(1)}) custom-call(s32[512]{0:T(512)S(1)} %multiply_add_fusion.tick_ref, bf16[1024,4608]{1,0:T(8,128)(2,1)} %coeffs_ref.9, bf16[1024,1024]{1,0:T(8,128)(2,1)} %earlier_ref.9, bf16[352,512]{1,0:T(8,128)(2,1)S(1)} %fusion.2.refs_0_, ...), custom_call_target="tpu_custom_call" | custom-call | flops 1476395008 | bytes 2883584 | tf_op jit(solution)/shard_map/accumulate/pallas_call | solution.py:241
  96.4 4.0 %accumulate.5 = (f32[1024,512]{1,0:T(8,128)S(1)}, f32[3,128,128]{2,1,0:T(8,128)S(1)}) custom-call(s32[512]{0:T(512)S(1)} %multiply_add_fusion.tick_ref, bf16[1024,4608]{1,0:T(8,128)(2,1)} %coeffs_ref.9, bf16[1024,1024]{1,0:T(8,128)(2,1)} %earlier_ref.9, ...), custom_call_target="tpu_custom_call", output_to_operand_aliasing={{0}: (7, {}), {1}: (8, {})} | custom-call | flops 1476395008 | bytes 2883584 | tf_op jit(solution)/shard_map/accumulate/pallas_call | solution.py:241
  100.4 4.0 %accumulate.6 = (f32[1024,512]{1,0:T(8,128)S(1)}, f32[3,128,128]{2,1,0:T(8,128)S(1)}) custom-call(s32[512]{0:T(512)S(1)} %multiply_add_fusion.2.tick_ref, bf16[1024,4608]{1,0:T(8,128)(2,1)} %coeffs_ref.9, bf16[1024,1024]{1,0:T(8,128)(2,1)} %earlier_ref.9, bf16[352,512]{1,0:T(8,128)(2,1)S(1)} %choose.3.refs_0_, ...), custom_call_target="tpu_custom_call", output_to_operand_aliasing={{0}: (7, {}), {1}: (8, {})} | custom-call | flops 1476395008 | bytes 2883584 | tf_op jit(solution)/shard_map/accumulate/pallas_call | solution.py:241
  106.8 5.8 %collective-permute-done.32 = f32[3,128,128]{2,1,0:T(8,128)S(1)} collective-permute-done((f32[3,128,128]{2,1,0:T(8,128)S(1)}, f32[3,128,128]{2,1,0:T(8,128)S(1)}, u32[]{:S(2)}, u32[]{:S(2)}) %collective-permute-start.32) | collective-permute-done | bytes 196640 | tf_op jit(solution)/shard_map/ppermute | solution.py:85
  112.7 4.0 %accumulate.7.partial_ref = f32[1024,512]{1,0:T(8,128)S(1)} custom-call(s32[512]{0:T(512)S(1)} %multiply_add_fusion.2.tick_ref, bf16[1024,4608]{1,0:T(8,128)(2,1)} %coeffs_ref.9, bf16[1024,1024]{1,0:T(8,128)(2,1)} %earlier_ref.9, bf16[352,512]{1,0:T(8,128)(2,1)S(1)} %choose.2.refs_0_, ...), custom_call_target="tpu_custom_call", output_to_operand_aliasing={{}: (7, {})} | custom-call | flops 1476395008 | bytes 2883584 | tf_op jit(solution)/shard_map/accumulate/pallas_call | solution.py:241
  116.7 2.3 %recur.7 = (f32[256,256]{1,0:T(8,128)S(1)}, f32[256,256]{1,0:T(8,128)S(1)}) custom-call(f32[1024,512]{1,0:T(8,128)S(1)} %accumulate.7.partial_ref, f32[3,128,128]{2,1,0:T(8,128)S(1)} %add.24.mine_ref, f32[3,128,128]{2,1,0:T(8,128)S(1)} %collective-permute-done.33.other_ref, f32[4,128,128]{2,1,0:T(8,128)S(1)} %copy-done), custom_call_target="tpu_custom_call" | custom-call | tf_op jit(solution)/shard_map/recur/pallas_call | solution.py:427
  119.0 1.6 %collective-permute-start.37 = (f32[256,256]{1,0:T(8,128)S(1)}, f32[256,256]{1,0:T(8,128)S(1)}, u32[]{:S(2)}, u32[]{:S(2)}) collective-permute-start(f32[256,256]{1,0:T(8,128)S(1)} %get-tuple-element.64), channel_id=1, source_target_pairs={{0,1},{1,0},{2,3},{3,2},{4,5},{5,4},{6,7},{7,6},{8,9},{9,8},{10,11... | collective-permute-start | bytes 786440 | tf_op jit(solution)/shard_map/ppermute | solution.py:85
  120.6 2.3 %recur.6 = (f32[256,256]{1,0:T(8,128)S(1)}, f32[256,256]{1,0:T(8,128)S(1)}) custom-call(f32[1024,512]{1,0:T(8,128)S(1)} %accumulate.7.partial_ref, f32[3,128,128]{2,1,0:T(8,128)S(1)} %add.24.mine_ref, f32[3,128,128]{2,1,0:T(8,128)S(1)} %collective-permute-done.33.other_ref, f32[4,128,128]{2,1,0:T(8,128)S(1)} %copy-done), custom_call_target="tpu_custom_call" | custom-call | tf_op jit(solution)/shard_map/recur/pallas_call | solution.py:427
  123.5 2.3 %recur.5 = (f32[256,256]{1,0:T(8,128)S(1)}, f32[256,256]{1,0:T(8,128)S(1)}) custom-call(f32[1024,512]{1,0:T(8,128)S(1)} %accumulate.7.partial_ref, f32[3,128,128]{2,1,0:T(8,128)S(1)} %add.24.mine_ref, f32[3,128,128]{2,1,0:T(8,128)S(1)} %collective-permute-done.33.other_ref, f32[4,128,128]{2,1,0:T(8,128)S(1)} %copy-done), custom_call_target="tpu_custom_call" | custom-call | tf_op jit(solution)/shard_map/recur/pallas_call | solution.py:427
  127.4 2.3 %recur.4 = (f32[256,256]{1,0:T(8,128)S(1)}, f32[256,256]{1,0:T(8,128)S(1)}) custom-call(f32[1024,512]{1,0:T(8,128)S(1)} %accumulate.7.partial_ref, f32[3,128,128]{2,1,0:T(8,128)S(1)} %add.24.mine_ref, f32[3,128,128]{2,1,0:T(8,128)S(1)} %collective-permute-done.33.other_ref, f32[4,128,128]{2,1,0:T(8,128)S(1)} %copy-done), custom_call_target="tpu_custom_call" | custom-call | tf_op jit(solution)/shard_map/recur/pallas_call | solution.py:427
  131.0 2.9 %collective-permute-done.36.taken_ref = f32[256,256]{1,0:T(8,128)S(1)} collective-permute-done((f32[256,256]{1,0:T(8,128)S(1)}, f32[256,256]{1,0:T(8,128)S(1)}, u32[]{:S(2)}, u32[]{:S(2)}) %collective-permute-start.36) | collective-permute-done | bytes 262176 | tf_op jit(solution)/shard_map/ppermute | solution.py:85
  134.6 4.9 %collective-permute-done.35.taken_ref = f32[256,256]{1,0:T(8,128)S(1)} collective-permute-done((f32[256,256]{1,0:T(8,128)S(1)}, f32[256,256]{1,0:T(8,128)S(1)}, u32[]{:S(2)}, u32[]{:S(2)}) %collective-permute-start.35) | collective-permute-done | bytes 262176 | tf_op jit(solution)/shard_map/ppermute | solution.py:85
  140.2 4.4 %collective-permute-done.34.taken_ref = f32[256,256]{1,0:T(8,128)S(1)} collective-permute-done((f32[256,256]{1,0:T(8,128)S(1)}, f32[256,256]{1,0:T(8,128)S(1)}, u32[]{:S(2)}, u32[]{:S(2)}) %collective-permute-start.34) | collective-permute-done | bytes 262176 | tf_op jit(solution)/shard_map/ppermute | solution.py:85
  (90 shorter events, 22.3 us)
Async XLA Ops:
  6.6 7.5 %collective-permute-start.1 = (bf16[96,352]{1,0:T(8,128)(2,1)S(1)}, bf16[96,352]{1,0:T(8,128)(2,1)S(1)}, u32[]{:S(2)}, u32[]{:S(2)}) collective-permute-start(bf16[96,352]{1,0:T(8,128)(2,1)S(1)} %get-tuple-element.37), channel_id=1, source_target_pairs={{0,4},{2,6},{4,0},{6,2},{8,12},{10,14},{12,8},{14,10},{16,20},{18,... | collective-permute-start | bytes 202760 | tf_op jit(solution)/shard_map/ppermute | solution.py:85
  9.2 7.8 %collective-permute-start.3 = (bf16[96,352]{1,0:T(8,128)(2,1)S(1)}, bf16[96,352]{1,0:T(8,128)(2,1)S(1)}, u32[]{:S(2)}, u32[]{:S(2)}) collective-permute-start(bf16[96,352]{1,0:T(8,128)(2,1)S(1)} %get-tuple-element.39), channel_id=1, source_target_pairs={{0,8},{2,10},{4,12},{6,14},{8,0},{10,2},{12,4},{14,6},{16,24},{18,... | collective-permute-start | bytes 202760 | tf_op jit(solution)/shard_map/ppermute | solution.py:85
  11.3 9.4 %collective-permute-start.5 = (bf16[96,352]{1,0:T(8,128)(2,1)S(1)}, bf16[96,352]{1,0:T(8,128)(2,1)S(1)}, u32[]{:S(2)}, u32[]{:S(2)}) collective-permute-start(bf16[96,352]{1,0:T(8,128)(2,1)S(1)} %get-tuple-element.41), channel_id=1, source_target_pairs={{0,12},{2,14},{4,8},{6,10},{8,4},{10,6},{12,0},{14,2},{16,28},{18,... | collective-permute-start | bytes 202760 | tf_op jit(solution)/shard_map/ppermute | solution.py:85
  14.1 7.2 %collective-permute-start.6 = (bf16[96,352]{1,0:T(8,128)(2,1)S(1)}, bf16[96,352]{1,0:T(8,128)(2,1)S(1)}, u32[]{:S(2)}, u32[]{:S(2)}) collective-permute-start(bf16[96,352]{1,0:T(8,128)(2,1)S(1)} %get-tuple-element.42), channel_id=1, source_target_pairs={{0,14},{2,12},{4,10},{6,8},{8,6},{10,4},{12,2},{14,0},{16,30},{18,... | collective-permute-start | bytes 202760 | tf_op jit(solution)/shard_map/ppermute | solution.py:85
  14.2 10.3 %collective-permute-start.7 = (bf16[96,352]{1,0:T(8,128)(2,1)S(1)}, bf16[96,352]{1,0:T(8,128)(2,1)S(1)}, u32[]{:S(2)}, u32[]{:S(2)}) collective-permute-start(bf16[96,352]{1,0:T(8,128)(2,1)S(1)} %get-tuple-element.43), channel_id=1, source_target_pairs={{0,16},{2,18},{4,20},{6,22},{8,24},{10,26},{12,28},{14,30},{16,0},... | collective-permute-start | bytes 202760 | tf_op jit(solution)/shard_map/ppermute | solution.py:85
  17.0 13.1 %collective-permute-start.8 = (bf16[96,352]{1,0:T(8,128)(2,1)S(1)}, bf16[96,352]{1,0:T(8,128)(2,1)S(1)}, u32[]{:S(2)}, u32[]{:S(2)}) collective-permute-start(bf16[96,352]{1,0:T(8,128)(2,1)S(1)} %get-tuple-element.44), channel_id=1, source_target_pairs={{0,18},{2,16},{4,22},{6,20},{8,26},{10,24},{12,30},{14,28},{16,2},... | collective-permute-start | bytes 202760 | tf_op jit(solution)/shard_map/ppermute | solution.py:85
  17.9 15.8 %collective-permute-start.9 = (bf16[96,352]{1,0:T(8,128)(2,1)S(1)}, bf16[96,352]{1,0:T(8,128)(2,1)S(1)}, u32[]{:S(2)}, u32[]{:S(2)}) collective-permute-start(bf16[96,352]{1,0:T(8,128)(2,1)S(1)} %get-tuple-element.45), channel_id=1, source_target_pairs={{0,20},{2,22},{4,16},{6,18},{8,28},{10,30},{12,24},{14,26},{16,4},... | collective-permute-start | bytes 202760 | tf_op jit(solution)/shard_map/ppermute | solution.py:85
  20.8 15.5 %collective-permute-start.10 = (bf16[96,352]{1,0:T(8,128)(2,1)S(1)}, bf16[96,352]{1,0:T(8,128)(2,1)S(1)}, u32[]{:S(2)}, u32[]{:S(2)}) collective-permute-start(bf16[96,352]{1,0:T(8,128)(2,1)S(1)} %get-tuple-element.46), channel_id=1, source_target_pairs={{0,22},{2,20},{4,18},{6,16},{8,30},{10,28},{12,26},{14,24},{16,6},... | collective-permute-start | bytes 202760 | tf_op jit(solution)/shard_map/ppermute | solution.py:85
  21.3 15.0 %collective-permute-start.11 = (bf16[96,352]{1,0:T(8,128)(2,1)S(1)}, bf16[96,352]{1,0:T(8,128)(2,1)S(1)}, u32[]{:S(2)}, u32[]{:S(2)}) collective-permute-start(bf16[96,352]{1,0:T(8,128)(2,1)S(1)} %get-tuple-element.47), channel_id=1, source_target_pairs={{0,24},{2,26},{4,28},{6,30},{8,16},{10,18},{12,20},{14,22},{16,8},... | collective-permute-start | bytes 202760 | tf_op jit(solution)/shard_map/ppermute | solution.py:85
  24.6 11.8 %collective-permute-start.12 = (bf16[96,352]{1,0:T(8,128)(2,1)S(1)}, bf16[96,352]{1,0:T(8,128)(2,1)S(1)}, u32[]{:S(2)}, u32[]{:S(2)}) collective-permute-start(bf16[96,352]{1,0:T(8,128)(2,1)S(1)} %get-tuple-element.48), channel_id=1, source_target_pairs={{0,26},{2,24},{4,30},{6,28},{8,18},{10,16},{12,22},{14,20},{16,10}... | collective-permute-start | bytes 202760 | tf_op jit(solution)/shard_map/ppermute | solution.py:85
  30.1 7.2 %collective-permute-start.13 = (bf16[96,352]{1,0:T(8,128)(2,1)S(1)}, bf16[96,352]{1,0:T(8,128)(2,1)S(1)}, u32[]{:S(2)}, u32[]{:S(2)}) collective-permute-start(bf16[96,352]{1,0:T(8,128)(2,1)S(1)} %get-tuple-element.49), channel_id=1, source_target_pairs={{0,28},{2,30},{4,24},{6,26},{8,20},{10,22},{12,16},{14,18},{16,12}... | collective-permute-start | bytes 202760 | tf_op jit(solution)/shard_map/ppermute | solution.py:85
  41.8 13.8 %collective-permute-start.15 = (bf16[352,512]{1,0:T(8,128)(2,1)S(1)}, bf16[352,512]{1,0:T(8,128)(2,1)S(1)}, u32[]{:S(2)}, u32[]{:S(2)}) collective-permute-start(bf16[352,512]{1,0:T(8,128)(2,1)S(1)} %fusion.2.refs_0_), channel_id=1, source_target_pairs={{0,8},{2,10},{4,12},{6,14},{8,0},{10,2},{12,4},{14,6},{16,24},{18,... | collective-permute-start | bytes 1081352 | tf_op jit(solution)/shard_map/ppermute | solution.py:85
  46.9 10.0 %collective-permute-start.21 = (bf16[352,512]{1,0:T(8,128)(2,1)S(1)}, bf16[352,512]{1,0:T(8,128)(2,1)S(1)}, u32[]{:S(2)}, u32[]{:S(2)}) collective-permute-start(bf16[352,512]{1,0:T(8,128)(2,1)S(1)} %fusion.2.refs_0_), channel_id=1, source_target_pairs={{8,16},{10,18},{12,20},{14,22},{16,8},{18,10},{20,12},{22,14},{9,1... | collective-permute-start | bytes 1081352 | tf_op jit(solution)/shard_map/ppermute | solution.py:500
  56.3 9.9 %collective-permute-start.30 = (bf16[352,512]{1,0:T(8,128)(2,1)S(1)}, bf16[352,512]{1,0:T(8,128)(2,1)S(1)}, u32[]{:S(2)}, u32[]{:S(2)}) collective-permute-start(bf16[352,512]{1,0:T(8,128)(2,1)S(1)} %fusion.2.refs_0_), channel_id=1, source_target_pairs={{0,4},{2,6},{4,0},{6,2},{8,12},{10,14},{12,8},{14,10},{16,20},{18,... | collective-permute-start | bytes 1081352 | tf_op jit(solution)/shard_map/ppermute | solution.py:85
  56.9 14.3 %collective-permute-start.22 = (bf16[352,512]{1,0:T(8,128)(2,1)S(1)}, bf16[352,512]{1,0:T(8,128)(2,1)S(1)}, u32[]{:S(2)}, u32[]{:S(2)}) collective-permute-start(bf16[352,512]{1,0:T(8,128)(2,1)S(1)} %collective-permute-done.21.refs_0_), channel_id=1, source_target_pairs={{8,0},{10,2},{12,4},{14,6},{16,24},{18,26},{20,28},{22,30},{9,1},{... | collective-permute-start | bytes 1081352 | tf_op jit(solution)/shard_map/ppermute | solution.py:504
  58.2 19.8 %collective-permute-start.17 = (bf16[352,512]{1,0:T(8,128)(2,1)S(1)}, bf16[352,512]{1,0:T(8,128)(2,1)S(1)}, u32[]{:S(2)}, u32[]{:S(2)}) collective-permute-start(bf16[352,512]{1,0:T(8,128)(2,1)S(1)} %collective-permute-done.16.refs_0_), channel_id=1, source_target_pairs={{8,0},{10,2},{12,4},{14,6},{16,24},{18,26},{20,28},{22,30},{9,1},{... | collective-permute-start | bytes 1081352 | tf_op jit(solution)/shard_map/ppermute | solution.py:504
  59.5 18.6 %collective-permute-start.29 = (bf16[352,512]{1,0:T(8,128)(2,1)S(1)}, bf16[352,512]{1,0:T(8,128)(2,1)S(1)}, u32[]{:S(2)}, u32[]{:S(2)}) collective-permute-start(bf16[352,512]{1,0:T(8,128)(2,1)S(1)} %fusion.2.refs_0_), channel_id=1, source_target_pairs={{0,2},{2,0},{4,6},{6,4},{8,10},{10,8},{12,14},{14,12},{16,18},{18,... | collective-permute-start | bytes 1081352 | tf_op jit(solution)/shard_map/ppermute | solution.py:85
  66.2 13.1 %collective-permute-start.31 = (bf16[352,512]{1,0:T(8,128)(2,1)S(1)}, bf16[352,512]{1,0:T(8,128)(2,1)S(1)}, u32[]{:S(2)}, u32[]{:S(2)}) collective-permute-start(bf16[352,512]{1,0:T(8,128)(2,1)S(1)} %collective-permute-done.30.refs_2_), channel_id=1, source_target_pairs={{0,2},{2,0},{4,6},{6,4},{8,10},{10,8},{12,14},{14,12},{16,18},{18,... | collective-permute-start | bytes 1081352 | tf_op jit(solution)/shard_map/ppermute | solution.py:85
  66.2 13.3 %collective-permute-start.27 = (bf16[352,512]{1,0:T(8,128)(2,1)S(1)}, bf16[352,512]{1,0:T(8,128)(2,1)S(1)}, u32[]{:S(2)}, u32[]{:S(2)}) collective-permute-start(bf16[352,512]{1,0:T(8,128)(2,1)S(1)} %collective-permute-done.15.refs_0_), channel_id=1, source_target_pairs={{0,4},{2,6},{4,0},{6,2},{8,12},{10,14},{12,8},{14,10},{16,20},{18,... | collective-permute-start | bytes 1081352 | tf_op jit(solution)/shard_map/ppermute | solution.py:85
  71.2 14.0 %collective-permute-start.24 = (bf16[352,512]{1,0:T(8,128)(2,1)S(1)}, bf16[352,512]{1,0:T(8,128)(2,1)S(1)}, u32[]{:S(2)}, u32[]{:S(2)}) collective-permute-start(bf16[352,512]{1,0:T(8,128)(2,1)S(1)} %choose.3.refs_0_), channel_id=1, source_target_pairs={{0,4},{2,6},{4,0},{6,2},{8,12},{10,14},{12,8},{14,10},{16,20},{18,... | collective-permute-start | bytes 1081352 | tf_op jit(solution)/shard_map/ppermute | solution.py:85
  78.0 7.3 %collective-permute-start.26 = (bf16[352,512]{1,0:T(8,128)(2,1)S(1)}, bf16[352,512]{1,0:T(8,128)(2,1)S(1)}, u32[]{:S(2)}, u32[]{:S(2)}) collective-permute-start(bf16[352,512]{1,0:T(8,128)(2,1)S(1)} %collective-permute-done.15.refs_0_), channel_id=1, source_target_pairs={{0,2},{2,0},{4,6},{6,4},{8,10},{10,8},{12,14},{14,12},{16,18},{18,... | collective-permute-start | bytes 1081352 | tf_op jit(solution)/shard_map/ppermute | solution.py:85
  78.0 14.5 %collective-permute-start.19 = (bf16[352,512]{1,0:T(8,128)(2,1)S(1)}, bf16[352,512]{1,0:T(8,128)(2,1)S(1)}, u32[]{:S(2)}, u32[]{:S(2)}) collective-permute-start(bf16[352,512]{1,0:T(8,128)(2,1)S(1)} %choose.2.refs_0_), channel_id=1, source_target_pairs={{0,4},{2,6},{4,0},{6,2},{8,12},{10,14},{12,8},{14,10},{16,20},{18,... | collective-permute-start | bytes 1081352 | tf_op jit(solution)/shard_map/ppermute | solution.py:85
  79.3 21.1 %collective-permute-start.23 = (bf16[352,512]{1,0:T(8,128)(2,1)S(1)}, bf16[352,512]{1,0:T(8,128)(2,1)S(1)}, u32[]{:S(2)}, u32[]{:S(2)}) collective-permute-start(bf16[352,512]{1,0:T(8,128)(2,1)S(1)} %choose.3.refs_0_), channel_id=1, source_target_pairs={{0,2},{2,0},{4,6},{6,4},{8,10},{10,8},{12,14},{14,12},{16,18},{18,... | collective-permute-start | bytes 1081352 | tf_op jit(solution)/shard_map/ppermute | solution.py:85
  79.5 16.9 %collective-permute-start.28 = (bf16[352,512]{1,0:T(8,128)(2,1)S(1)}, bf16[352,512]{1,0:T(8,128)(2,1)S(1)}, u32[]{:S(2)}, u32[]{:S(2)}) collective-permute-start(bf16[352,512]{1,0:T(8,128)(2,1)S(1)} %collective-permute-done.27.refs_2_), channel_id=1, source_target_pairs={{0,2},{2,0},{4,6},{6,4},{8,10},{10,8},{12,14},{14,12},{16,18},{18,... | collective-permute-start | bytes 1081352 | tf_op jit(solution)/shard_map/ppermute | solution.py:85
  85.2 15.2 %collective-permute-start.25 = (bf16[352,512]{1,0:T(8,128)(2,1)S(1)}, bf16[352,512]{1,0:T(8,128)(2,1)S(1)}, u32[]{:S(2)}, u32[]{:S(2)}) collective-permute-start(bf16[352,512]{1,0:T(8,128)(2,1)S(1)} %collective-permute-done.24.refs_2_), channel_id=1, source_target_pairs={{0,2},{2,0},{4,6},{6,4},{8,10},{10,8},{12,14},{14,12},{16,18},{18,... | collective-permute-start | bytes 1081352 | tf_op jit(solution)/shard_map/ppermute | solution.py:85
  85.3 19.1 %collective-permute-start.18 = (bf16[352,512]{1,0:T(8,128)(2,1)S(1)}, bf16[352,512]{1,0:T(8,128)(2,1)S(1)}, u32[]{:S(2)}, u32[]{:S(2)}) collective-permute-start(bf16[352,512]{1,0:T(8,128)(2,1)S(1)} %choose.2.refs_0_), channel_id=1, source_target_pairs={{0,2},{2,0},{4,6},{6,4},{8,10},{10,8},{12,14},{14,12},{16,18},{18,... | collective-permute-start | bytes 1081352 | tf_op jit(solution)/shard_map/ppermute | solution.py:85
  92.5 12.3 %collective-permute-start.20 = (bf16[352,512]{1,0:T(8,128)(2,1)S(1)}, bf16[352,512]{1,0:T(8,128)(2,1)S(1)}, u32[]{:S(2)}, u32[]{:S(2)}) collective-permute-start(bf16[352,512]{1,0:T(8,128)(2,1)S(1)} %collective-permute-done.19.refs_2_.refs_0_), channel_id=1, source_target_pairs={{0,2},{2,0},{4,6},{6,4},{8,10},{10,8},{12,14},{14,12},{16,18},{18,... | collective-permute-start | bytes 1081352 | tf_op jit(solution)/shard_map/ppermute | solution.py:85
  105.3 7.3 %collective-permute-start.32 = (f32[3,128,128]{2,1,0:T(8,128)S(1)}, f32[3,128,128]{2,1,0:T(8,128)S(1)}, u32[]{:S(2)}, u32[]{:S(2)}) collective-permute-start(f32[3,128,128]{2,1,0:T(8,128)S(1)} %lower.3), channel_id=1, source_target_pairs={{0,1},{1,0},{2,3},{3,2},{4,5},{5,4},{6,7},{7,6},{8,9},{9,8},{10,11... | collective-permute-start | bytes 589832 | tf_op jit(solution)/shard_map/ppermute | solution.py:85
  119.0 11.3 %collective-permute-start.37 = (f32[256,256]{1,0:T(8,128)S(1)}, f32[256,256]{1,0:T(8,128)S(1)}, u32[]{:S(2)}, u32[]{:S(2)}) collective-permute-start(f32[256,256]{1,0:T(8,128)S(1)} %get-tuple-element.64), channel_id=1, source_target_pairs={{0,1},{1,0},{2,3},{3,2},{4,5},{5,4},{6,7},{7,6},{8,9},{9,8},{10,11... | collective-permute-start | bytes 786440 | tf_op jit(solution)/shard_map/ppermute | solution.py:85
  122.9 11.0 %collective-permute-start.36 = (f32[256,256]{1,0:T(8,128)S(1)}, f32[256,256]{1,0:T(8,128)S(1)}, u32[]{:S(2)}, u32[]{:S(2)}) collective-permute-start(f32[256,256]{1,0:T(8,128)S(1)} %get-tuple-element.62), channel_id=1, source_target_pairs={{0,1},{1,0},{2,3},{3,2},{4,5},{5,4},{6,7},{7,6},{8,9},{9,8},{10,11... | collective-permute-start | bytes 786440 | tf_op jit(solution)/shard_map/ppermute | solution.py:85
  125.8 13.7 %collective-permute-start.35 = (f32[256,256]{1,0:T(8,128)S(1)}, f32[256,256]{1,0:T(8,128)S(1)}, u32[]{:S(2)}, u32[]{:S(2)}) collective-permute-start(f32[256,256]{1,0:T(8,128)S(1)} %get-tuple-element.60), channel_id=1, source_target_pairs={{0,1},{1,0},{2,3},{3,2},{4,5},{5,4},{6,7},{7,6},{8,9},{9,8},{10,11... | collective-permute-start | bytes 786440 | tf_op jit(solution)/shard_map/ppermute | solution.py:85
  129.7 14.9 %collective-permute-start.34 = (f32[256,256]{1,0:T(8,128)S(1)}, f32[256,256]{1,0:T(8,128)S(1)}, u32[]{:S(2)}, u32[]{:S(2)}) collective-permute-start(f32[256,256]{1,0:T(8,128)S(1)} %get-tuple-element.58), channel_id=1, source_target_pairs={{0,1},{1,0},{2,3},{3,2},{4,5},{5,4},{6,7},{7,6},{8,9},{9,8},{10,11... | collective-permute-start | bytes 786440 | tf_op jit(solution)/shard_map/ppermute | solution.py:85
  (9 other events, 88.7 us)

commit v5 on v4

--- a/solution.py
+++ b/solution.py
@@ -465,6 +465,7 @@
     lines = size // GROUP
     me = lax.axis_index("wide")
     panel = piv_local.shape[0]
+    block = inv_tiles.shape[1]
     blocks = inv_tiles.shape[0]
     capacity = 3 * panel // size
     widths = [source.shape[1] // size for source in (coeffs, earlier)]
@@ -521,15 +522,16 @@
         corner = exchange(across, "wide", 1, size)
         groups.append([piece, beside, across, corner])
     ticks = {hop: tick(owners if hop % 2 else piv_local, hop) for hop in range(1, lines - 1)}
+    pairs = len(lower_pairs(blocks)[0])
+    mine = jnp.zeros((pairs, block, block), jnp.float32)
+    mine = lower_only(blocks, edge, tuple(range(GROUP)), mine, groups[0])
+    steps = (("narrow", 1), ("wide", 2 * GROUP), ("wide", GROUP))
+    for axis, bit in steps:
+        mine = mine + exchange(mine, axis, bit, lax.axis_size(axis))
     state = None
     for index, (source, group) in enumerate(zip(sources, groups)):
-        final = index == lines - 1
-        if final:
-            mine = lower_only(blocks, edge, (0, 1), state[1], group[:2])
-            mine = lower_only(blocks, edge, (2, 3), mine, group[2:])
         ticked = ticks[min(max(index, 1), lines - 2)]
-        state = accumulate(source, blocks, ticked, coeffs, earlier, group, state, final)
-    mine = mine + exchange(mine, "narrow", 1, 2)
+        state = accumulate(source, blocks, ticked, coeffs, earlier, group, state, True)
     other = exchange(mine, "wide", 1, size)
     result = None
     for index in range(SENDS):

time: 147 us -> 134 us (0.912); the launches traced: 145 us -> 134 us
  waiting for transfers between devices: 60.3 us -> 46 us
  starting transfers between devices: 48.3 us -> 51.2 us
    ppermute x34 -> x36, waiting for transfers between devices: 50.6 us -> 33.4 us  [exchange(): return lax.ppermute(value, axis, [(i, i ^ bit) for i in range(size)])]
    ppermute x2, waiting for transfers between devices: 9.67 us -> 12.6 us  [send_out(): return lax.ppermute(value, 'wide', pairs)]
    ppermute x34 -> x36, starting transfers between devices: 44.4 us -> 47.3 us  [exchange(): return lax.ppermute(value, axis, [(i, i ^ bit) for i in range(size)])]
  transfers between devices with their start and end apart: 38 -> 40, of which waited for: 14 -> 14; matrix products, arithmetic and copies ran while one was open for 0% -> 0% of each run, Pallas kernels for 17% -> 19%
where the time goes in v5:
time: 134 us
  starting transfers between devices  51.2 us (38%)
  waiting for transfers between devices  46 us (34%)
  Pallas kernels  34.1 us (25%)
    ppermute x36, starting transfers between devices, exchange(): return lax.ppermute(value, axis, [(i, i ^ bit) for i in range(size)])  47.3 us
    ppermute x36, waiting for transfers between devices, exchange(): return lax.ppermute(value, axis, [(i, i ^ bit) for i in range(size)])  33.4 us
    pallas_call x4, Pallas kernels, accumulate(): pl.pallas_call(functools.partial(accumulate_kernel, table, blocks, fresh,...  15.8 us
    ppermute x2, waiting for transfers between devices, send_out(): return lax.ppermute(value, 'wide', pairs)  12.6 us
    pallas_call x4, Pallas kernels, recur(): pl.pallas_call(functools.partial(recur_kernel, blocks), grid=(1,), in_spe...  9.2 us
    pallas_call x1, Pallas kernels, cut(): pl.pallas_call(functools.partial(cut_kernel, hops, lines), in_specs=[vmem...  5.34 us
    pallas_call x4, Pallas kernels, finish(): pl.pallas_call(finish_kernel, grid=(1,), in_specs=[vmem, vmem] + [anywher...  2.92 us
  transfers between devices with their start and end apart: 40, of which 14 were waited for; matrix products, arithmetic and copies ran while one was open for 0% of the time, Pallas kernels for 19%

profile of v5, /device:TPU:0, one launch (start us, length us, event | category | flops | bytes accessed | tf_op | source)
XLA Modules:
  0.0 134.0 jit_solution(9687323252083675022)
XLA Ops:
  0.7 5.3 %cut.1 = (bf16[96,352]{1,0:T(8,128)(2,1)S(1)}, bf16[96,352]{1,0:T(8,128)(2,1)S(1)}, bf16[96,352]{1,0:T(8,128)(2,1)S(1)}, bf16[96,352]{1,0:T(8,128)(2,1)S(1)}, bf...) custom-call(s32[2,512]{1,0:T(2,128)S(1)} %pad_add_fusion.pivot_ref, ...), custom_call_target="tpu_custom_call" | custom-call | tf_op jit(solution)/shard_map/cut/pallas_call | solution.py:318
  6.6 2.6 %collective-permute-start.1 = (bf16[96,352]{1,0:T(8,128)(2,1)S(1)}, bf16[96,352]{1,0:T(8,128)(2,1)S(1)}, u32[]{:S(2)}, u32[]{:S(2)}) collective-permute-start(bf16[96,352]{1,0:T(8,128)(2,1)S(1)} %get-tuple-element.31), channel_id=1, source_target_pairs={{0,4},{2,6},{4,0},{6,2},{8,12},{10,14},{12,8},{14,10},{16,20},{18,... | collective-permute-start | bytes 202760 | tf_op jit(solution)/shard_map/ppermute | solution.py:85
  9.2 1.8 %collective-permute-start.3 = (bf16[96,352]{1,0:T(8,128)(2,1)S(1)}, bf16[96,352]{1,0:T(8,128)(2,1)S(1)}, u32[]{:S(2)}, u32[]{:S(2)}) collective-permute-start(bf16[96,352]{1,0:T(8,128)(2,1)S(1)} %get-tuple-element.33), channel_id=1, source_target_pairs={{0,8},{2,10},{4,12},{6,14},{8,0},{10,2},{12,4},{14,6},{16,24},{18,... | collective-permute-start | bytes 202760 | tf_op jit(solution)/shard_map/ppermute | solution.py:85
  11.3 2.7 %collective-permute-start.5 = (bf16[96,352]{1,0:T(8,128)(2,1)S(1)}, bf16[96,352]{1,0:T(8,128)(2,1)S(1)}, u32[]{:S(2)}, u32[]{:S(2)}) collective-permute-start(bf16[96,352]{1,0:T(8,128)(2,1)S(1)} %get-tuple-element.35), channel_id=1, source_target_pairs={{0,12},{2,14},{4,8},{6,10},{8,4},{10,6},{12,0},{14,2},{16,28},{18,... | collective-permute-start | bytes 202760 | tf_op jit(solution)/shard_map/ppermute | solution.py:85
  14.2 2.7 %collective-permute-start.7 = (bf16[96,352]{1,0:T(8,128)(2,1)S(1)}, bf16[96,352]{1,0:T(8,128)(2,1)S(1)}, u32[]{:S(2)}, u32[]{:S(2)}) collective-permute-start(bf16[96,352]{1,0:T(8,128)(2,1)S(1)} %get-tuple-element.37), channel_id=1, source_target_pairs={{0,16},{2,18},{4,20},{6,22},{8,24},{10,26},{12,28},{14,30},{16,0},... | collective-permute-start | bytes 202760 | tf_op jit(solution)/shard_map/ppermute | solution.py:85
  17.9 2.8 %collective-permute-start.9 = (bf16[96,352]{1,0:T(8,128)(2,1)S(1)}, bf16[96,352]{1,0:T(8,128)(2,1)S(1)}, u32[]{:S(2)}, u32[]{:S(2)}) collective-permute-start(bf16[96,352]{1,0:T(8,128)(2,1)S(1)} %get-tuple-element.39), channel_id=1, source_target_pairs={{0,20},{2,22},{4,16},{6,18},{8,28},{10,30},{12,24},{14,26},{16,4},... | collective-permute-start | bytes 202760 | tf_op jit(solution)/shard_map/ppermute | solution.py:85
  21.3 3.2 %collective-permute-start.11 = (bf16[96,352]{1,0:T(8,128)(2,1)S(1)}, bf16[96,352]{1,0:T(8,128)(2,1)S(1)}, u32[]{:S(2)}, u32[]{:S(2)}) collective-permute-start(bf16[96,352]{1,0:T(8,128)(2,1)S(1)} %get-tuple-element.41), channel_id=1, source_target_pairs={{0,24},{2,26},{4,28},{6,30},{8,16},{10,18},{12,20},{14,22},{16,8},... | collective-permute-start | bytes 202760 | tf_op jit(solution)/shard_map/ppermute | solution.py:85
  24.6 4.3 %collective-permute-start.12 = (bf16[96,352]{1,0:T(8,128)(2,1)S(1)}, bf16[96,352]{1,0:T(8,128)(2,1)S(1)}, u32[]{:S(2)}, u32[]{:S(2)}) collective-permute-start(bf16[96,352]{1,0:T(8,128)(2,1)S(1)} %get-tuple-element.42), channel_id=1, source_target_pairs={{0,26},{2,24},{4,30},{6,28},{8,18},{10,16},{12,22},{14,20},{16,10}... | collective-permute-start | bytes 202760 | tf_op jit(solution)/shard_map/ppermute | solution.py:85
  30.1 3.4 %collective-permute-start.13 = (bf16[96,352]{1,0:T(8,128)(2,1)S(1)}, bf16[96,352]{1,0:T(8,128)(2,1)S(1)}, u32[]{:S(2)}, u32[]{:S(2)}) collective-permute-start(bf16[96,352]{1,0:T(8,128)(2,1)S(1)} %get-tuple-element.43), channel_id=1, source_target_pairs={{0,28},{2,30},{4,24},{6,26},{8,20},{10,22},{12,16},{14,18},{16,12}... | collective-permute-start | bytes 202760 | tf_op jit(solution)/shard_map/ppermute | solution.py:85
  33.7 2.6 %collective-permute-start.14 = (bf16[96,352]{1,0:T(8,128)(2,1)S(1)}, bf16[96,352]{1,0:T(8,128)(2,1)S(1)}, u32[]{:S(2)}, u32[]{:S(2)}) collective-permute-start(bf16[96,352]{1,0:T(8,128)(2,1)S(1)} %get-tuple-element.44), channel_id=1, source_target_pairs={{0,30},{2,28},{4,26},{6,24},{8,22},{10,20},{12,18},{14,16},{16,14}... | collective-permute-start | bytes 202760 | tf_op jit(solution)/shard_map/ppermute | solution.py:85
  37.3 3.5 %collective-permute-done.14 = bf16[96,352]{1,0:T(8,128)(2,1)S(1)} collective-permute-done((bf16[96,352]{1,0:T(8,128)(2,1)S(1)}, bf16[96,352]{1,0:T(8,128)(2,1)S(1)}, u32[]{:S(2)}, u32[]{:S(2)}) %collective-permute-start.14) | collective-permute-done | bytes 67616 | tf_op jit(solution)/shard_map/ppermute | solution.py:85
  41.8 5.1 %collective-permute-start.15 = (bf16[352,512]{1,0:T(8,128)(2,1)S(1)}, bf16[352,512]{1,0:T(8,128)(2,1)S(1)}, u32[]{:S(2)}, u32[]{:S(2)}) collective-permute-start(bf16[352,512]{1,0:T(8,128)(2,1)S(1)} %fusion.2.refs_0_), channel_id=1, source_target_pairs={{0,8},{2,10},{4,12},{6,14},{8,0},{10,2},{12,4},{14,6},{16,24},{18,... | collective-permute-start | bytes 1081352 | tf_op jit(solution)/shard_map/ppermute | solution.py:85
  48.1 7.5 %collective-permute-done.15.refs_0_ = bf16[352,512]{1,0:T(8,128)(2,1)S(1)} collective-permute-done((bf16[352,512]{1,0:T(8,128)(2,1)S(1)}, bf16[352,512]{1,0:T(8,128)(2,1)S(1)}, u32[]{:S(2)}, u32[]{:S(2)}) %collective-permute-start.15) | collective-permute-done | bytes 360480 | tf_op jit(solution)/shard_map/ppermute | solution.py:85
  60.9 1.6 %collective-permute-start.32 = (f32[3,128,128]{2,1,0:T(8,128)S(1)}, f32[3,128,128]{2,1,0:T(8,128)S(1)}, u32[]{:S(2)}, u32[]{:S(2)}) collective-permute-start(f32[3,128,128]{2,1,0:T(8,128)S(1)} %lower.1), channel_id=1, source_target_pairs={{0,1},{1,0},{2,3},{3,2},{4,5},{5,4},{6,7},{7,6},{8,9},{9,8},{10,11... | collective-permute-start | bytes 589832 | tf_op jit(solution)/shard_map/ppermute | solution.py:85
  62.5 9.4 %collective-permute-done.22.refs_1_ = bf16[352,512]{1,0:T(8,128)(2,1)S(1)} collective-permute-done((bf16[352,512]{1,0:T(8,128)(2,1)S(1)}, bf16[352,512]{1,0:T(8,128)(2,1)S(1)}, u32[]{:S(2)}, u32[]{:S(2)}) %collective-permute-start.22) | collective-permute-done | bytes 360480 | tf_op jit(solution)/shard_map/ppermute | solution.py:505
  73.1 4.5 %collective-permute-start.33 = (f32[3,128,128]{2,1,0:T(8,128)S(1)}, f32[3,128,128]{2,1,0:T(8,128)S(1)}, u32[]{:S(2)}, u32[]{:S(2)}) collective-permute-start(f32[3,128,128]{2,1,0:T(8,128)S(1)} %add.30), channel_id=1, source_target_pairs={{0,16},{2,18},{4,20},{6,22},{8,24},{10,26},{12,28},{14,30},{16,0},... | collective-permute-start | bytes 589832 | tf_op jit(solution)/shard_map/ppermute | solution.py:85
  77.6 3.2 %collective-permute-done.17.refs_1_ = bf16[352,512]{1,0:T(8,128)(2,1)S(1)} collective-permute-done((bf16[352,512]{1,0:T(8,128)(2,1)S(1)}, bf16[352,512]{1,0:T(8,128)(2,1)S(1)}, u32[]{:S(2)}, u32[]{:S(2)}) %collective-permute-start.17) | collective-permute-done | bytes 360480 | tf_op jit(solution)/shard_map/ppermute | solution.py:505
  81.2 3.9 %collective-permute-done.33 = f32[3,128,128]{2,1,0:T(8,128)S(1)} collective-permute-done((f32[3,128,128]{2,1,0:T(8,128)S(1)}, f32[3,128,128]{2,1,0:T(8,128)S(1)}, u32[]{:S(2)}, u32[]{:S(2)}) %collective-permute-start.33) | collective-permute-done | bytes 196640 | tf_op jit(solution)/shard_map/ppermute | solution.py:85
  85.8 3.6 %collective-permute-done.19.refs_2_ = bf16[352,512]{1,0:T(8,128)(2,1)S(1)} collective-permute-done((bf16[352,512]{1,0:T(8,128)(2,1)S(1)}, bf16[352,512]{1,0:T(8,128)(2,1)S(1)}, u32[]{:S(2)}, u32[]{:S(2)}) %collective-permute-start.19) | collective-permute-done | bytes 360480 | tf_op jit(solution)/shard_map/ppermute | solution.py:85
  89.3 3.9 %accumulate.4.refs_4_ = f32[1024,512]{1,0:T(8,128)S(1)} custom-call(s32[512]{0:T(512)S(1)} %multiply_add_fusion.tick_ref, bf16[1024,4608]{1,0:T(8,128)(2,1)} %coeffs_ref.9, bf16[1024,1024]{1,0:T(8,128)(2,1)} %earlier_ref.9, bf16[352,512]{1,0:T(8,128)(2,1)S(1)} %fusion.2.refs_0_, bf16[352,512]{1,0:T(8,128)(2,1)S(1)} %collective-permute-done.29.refs_1_, ...), custom_call_target="tpu_custom_call" | custom-call | flops 1476395008 | bytes 2883584 | tf_op jit(solution)/shard_map/accumulate/pallas_call | solution.py:241
  93.3 4.0 %accumulate.5.refs_4_ = f32[1024,512]{1,0:T(8,128)S(1)} custom-call(s32[512]{0:T(512)S(1)} %multiply_add_fusion.tick_ref, bf16[1024,4608]{1,0:T(8,128)(2,1)} %coeffs_ref.9, bf16[1024,1024]{1,0:T(8,128)(2,1)} %earlier_ref.9, bf16[352,512]{1,0:T(8,128)(2,1)S(1)} %collective-permute-done.15.refs_0_, ...), custom_call_target="tpu_custom_call", output_to_operand_aliasing={{}: (7, {})} | custom-call | flops 1476395008 | bytes 2883584 | tf_op jit(solution)/shard_map/accumulate/pallas_call | solution.py:241
  97.8 3.9 %accumulate.6.refs_4_ = f32[1024,512]{1,0:T(8,128)S(1)} custom-call(s32[512]{0:T(512)S(1)} %multiply_add_fusion.2.tick_ref, bf16[1024,4608]{1,0:T(8,128)(2,1)} %coeffs_ref.9, bf16[1024,1024]{1,0:T(8,128)(2,1)} %earlier_ref.9, bf16[352,512]{1,0:T(8,128)(2,1)S(1)} %choose.3.refs_0_, ...), custom_call_target="tpu_custom_call", output_to_operand_aliasing={{}: (7, {})} | custom-call | flops 1476395008 | bytes 2883584 | tf_op jit(solution)/shard_map/accumulate/pallas_call | solution.py:241
  101.8 4.0 %accumulate.7.partial_ref = f32[1024,512]{1,0:T(8,128)S(1)} custom-call(s32[512]{0:T(512)S(1)} %multiply_add_fusion.2.tick_ref, bf16[1024,4608]{1,0:T(8,128)(2,1)} %coeffs_ref.9, bf16[1024,1024]{1,0:T(8,128)(2,1)} %earlier_ref.9, bf16[352,512]{1,0:T(8,128)(2,1)S(1)} %choose.2.refs_0_, ...), custom_call_target="tpu_custom_call", output_to_operand_aliasing={{}: (7, {})} | custom-call | flops 1476395008 | bytes 2883584 | tf_op jit(solution)/shard_map/accumulate/pallas_call | solution.py:241
  105.8 2.3 %recur.7 = (f32[256,256]{1,0:T(8,128)S(1)}, f32[256,256]{1,0:T(8,128)S(1)}) custom-call(f32[1024,512]{1,0:T(8,128)S(1)} %accumulate.7.partial_ref, f32[3,128,128]{2,1,0:T(8,128)S(1)} %add.32.mine_ref, f32[3,128,128]{2,1,0:T(8,128)S(1)} %collective-permute-done.35.other_ref, f32[4,128,128]{2,1,0:T(8,128)S(1)} %copy-done), custom_call_target="tpu_custom_call" | custom-call | tf_op jit(solution)/shard_map/recur/pallas_call | solution.py:427
  108.1 1.6 %collective-permute-start.39 = (f32[256,256]{1,0:T(8,128)S(1)}, f32[256,256]{1,0:T(8,128)S(1)}, u32[]{:S(2)}, u32[]{:S(2)}) collective-permute-start(f32[256,256]{1,0:T(8,128)S(1)} %get-tuple-element.52), channel_id=1, source_target_pairs={{0,1},{1,0},{2,3},{3,2},{4,5},{5,4},{6,7},{7,6},{8,9},{9,8},{10,11... | collective-permute-start | bytes 786440 | tf_op jit(solution)/shard_map/ppermute | solution.py:85
  109.7 2.3 %recur.6 = (f32[256,256]{1,0:T(8,128)S(1)}, f32[256,256]{1,0:T(8,128)S(1)}) custom-call(f32[1024,512]{1,0:T(8,128)S(1)} %accumulate.7.partial_ref, f32[3,128,128]{2,1,0:T(8,128)S(1)} %add.32.mine_ref, f32[3,128,128]{2,1,0:T(8,128)S(1)} %collective-permute-done.35.other_ref, f32[4,128,128]{2,1,0:T(8,128)S(1)} %copy-done), custom_call_target="tpu_custom_call" | custom-call | tf_op jit(solution)/shard_map/recur/pallas_call | solution.py:427
  112.6 2.3 %recur.5 = (f32[256,256]{1,0:T(8,128)S(1)}, f32[256,256]{1,0:T(8,128)S(1)}) custom-call(f32[1024,512]{1,0:T(8,128)S(1)} %accumulate.7.partial_ref, f32[3,128,128]{2,1,0:T(8,128)S(1)} %add.32.mine_ref, f32[3,128,128]{2,1,0:T(8,128)S(1)} %collective-permute-done.35.other_ref, f32[4,128,128]{2,1,0:T(8,128)S(1)} %copy-done), custom_call_target="tpu_custom_call" | custom-call | tf_op jit(solution)/shard_map/recur/pallas_call | solution.py:427
  114.9 1.6 %collective-permute-start.37 = (f32[256,256]{1,0:T(8,128)S(1)}, f32[256,256]{1,0:T(8,128)S(1)}, u32[]{:S(2)}, u32[]{:S(2)}) collective-permute-start(f32[256,256]{1,0:T(8,128)S(1)} %get-tuple-element.48), channel_id=1, source_target_pairs={{0,1},{1,0},{2,3},{3,2},{4,5},{5,4},{6,7},{7,6},{8,9},{9,8},{10,11... | collective-permute-start | bytes 786440 | tf_op jit(solution)/shard_map/ppermute | solution.py:85
  116.5 2.3 %recur.4 = (f32[256,256]{1,0:T(8,128)S(1)}, f32[256,256]{1,0:T(8,128)S(1)}) custom-call(f32[1024,512]{1,0:T(8,128)S(1)} %accumulate.7.partial_ref, f32[3,128,128]{2,1,0:T(8,128)S(1)} %add.32.mine_ref, f32[3,128,128]{2,1,0:T(8,128)S(1)} %collective-permute-done.35.other_ref, f32[4,128,128]{2,1,0:T(8,128)S(1)} %copy-done), custom_call_target="tpu_custom_call" | custom-call | tf_op jit(solution)/shard_map/recur/pallas_call | solution.py:427
  120.1 2.9 %collective-permute-done.38.taken_ref = f32[256,256]{1,0:T(8,128)S(1)} collective-permute-done((f32[256,256]{1,0:T(8,128)S(1)}, f32[256,256]{1,0:T(8,128)S(1)}, u32[]{:S(2)}, u32[]{:S(2)}) %collective-permute-start.38) | collective-permute-done | bytes 262176 | tf_op jit(solution)/shard_map/ppermute | solution.py:85
  123.7 4.9 %collective-permute-done.37.taken_ref = f32[256,256]{1,0:T(8,128)S(1)} collective-permute-done((f32[256,256]{1,0:T(8,128)S(1)}, f32[256,256]{1,0:T(8,128)S(1)}, u32[]{:S(2)}, u32[]{:S(2)}) %collective-permute-start.37) | collective-permute-done | bytes 262176 | tf_op jit(solution)/shard_map/ppermute | solution.py:85
  129.3 4.0 %collective-permute-done.36.taken_ref = f32[256,256]{1,0:T(8,128)S(1)} collective-permute-done((f32[256,256]{1,0:T(8,128)S(1)}, f32[256,256]{1,0:T(8,128)S(1)}, u32[]{:S(2)}, u32[]{:S(2)}) %collective-permute-start.36) | collective-permute-done | bytes 262176 | tf_op jit(solution)/shard_map/ppermute | solution.py:85
  (96 shorter events, 20.0 us)
Async XLA Ops:
  6.6 7.5 %collective-permute-start.1 = (bf16[96,352]{1,0:T(8,128)(2,1)S(1)}, bf16[96,352]{1,0:T(8,128)(2,1)S(1)}, u32[]{:S(2)}, u32[]{:S(2)}) collective-permute-start(bf16[96,352]{1,0:T(8,128)(2,1)S(1)} %get-tuple-element.31), channel_id=1, source_target_pairs={{0,4},{2,6},{4,0},{6,2},{8,12},{10,14},{12,8},{14,10},{16,20},{18,... | collective-permute-start | bytes 202760 | tf_op jit(solution)/shard_map/ppermute | solution.py:85
  9.2 7.8 %collective-permute-start.3 = (bf16[96,352]{1,0:T(8,128)(2,1)S(1)}, bf16[96,352]{1,0:T(8,128)(2,1)S(1)}, u32[]{:S(2)}, u32[]{:S(2)}) collective-permute-start(bf16[96,352]{1,0:T(8,128)(2,1)S(1)} %get-tuple-element.33), channel_id=1, source_target_pairs={{0,8},{2,10},{4,12},{6,14},{8,0},{10,2},{12,4},{14,6},{16,24},{18,... | collective-permute-start | bytes 202760 | tf_op jit(solution)/shard_map/ppermute | solution.py:85
  11.3 9.4 %collective-permute-start.5 = (bf16[96,352]{1,0:T(8,128)(2,1)S(1)}, bf16[96,352]{1,0:T(8,128)(2,1)S(1)}, u32[]{:S(2)}, u32[]{:S(2)}) collective-permute-start(bf16[96,352]{1,0:T(8,128)(2,1)S(1)} %get-tuple-element.35), channel_id=1, source_target_pairs={{0,12},{2,14},{4,8},{6,10},{8,4},{10,6},{12,0},{14,2},{16,28},{18,... | collective-permute-start | bytes 202760 | tf_op jit(solution)/shard_map/ppermute | solution.py:85
  14.1 7.2 %collective-permute-start.6 = (bf16[96,352]{1,0:T(8,128)(2,1)S(1)}, bf16[96,352]{1,0:T(8,128)(2,1)S(1)}, u32[]{:S(2)}, u32[]{:S(2)}) collective-permute-start(bf16[96,352]{1,0:T(8,128)(2,1)S(1)} %get-tuple-element.36), channel_id=1, source_target_pairs={{0,14},{2,12},{4,10},{6,8},{8,6},{10,4},{12,2},{14,0},{16,30},{18,... | collective-permute-start | bytes 202760 | tf_op jit(solution)/shard_map/ppermute | solution.py:85
  14.2 10.3 %collective-permute-start.7 = (bf16[96,352]{1,0:T(8,128)(2,1)S(1)}, bf16[96,352]{1,0:T(8,128)(2,1)S(1)}, u32[]{:S(2)}, u32[]{:S(2)}) collective-permute-start(bf16[96,352]{1,0:T(8,128)(2,1)S(1)} %get-tuple-element.37), channel_id=1, source_target_pairs={{0,16},{2,18},{4,20},{6,22},{8,24},{10,26},{12,28},{14,30},{16,0},... | collective-permute-start | bytes 202760 | tf_op jit(solution)/shard_map/ppermute | solution.py:85
  17.0 13.1 %collective-permute-start.8 = (bf16[96,352]{1,0:T(8,128)(2,1)S(1)}, bf16[96,352]{1,0:T(8,128)(2,1)S(1)}, u32[]{:S(2)}, u32[]{:S(2)}) collective-permute-start(bf16[96,352]{1,0:T(8,128)(2,1)S(1)} %get-tuple-element.38), channel_id=1, source_target_pairs={{0,18},{2,16},{4,22},{6,20},{8,26},{10,24},{12,30},{14,28},{16,2},... | collective-permute-start | bytes 202760 | tf_op jit(solution)/shard_map/ppermute | solution.py:85
  17.9 15.8 %collective-permute-start.9 = (bf16[96,352]{1,0:T(8,128)(2,1)S(1)}, bf16[96,352]{1,0:T(8,128)(2,1)S(1)}, u32[]{:S(2)}, u32[]{:S(2)}) collective-permute-start(bf16[96,352]{1,0:T(8,128)(2,1)S(1)} %get-tuple-element.39), channel_id=1, source_target_pairs={{0,20},{2,22},{4,16},{6,18},{8,28},{10,30},{12,24},{14,26},{16,4},... | collective-permute-start | bytes 202760 | tf_op jit(solution)/shard_map/ppermute | solution.py:85
  20.8 15.5 %collective-permute-start.10 = (bf16[96,352]{1,0:T(8,128)(2,1)S(1)}, bf16[96,352]{1,0:T(8,128)(2,1)S(1)}, u32[]{:S(2)}, u32[]{:S(2)}) collective-permute-start(bf16[96,352]{1,0:T(8,128)(2,1)S(1)} %get-tuple-element.40), channel_id=1, source_target_pairs={{0,22},{2,20},{4,18},{6,16},{8,30},{10,28},{12,26},{14,24},{16,6},... | collective-permute-start | bytes 202760 | tf_op jit(solution)/shard_map/ppermute | solution.py:85
  21.3 15.0 %collective-permute-start.11 = (bf16[96,352]{1,0:T(8,128)(2,1)S(1)}, bf16[96,352]{1,0:T(8,128)(2,1)S(1)}, u32[]{:S(2)}, u32[]{:S(2)}) collective-permute-start(bf16[96,352]{1,0:T(8,128)(2,1)S(1)} %get-tuple-element.41), channel_id=1, source_target_pairs={{0,24},{2,26},{4,28},{6,30},{8,16},{10,18},{12,20},{14,22},{16,8},... | collective-permute-start | bytes 202760 | tf_op jit(solution)/shard_map/ppermute | solution.py:85
  24.6 11.8 %collective-permute-start.12 = (bf16[96,352]{1,0:T(8,128)(2,1)S(1)}, bf16[96,352]{1,0:T(8,128)(2,1)S(1)}, u32[]{:S(2)}, u32[]{:S(2)}) collective-permute-start(bf16[96,352]{1,0:T(8,128)(2,1)S(1)} %get-tuple-element.42), channel_id=1, source_target_pairs={{0,26},{2,24},{4,30},{6,28},{8,18},{10,16},{12,22},{14,20},{16,10}... | collective-permute-start | bytes 202760 | tf_op jit(solution)/shard_map/ppermute | solution.py:85
  41.8 13.8 %collective-permute-start.15 = (bf16[352,512]{1,0:T(8,128)(2,1)S(1)}, bf16[352,512]{1,0:T(8,128)(2,1)S(1)}, u32[]{:S(2)}, u32[]{:S(2)}) collective-permute-start(bf16[352,512]{1,0:T(8,128)(2,1)S(1)} %fusion.2.refs_0_), channel_id=1, source_target_pairs={{0,8},{2,10},{4,12},{6,14},{8,0},{10,2},{12,4},{14,6},{16,24},{18,... | collective-permute-start | bytes 1081352 | tf_op jit(solution)/shard_map/ppermute | solution.py:85
  46.9 10.2 %collective-permute-start.30 = (bf16[352,512]{1,0:T(8,128)(2,1)S(1)}, bf16[352,512]{1,0:T(8,128)(2,1)S(1)}, u32[]{:S(2)}, u32[]{:S(2)}) collective-permute-start(bf16[352,512]{1,0:T(8,128)(2,1)S(1)} %fusion.2.refs_0_), channel_id=1, source_target_pairs={{0,4},{2,6},{4,0},{6,2},{8,12},{10,14},{12,8},{14,10},{16,20},{18,... | collective-permute-start | bytes 1081352 | tf_op jit(solution)/shard_map/ppermute | solution.py:85
  47.4 9.7 %collective-permute-start.21 = (bf16[352,512]{1,0:T(8,128)(2,1)S(1)}, bf16[352,512]{1,0:T(8,128)(2,1)S(1)}, u32[]{:S(2)}, u32[]{:S(2)}) collective-permute-start(bf16[352,512]{1,0:T(8,128)(2,1)S(1)} %fusion.2.refs_0_), channel_id=1, source_target_pairs={{8,16},{10,18},{12,20},{14,22},{16,8},{18,10},{20,12},{22,14},{9,1... | collective-permute-start | bytes 1081352 | tf_op jit(solution)/shard_map/ppermute | solution.py:501
  57.1 14.8 %collective-permute-start.22 = (bf16[352,512]{1,0:T(8,128)(2,1)S(1)}, bf16[352,512]{1,0:T(8,128)(2,1)S(1)}, u32[]{:S(2)}, u32[]{:S(2)}) collective-permute-start(bf16[352,512]{1,0:T(8,128)(2,1)S(1)} %collective-permute-done.21.refs_0_), channel_id=1, source_target_pairs={{8,0},{10,2},{12,4},{14,6},{16,24},{18,26},{20,28},{22,30},{9,1},{... | collective-permute-start | bytes 1081352 | tf_op jit(solution)/shard_map/ppermute | solution.py:505
  58.4 14.2 %collective-permute-start.27 = (bf16[352,512]{1,0:T(8,128)(2,1)S(1)}, bf16[352,512]{1,0:T(8,128)(2,1)S(1)}, u32[]{:S(2)}, u32[]{:S(2)}) collective-permute-start(bf16[352,512]{1,0:T(8,128)(2,1)S(1)} %collective-permute-done.15.refs_0_), channel_id=1, source_target_pairs={{0,4},{2,6},{4,0},{6,2},{8,12},{10,14},{12,8},{14,10},{16,20},{18,... | collective-permute-start | bytes 1081352 | tf_op jit(solution)/shard_map/ppermute | solution.py:85
  58.9 21.9 %collective-permute-start.17 = (bf16[352,512]{1,0:T(8,128)(2,1)S(1)}, bf16[352,512]{1,0:T(8,128)(2,1)S(1)}, u32[]{:S(2)}, u32[]{:S(2)}) collective-permute-start(bf16[352,512]{1,0:T(8,128)(2,1)S(1)} %collective-permute-done.16.refs_0_), channel_id=1, source_target_pairs={{8,0},{10,2},{12,4},{14,6},{16,24},{18,26},{20,28},{22,30},{9,1},{... | collective-permute-start | bytes 1081352 | tf_op jit(solution)/shard_map/ppermute | solution.py:505
  60.9 12.2 %collective-permute-start.32 = (f32[3,128,128]{2,1,0:T(8,128)S(1)}, f32[3,128,128]{2,1,0:T(8,128)S(1)}, u32[]{:S(2)}, u32[]{:S(2)}) collective-permute-start(f32[3,128,128]{2,1,0:T(8,128)S(1)} %lower.1), channel_id=1, source_target_pairs={{0,1},{1,0},{2,3},{3,2},{4,5},{5,4},{6,7},{7,6},{8,9},{9,8},{10,11... | collective-permute-start | bytes 589832 | tf_op jit(solution)/shard_map/ppermute | solution.py:85
  71.9 9.3 %collective-permute-start.24 = (bf16[352,512]{1,0:T(8,128)(2,1)S(1)}, bf16[352,512]{1,0:T(8,128)(2,1)S(1)}, u32[]{:S(2)}, u32[]{:S(2)}) collective-permute-start(bf16[352,512]{1,0:T(8,128)(2,1)S(1)} %choose.3.refs_0_), channel_id=1, source_target_pairs={{0,4},{2,6},{4,0},{6,2},{8,12},{10,14},{12,8},{14,10},{16,20},{18,... | collective-permute-start | bytes 1081352 | tf_op jit(solution)/shard_map/ppermute | solution.py:85
  72.6 12.6 %collective-permute-start.26 = (bf16[352,512]{1,0:T(8,128)(2,1)S(1)}, bf16[352,512]{1,0:T(8,128)(2,1)S(1)}, u32[]{:S(2)}, u32[]{:S(2)}) collective-permute-start(bf16[352,512]{1,0:T(8,128)(2,1)S(1)} %collective-permute-done.15.refs_0_), channel_id=1, source_target_pairs={{0,2},{2,0},{4,6},{6,4},{8,10},{10,8},{12,14},{14,12},{16,18},{18,... | collective-permute-start | bytes 1081352 | tf_op jit(solution)/shard_map/ppermute | solution.py:85
  72.6 13.2 %collective-permute-start.28 = (bf16[352,512]{1,0:T(8,128)(2,1)S(1)}, bf16[352,512]{1,0:T(8,128)(2,1)S(1)}, u32[]{:S(2)}, u32[]{:S(2)}) collective-permute-start(bf16[352,512]{1,0:T(8,128)(2,1)S(1)} %collective-permute-done.27.refs_2_), channel_id=1, source_target_pairs={{0,2},{2,0},{4,6},{6,4},{8,10},{10,8},{12,14},{14,12},{16,18},{18,... | collective-permute-start | bytes 1081352 | tf_op jit(solution)/shard_map/ppermute | solution.py:85
  73.1 12.0 %collective-permute-start.33 = (f32[3,128,128]{2,1,0:T(8,128)S(1)}, f32[3,128,128]{2,1,0:T(8,128)S(1)}, u32[]{:S(2)}, u32[]{:S(2)}) collective-permute-start(f32[3,128,128]{2,1,0:T(8,128)S(1)} %add.30), channel_id=1, source_target_pairs={{0,16},{2,18},{4,20},{6,22},{8,24},{10,26},{12,28},{14,30},{16,0},... | collective-permute-start | bytes 589832 | tf_op jit(solution)/shard_map/ppermute | solution.py:85
  81.0 8.3 %collective-permute-start.19 = (bf16[352,512]{1,0:T(8,128)(2,1)S(1)}, bf16[352,512]{1,0:T(8,128)(2,1)S(1)}, u32[]{:S(2)}, u32[]{:S(2)}) collective-permute-start(bf16[352,512]{1,0:T(8,128)(2,1)S(1)} %choose.2.refs_0_), channel_id=1, source_target_pairs={{0,4},{2,6},{4,0},{6,2},{8,12},{10,14},{12,8},{14,10},{16,20},{18,... | collective-permute-start | bytes 1081352 | tf_op jit(solution)/shard_map/ppermute | solution.py:85
  81.2 16.6 %collective-permute-start.23 = (bf16[352,512]{1,0:T(8,128)(2,1)S(1)}, bf16[352,512]{1,0:T(8,128)(2,1)S(1)}, u32[]{:S(2)}, u32[]{:S(2)}) collective-permute-start(bf16[352,512]{1,0:T(8,128)(2,1)S(1)} %choose.3.refs_0_), channel_id=1, source_target_pairs={{0,2},{2,0},{4,6},{6,4},{8,10},{10,8},{12,14},{14,12},{16,18},{18,... | collective-permute-start | bytes 1081352 | tf_op jit(solution)/shard_map/ppermute | solution.py:85
  85.2 12.7 %collective-permute-start.25 = (bf16[352,512]{1,0:T(8,128)(2,1)S(1)}, bf16[352,512]{1,0:T(8,128)(2,1)S(1)}, u32[]{:S(2)}, u32[]{:S(2)}) collective-permute-start(bf16[352,512]{1,0:T(8,128)(2,1)S(1)} %collective-permute-done.24.refs_2_), channel_id=1, source_target_pairs={{0,2},{2,0},{4,6},{6,4},{8,10},{10,8},{12,14},{14,12},{16,18},{18,... | collective-permute-start | bytes 1081352 | tf_op jit(solution)/shard_map/ppermute | solution.py:85
  85.2 16.6 %collective-permute-start.18 = (bf16[352,512]{1,0:T(8,128)(2,1)S(1)}, bf16[352,512]{1,0:T(8,128)(2,1)S(1)}, u32[]{:S(2)}, u32[]{:S(2)}) collective-permute-start(bf16[352,512]{1,0:T(8,128)(2,1)S(1)} %choose.2.refs_0_), channel_id=1, source_target_pairs={{0,2},{2,0},{4,6},{6,4},{8,10},{10,8},{12,14},{14,12},{16,18},{18,... | collective-permute-start | bytes 1081352 | tf_op jit(solution)/shard_map/ppermute | solution.py:85
  85.8 11.4 %collective-permute-start.34 = (f32[3,128,128]{2,1,0:T(8,128)S(1)}, f32[3,128,128]{2,1,0:T(8,128)S(1)}, u32[]{:S(2)}, u32[]{:S(2)}) collective-permute-start(f32[3,128,128]{2,1,0:T(8,128)S(1)} %add.31), channel_id=1, source_target_pairs={{0,8},{2,10},{4,12},{6,14},{8,0},{10,2},{12,4},{14,6},{16,24},{18,... | collective-permute-start | bytes 589832 | tf_op jit(solution)/shard_map/ppermute | solution.py:85
  89.3 12.5 %collective-permute-start.20 = (bf16[352,512]{1,0:T(8,128)(2,1)S(1)}, bf16[352,512]{1,0:T(8,128)(2,1)S(1)}, u32[]{:S(2)}, u32[]{:S(2)}) collective-permute-start(bf16[352,512]{1,0:T(8,128)(2,1)S(1)} %collective-permute-done.19.refs_2_), channel_id=1, source_target_pairs={{0,2},{2,0},{4,6},{6,4},{8,10},{10,8},{12,14},{14,12},{16,18},{18,... | collective-permute-start | bytes 1081352 | tf_op jit(solution)/shard_map/ppermute | solution.py:85
  97.3 8.5 %collective-permute-start.35 = (f32[3,128,128]{2,1,0:T(8,128)S(1)}, f32[3,128,128]{2,1,0:T(8,128)S(1)}, u32[]{:S(2)}, u32[]{:S(2)}) collective-permute-start(f32[3,128,128]{2,1,0:T(8,128)S(1)} %add.32.mine_ref), channel_id=1, source_target_pairs={{0,2},{2,0},{4,6},{6,4},{8,10},{10,8},{12,14},{14,12},{16,18},{18,... | collective-permute-start | bytes 589832 | tf_op jit(solution)/shard_map/ppermute | solution.py:85
  108.1 11.3 %collective-permute-start.39 = (f32[256,256]{1,0:T(8,128)S(1)}, f32[256,256]{1,0:T(8,128)S(1)}, u32[]{:S(2)}, u32[]{:S(2)}) collective-permute-start(f32[256,256]{1,0:T(8,128)S(1)} %get-tuple-element.52), channel_id=1, source_target_pairs={{0,1},{1,0},{2,3},{3,2},{4,5},{5,4},{6,7},{7,6},{8,9},{9,8},{10,11... | collective-permute-start | bytes 786440 | tf_op jit(solution)/shard_map/ppermute | solution.py:85
  112.0 11.0 %collective-permute-start.38 = (f32[256,256]{1,0:T(8,128)S(1)}, f32[256,256]{1,0:T(8,128)S(1)}, u32[]{:S(2)}, u32[]{:S(2)}) collective-permute-start(f32[256,256]{1,0:T(8,128)S(1)} %get-tuple-element.50), channel_id=1, source_target_pairs={{0,1},{1,0},{2,3},{3,2},{4,5},{5,4},{6,7},{7,6},{8,9},{9,8},{10,11... | collective-permute-start | bytes 786440 | tf_op jit(solution)/shard_map/ppermute | solution.py:85
  114.9 13.7 %collective-permute-start.37 = (f32[256,256]{1,0:T(8,128)S(1)}, f32[256,256]{1,0:T(8,128)S(1)}, u32[]{:S(2)}, u32[]{:S(2)}) collective-permute-start(f32[256,256]{1,0:T(8,128)S(1)} %get-tuple-element.48), channel_id=1, source_target_pairs={{0,1},{1,0},{2,3},{3,2},{4,5},{5,4},{6,7},{7,6},{8,9},{9,8},{10,11... | collective-permute-start | bytes 786440 | tf_op jit(solution)/shard_map/ppermute | solution.py:85
  118.8 14.5 %collective-permute-start.36 = (f32[256,256]{1,0:T(8,128)S(1)}, f32[256,256]{1,0:T(8,128)S(1)}, u32[]{:S(2)}, u32[]{:S(2)}) collective-permute-start(f32[256,256]{1,0:T(8,128)S(1)} %get-tuple-element.46), channel_id=1, source_target_pairs={{0,1},{1,0},{2,3},{3,2},{4,5},{5,4},{6,7},{7,6},{8,9},{9,8},{10,11... | collective-permute-start | bytes 786440 | tf_op jit(solution)/shard_map/ppermute | solution.py:85
  (11 other events, 80.5 us)
